TPU v7x, 32 devices: a whole 2x2x4 slice. The times are simulated.
32 devices in a mesh: dp: 4 (over z), tp: 8 (over y, x, core).
Axes of the slice: x: 2, y: 2, z: 4, core: 2. Of those that a mesh axis runs over, the one named last changes fastest.
Arguments:
- tokens: bfloat16 [8192, 2048], P(('dp', 'tp')), may hold values from -6 to 6
- segment_ids: int32 [8, 1024], P('dp'), may hold values from 0 to 3, as said below
- prefix_lengths: int32 [8, 4], P('dp'), may hold values from 1 to 512, as said below
- positions: int32 [8, 1024], P('dp'), may hold values from 0 to 511, as said below
- norm_gains: float32 [2, 2048], replicated, may hold values from 0.5 to 1.5
- norm_offsets: float32 [2, 2048], replicated, may hold values from -1.75 to 1.75
- input_weight: bfloat16 [2048, 6144], P(None, 'tp'), may hold values from -0.125 to 0.125
- input_offset: float32 [6144], P('tp'), may hold values from -0.625 to 0.625
- output_weight: bfloat16 [2048, 2048], P('tp'), may hold values from -8 to 8
- output_offset: float32 [2048], replicated, may hold values from -3 to 3
- expand_weight: bfloat16 [2048, 2, 5472], P(None, None, 'tp'), may hold values from -0.125 to 0.125
- expand_offset: float32 [2, 5472], P(None, 'tp'), may hold values from -1.75 to 1.75
- shrink_weight: bfloat16 [5472, 2048], P('tp'), may hold values from -1.25 to 1.25
- shrink_offset: float32 [2048], replicated, may hold values from -3 to 3
- cotangent: bfloat16 [8192, 2048], P(('dp', 'tp')), may hold values from -6 to 6
Outputs:
- layer_out: float32 [8192, 2048], P(('dp', 'tp'))
- tokens_grad: float32 [8192, 2048], P(('dp', 'tp'))
- input_weight_grad: float32 [2048, 6144], P(None, 'tp')
- input_offset_grad: float32 [6144], P('tp')
- output_weight_grad: float32 [2048, 2048], P('tp')
- output_offset_grad: float32 [2048], replicated
- expand_weight_grad: float32 [2048, 2, 5472], P(None, None, 'tp')
- expand_offset_grad: float32 [2, 5472], P(None, 'tp')
- shrink_weight_grad: float32 [5472, 2048], P('tp')
- shrink_offset_grad: float32 [2048], replicated
- norm_gains_grad: float32 [2, 2048], replicated
- norm_offsets_grad: float32 [2, 2048], replicated
Inputs may be any that keep to these rules, and one draw needn't show every extreme that they name: `segment_ids`: each row is one sequence of 4 packed documents: ids never fall, every document has one position or more, one document has exactly 512 positions and the others fewer. `positions`: each token's place within its document, counting from 0. `prefix_lengths`: entry k of a row belongs to document k of that sequence and is at most that document's length; some document has its whole length as prefix, some has a prefix of 1.
All inputs are finite; a program needn't handle non-finite values.
Results may differ from a plain program's by a relative error of at most 0.024.
Values may be sent and summed in bfloat16 or wider, within the bound.
A program may use at most 256 MiB of HBM per device.

v0:
```python
import jax
import jax.numpy as jnp
from jax import lax
from jax.sharding import PartitionSpec as P

HEAD_DIM = 128
FF_USED = 5461
LAYERS = 24
SEQ_LEN = 1024


epsilon = 1e-05
rope_base = 10000.0
masked_score = -1e30


def layer_norm(values, gains, offsets):
    average = jnp.mean(values, axis=-1, keepdims=True)
    centred = values - average
    variance = jnp.mean(centred * centred, axis=-1, keepdims=True)
    return centred * lax.rsqrt(variance + epsilon) * gains + offsets


def rotary_tables(places):
    half_dim = HEAD_DIM // 2
    exponents = lax.iota(jnp.float32, half_dim) * (-2.0 / HEAD_DIM)
    rates = jnp.power(rope_base, exponents)
    angles = places.astype(jnp.float32)[..., None] * rates
    angles = jnp.concatenate([angles, angles], axis=-1)
    return (jnp.cos(angles), jnp.sin(angles))


def rotate(values, cosine, sine):
    half_dim = HEAD_DIM // 2
    turned = jnp.concatenate([-values[..., half_dim:], values[..., :half_dim]], axis=-1)
    return values * cosine + turned * sine


def gated_gelu(gate_up, keep_units):
    return jax.nn.gelu(gate_up[:, 0], approximate=False) * gate_up[:, 1] * keep_units


def visible_mask(segments, places, prefixes):
    doc_count = prefixes.shape[0]
    matches = segments[:, None] == lax.iota(jnp.int32, doc_count)[None, :]
    own_prefix = jnp.sum(jnp.where(matches, prefixes[None, :], 0), axis=1)
    same_doc = segments[:, None] == segments[None, :]
    rows_at = lax.iota(jnp.int32, segments.shape[0])
    earlier = rows_at[None, :] <= rows_at[:, None]
    opened = places[None, :] < own_prefix[:, None]
    return same_doc & (earlier | opened)


def masked_scores(queries, keys_low, segments, places, prefixes):
    visible = visible_mask(segments, places, prefixes)
    scores = jnp.einsum(
        "ihe,jhe->hij", queries, keys_low, preferred_element_type=jnp.float32
    ) * HEAD_DIM ** (-0.5)
    return jnp.where(visible[None], scores, masked_score)


def attend_forward(pieces_in):
    queries, keys_low, values_low, segments, places, prefixes = pieces_in
    scores = masked_scores(queries, keys_low, segments, places, prefixes)
    row_peak = jnp.max(scores, axis=-1, keepdims=True)
    shifted = jnp.exp(scores - row_peak)
    totals = jnp.sum(shifted, axis=-1, keepdims=True)
    attend_probs = (shifted / totals).astype(jnp.bfloat16)
    mixed_heads = jnp.einsum(
        "hij,jhe->ihe", attend_probs, values_low, preferred_element_type=jnp.float32
    )
    return (mixed_heads.astype(jnp.bfloat16), (row_peak + jnp.log(totals))[..., 0])


def attend_backward(pieces_in):
    queries, keys_low, values_low, grad_mixed, log_totals, segments, places, prefixes = pieces_in
    score_scale = HEAD_DIM ** (-0.5)
    scores = masked_scores(queries, keys_low, segments, places, prefixes)
    attend_probs = jnp.exp(scores - log_totals[..., None])
    grad_probs = jnp.einsum(
        "ihe,jhe->hij", grad_mixed, values_low, preferred_element_type=jnp.float32
    )
    grad_values = jnp.einsum(
        "hij,ihe->jhe",
        attend_probs.astype(jnp.bfloat16),
        grad_mixed,
        preferred_element_type=jnp.float32,
    )
    inner_sum = jnp.sum(attend_probs * grad_probs, axis=-1, keepdims=True)
    grad_scores = (attend_probs * (grad_probs - inner_sum)).astype(jnp.bfloat16)
    grad_queries = (
        jnp.einsum("hij,jhe->ihe", grad_scores, keys_low, preferred_element_type=jnp.float32)
        * score_scale
    )
    grad_keys = (
        jnp.einsum("hij,ihe->jhe", grad_scores, queries, preferred_element_type=jnp.float32)
        * score_scale
    )
    return (grad_queries, grad_keys, grad_values)


def local(
    tokens,
    segment_ids,
    prefix_lengths,
    positions,
    norm_gains,
    norm_offsets,
    input_weight,
    input_offset,
    output_weight,
    output_offset,
    expand_weight,
    expand_offset,
    shrink_weight,
    shrink_offset,
    cotangent,
):
    residual_scale = (2.0 * LAYERS) ** 0.5
    seq_count = segment_ids.shape[0]
    group_rows = seq_count * SEQ_LEN
    heads_local = input_weight.shape[1] // (3 * HEAD_DIM)
    width_local = expand_weight.shape[2]
    unit_index = lax.axis_index("tp") * width_local + lax.iota(jnp.int32, width_local)
    keep_units = (unit_index < FF_USED).astype(jnp.float32)
    token_values = tokens.astype(jnp.float32)
    first_norm, first_back = jax.vjp(layer_norm, token_values, norm_gains[0], norm_offsets[0])
    first_low = first_norm.astype(jnp.bfloat16)
    projected = (
        jnp.dot(
            lax.all_gather(first_low, "tp", axis=0, tiled=True),
            input_weight,
            preferred_element_type=jnp.float32,
        )
        + input_offset
    )
    projected = projected.reshape(seq_count, SEQ_LEN, heads_local, 3, HEAD_DIM)
    cosine, sine = rotary_tables(positions)
    cosine = cosine[:, :, None, :]
    sine = sine[:, :, None, :]
    queries = rotate(projected[:, :, :, 0], cosine, sine).astype(jnp.bfloat16)
    keys_low = rotate(projected[:, :, :, 1], cosine, sine).astype(jnp.bfloat16)
    values_low = projected[:, :, :, 2].astype(jnp.bfloat16)
    mixed_heads, log_totals = lax.map(
        attend_forward, (queries, keys_low, values_low, segment_ids, positions, prefix_lengths)
    )
    mixed_low = mixed_heads.reshape(group_rows, heads_local * HEAD_DIM)
    own_heads = lax.all_to_all(mixed_low, "tp", split_axis=0, concat_axis=1, tiled=True)
    full_output = lax.all_gather(output_weight, "tp", axis=0, tiled=True)
    attention_sum = jnp.dot(own_heads, full_output, preferred_element_type=jnp.float32)
    middle = residual_scale * first_norm + attention_sum + output_offset
    second_norm, second_back = jax.vjp(layer_norm, middle, norm_gains[1], norm_offsets[1])
    second_low = second_norm.astype(jnp.bfloat16)
    gate_up = (
        jnp.einsum(
            "id,dcf->icf",
            lax.all_gather(second_low, "tp", axis=0, tiled=True),
            expand_weight,
            preferred_element_type=jnp.float32,
        )
        + expand_offset
    )
    hidden_values, gelu_back = jax.vjp(
        lambda gate_input: gated_gelu(gate_input, keep_units), gate_up
    )
    hidden_low = hidden_values.astype(jnp.bfloat16)
    shrink_sum = lax.psum_scatter(
        jnp.dot(hidden_low, shrink_weight, preferred_element_type=jnp.float32).astype(jnp.bfloat16),
        "tp",
        scatter_dimension=0,
        tiled=True,
    ).astype(jnp.float32)
    layer_out = residual_scale * second_norm + shrink_sum + shrink_offset
    grad_output = cotangent.astype(jnp.float32)
    shrink_offset_grad = jnp.sum(grad_output, axis=0)
    grad_gathered = lax.all_gather(cotangent, "tp", axis=0, tiled=True)
    shrink_weight_grad = jnp.einsum(
        "if,id->fd", hidden_low, grad_gathered, preferred_element_type=jnp.float32
    )
    grad_hidden = jnp.einsum(
        "id,fd->if", grad_gathered, shrink_weight, preferred_element_type=jnp.float32
    )
    grad_gate_up = gelu_back(grad_hidden)[0].astype(jnp.bfloat16)
    expand_offset_grad = jnp.sum(grad_gate_up.astype(jnp.float32), axis=0)
    grad_block = grad_gate_up
    expand_weight_grad = jnp.einsum(
        "id,icf->dcf",
        lax.all_gather(second_low, "tp", axis=0, tiled=True),
        grad_block,
        preferred_element_type=jnp.float32,
    )
    grad_block = grad_gate_up
    grad_second = residual_scale * grad_output + lax.psum_scatter(
        jnp.einsum(
            "icf,dcf->id", grad_block, expand_weight, preferred_element_type=jnp.float32
        ).astype(jnp.bfloat16),
        "tp",
        scatter_dimension=0,
        tiled=True,
    ).astype(jnp.float32)
    grad_middle, second_gain_grad, second_offset_grad = second_back(grad_second)
    grad_attention = grad_middle.astype(jnp.bfloat16)
    output_offset_grad = jnp.sum(grad_attention.astype(jnp.float32), axis=0)
    attention_gathered = lax.all_gather(grad_attention, "tp", axis=0, tiled=True)
    output_weight_grad = jnp.einsum(
        "ia,id->ad", mixed_low, attention_gathered, preferred_element_type=jnp.float32
    )
    grad_mixed = jnp.einsum(
        "id,ad->ia", attention_gathered, output_weight, preferred_element_type=jnp.float32
    ).astype(jnp.bfloat16)
    grad_mixed = grad_mixed.reshape(seq_count, SEQ_LEN, heads_local, HEAD_DIM)
    grad_queries, grad_keys, grad_values = lax.map(
        attend_backward,
        (
            queries,
            keys_low,
            values_low,
            grad_mixed,
            log_totals,
            segment_ids,
            positions,
            prefix_lengths,
        ),
    )
    grad_projected = jnp.stack(
        [rotate(grad_queries, cosine, -sine), rotate(grad_keys, cosine, -sine), grad_values], axis=3
    )
    grad_projected = grad_projected.reshape(group_rows, heads_local * 3 * HEAD_DIM).astype(
        jnp.bfloat16
    )
    input_offset_grad = jnp.sum(grad_projected.astype(jnp.float32), axis=0)
    grad_block = grad_projected
    input_weight_grad = jnp.einsum(
        "id,ic->dc",
        lax.all_gather(first_low, "tp", axis=0, tiled=True),
        grad_block,
        preferred_element_type=jnp.float32,
    )
    grad_block = grad_projected
    grad_first = residual_scale * grad_middle + lax.psum_scatter(
        jnp.einsum(
            "ic,dc->id", grad_block, input_weight, preferred_element_type=jnp.float32
        ).astype(jnp.bfloat16),
        "tp",
        scatter_dimension=0,
        tiled=True,
    ).astype(jnp.float32)
    tokens_grad, first_gain_grad, first_offset_grad = first_back(grad_first)
    summed_weights = (
        lax.psum(input_weight_grad.astype(jnp.bfloat16), "dp").astype(jnp.float32),
        lax.psum(input_offset_grad.astype(jnp.bfloat16), "dp").astype(jnp.float32),
        lax.psum(output_weight_grad.astype(jnp.bfloat16), "dp").astype(jnp.float32),
        lax.psum(expand_weight_grad.astype(jnp.bfloat16), "dp").astype(jnp.float32),
        lax.psum(expand_offset_grad.astype(jnp.bfloat16), "dp").astype(jnp.float32),
        lax.psum(shrink_weight_grad.astype(jnp.bfloat16), "dp").astype(jnp.float32),
    )
    summed_vectors = lax.psum(
        (
            jnp.stack([first_gain_grad, second_gain_grad]),
            jnp.stack([first_offset_grad, second_offset_grad]),
            output_offset_grad,
            shrink_offset_grad,
        ),
        ("dp", "tp"),
    )
    return (
        layer_out,
        tokens_grad,
        summed_weights[0],
        summed_weights[1],
        summed_weights[2],
        summed_vectors[2],
        summed_weights[3],
        summed_weights[4],
        summed_weights[5],
        summed_vectors[3],
        summed_vectors[0],
        summed_vectors[1],
    )


def solution(mesh):
    in_specs = (
        P(("dp", "tp"), None),
        P("dp", None),
        P("dp", None),
        P("dp", None),
        P(),
        P(),
        P(None, "tp"),
        P("tp"),
        P("tp", None),
        P(),
        P(None, None, "tp"),
        P(None, "tp"),
        P("tp", None),
        P(),
        P(("dp", "tp"), None),
    )
    out_specs = (
        P(("dp", "tp"), None),
        P(("dp", "tp"), None),
        P(None, "tp"),
        P("tp"),
        P("tp", None),
        P(),
        P(None, None, "tp"),
        P(None, "tp"),
        P("tp", None),
        P(),
        P(),
        P(),
    )
    return jax.shard_map(local, mesh=mesh, in_specs=in_specs, out_specs=out_specs, check_vma=False)
```

profile of v0, /device:TPU:2, one launch (start us, length us, event | category | flops | bytes accessed | tf_op | source)
XLA Modules:
  0.0 1275.7 jit_solution(5855190570922395362)
XLA Ops:
  16.7 17.1 %fusion.115 = (f32[2,1024,128]{1,0,2:T(2,128)}, f32[2,1024,128]{1,0,2:T(2,128)}, f32[2,1024,128]{1,0,2:T(2,128)}) fusion(f32[2,1024,64]{1,0,2:T(2,128)S(1)} %broadcast_multiply_fusion), kind=kLoop, calls=%fused_computation.195 | loop fusion | flops 524288 | bytes 3670016 | tf_op jit(solution)/shard_map/neg | solution.py:226
  33.8 36.8 %all-gather.6.cloned.1.call-done = bf16[2048,2048]{1,0:T(8,128)(2,1)} async-done(((bf16[256,2048]{1,0:T(8,128)(2,1)}), bf16[2048,2048]{1,0:T(8,128)(2,1)}) %all-gather.6.cloned.1.call-update) | async-done | bytes 8388624 | tf_op jit(solution)/shard_map/all_gather | solution.py:131
  120.0 29.4 %while.26 = (s32[]{:T(128)}, bf16[2,1024,2,128]{3,2,1,0:T(2,128)(2,1)}, f32[2,2,1024]{2,1,0:T(2,128)S(1)}, bf16[2,1024,2,128]{1,3,2,0:T(8,128)(2,1)}, s32[2,1024...) while((s32[]{:T(128)}, ...), condition=%wide.region_6.7_spmd, body=%wide.region_2.6_spmd.sunk | while | flops 1104421888 | bytes 37852364 | solution.py:144
  152.0 28.5 %all_to_all.19 = bf16[8,256,256]{2,1,0:T(8,128)(2,1)} all-to-all(bf16[8,256,256]{2,1,0:T(8,128)(2,1)} %all_to_all.14), channel_id=1, replica_groups=mesh['dp'=4,'tp'=8] {'tp'}, dimensions={0} | all-to-all | bytes 2097152 | tf_op jit(solution)/shard_map/all_to_all | solution.py:148
  205.8 45.5 %all-gather.10.cloned.1.call-done = bf16[2048,2048]{1,0:T(8,128)(2,1)} async-done(((bf16[256,2048]{1,0:T(8,128)(2,1)}), bf16[2048,2048]{1,0:T(8,128)(2,1)}) %all-gather.10.cloned.1.call-update) | async-done | bytes 8388624 | tf_op jit(solution)/shard_map/all_gather | solution.py:157
  251.3 19.2 %broadcast_add_fusion = f32[2048,2,684]{0,2,1:T(8,128)S(1)} fusion(f32[2,684]{1,0:T(2,128)S(1)} %copy-done.45, bf16[2048,2,684]{0,1,2:T(2,128)(2,1)} %param.29, bf16[2048,2048]{1,0:T(8,128)(2,1)} %all-gather.10.cloned.1.call-done), kind=kOutput, calls=%fused_computation.110 | convolution fusion | flops 11478417408 | bytes 25204064 | tf_op jit(solution)/shard_map/id,dcf->icf/dot_general | solution.py:155
  270.5 15.2 %multiply_bitcast_fusion = (f32[2048,1,684]{0,2,1:T(8,128)}, f32[2048,684]{0,1:T(8,128)}) fusion(f32[2048,684]{0,1:T(8,128)} %fusion.124, f32[684]{0:T(1024)S(1)} %fusion.111, f32[2048,2,684]{0,2,1:T(8,128)S(1)} %broadcast_add_fusion), kind=kLoop, calls=%fused_computation.96 | loop fusion | flops 92454912 | bytes 22416048 | tf_op jit(solution)/shard_map/transpose(jvp())/broadcast_in_dim | solution.py:40
  293.3 21.5 %bitcast_convert_fusion = bf16[2048,2048]{1,0:T(8,128)(2,1)} fusion(bf16[2048,2,684]{0,1,2:T(2,128)(2,1)} %param.29, f32[2048,1,684]{0,2,1:T(8,128)} %get-tuple-element.338, f32[2048,1,684]{0,2,1:T(8,128)} %get-tuple-element.328), kind=kOutput, calls=%fused_computation.71 | convolution fusion | flops 11485413376 | bytes 25198592 | tf_op jit(solution)/shard_map/icf,dcf->id/dot_general | solution.py:194
  314.9 11.7 convolution_convert_fusion
  326.6 59.6 %reduce-scatter.6.cloned.1.call-done = bf16[256,2048]{1,0:T(8,128)(2,1)} async-done(((bf16[2048,2048]{1,0:T(8,128)(2,1)}), bf16[256,2048]{1,0:T(8,128)(2,1)}) %reduce-scatter.6.cloned.1.call-update) | async-done | bytes 1048592 | tf_op jit(solution)/shard_map/reduce_scatter | solution.py:193
  390.1 71.1 %reduce-scatter.4.cloned.1.call-done = bf16[256,2048]{1,0:T(8,128)(2,1)} async-done(((bf16[2048,2048]{1,0:T(8,128)(2,1)}), bf16[256,2048]{1,0:T(8,128)(2,1)}) %reduce-scatter.4.cloned.1.call-update) | async-done | bytes 1048592 | tf_op jit(solution)/shard_map/reduce_scatter | solution.py:167
  473.3 50.9 %all-gather.14.cloned.1.call-done = bf16[2048,2048]{1,0:T(8,128)(2,1)} async-done(((bf16[256,2048]{1,0:T(8,128)(2,1)}), bf16[2048,2048]{1,0:T(8,128)(2,1)}) %all-gather.14.cloned.1.call-update) | async-done | bytes 8388624 | tf_op jit(solution)/shard_map/all_gather | solution.py:204
  533.3 166.2 %while.27 = (s32[]{:T(128)}, f32[2,1024,2,128]{1,0,3,2:T(2,128)}, f32[2,1024,2,128]{1,0,3,2:T(2,128)}, bf16[2,1024,2,128]{1,0,3,2:T(2,128)(2,1)}, bf16[2,1024,2,...) while((s32[]{:T(128)}, f32[2,1024,2,128]{1,0,3,2:T(2,128)}, ...), condition=%wide.region_16.17_spmd, body=%wide.region_13.16_spmd.sunk | while | flops 2721588224 | bytes 171013536 | solution.py:212
  544.7 17.8 %dynamic_update_slice.29 = bf16[2,1024,2,128]{1,0,3,2:T(2,128)(2,1)} dynamic-update-slice(bf16[2,1024,2,128]{1,0,3,2:T(2,128)(2,1)} %get-tuple-element.557, bf16[1,1024,2,128]{1,0,3,2:T(2,128)(2,1)} %copy.201, s32[]{:T(128)S(6)} %copy.220, s32[]{:T(128)} %constant.72.clone.1..sunk, s32[]{:T(128)} %constant.72.clone.1..sunk, s32[]{:T(128)} %constant.72.clone.1..sunk) | dynamic-update-slice | bytes 1048580 | tf_op jit(solution)/shard_map/while/body/jit(dynamic_update_index_in_dim)/dynamic_update_slice | solution.py:212
  578.8 18.8 %dynamic_update_slice.28 = f32[2,1024,2,128]{1,0,3,2:T(2,128)} dynamic-update-slice(f32[2,1024,2,128]{1,0,3,2:T(2,128)} %get-tuple-element.556, f32[1,1024,2,128]{1,0,3,2:T(1,128)} %copy.200, s32[]{:T(128)S(6)} %copy.220, s32[]{:T(128)} %constant.72.clone.1..sunk, s32[]{:T(128)} %constant.72.clone.1..sunk, s32[]{:T(128)} %constant.72.clone.1..sunk) | dynamic-update-slice | bytes 2097156 | tf_op jit(solution)/shard_map/while/body/jit(dynamic_update_index_in_dim)/dynamic_update_slice | solution.py:212
  597.7 18.8 %dynamic_update_slice.27 = f32[2,1024,2,128]{1,0,3,2:T(2,128)} dynamic-update-slice(f32[2,1024,2,128]{1,0,3,2:T(2,128)} %get-tuple-element.555, f32[1,1024,2,128]{1,0,3,2:T(1,128)} %copy.199, s32[]{:T(128)S(6)} %copy.220, s32[]{:T(128)} %constant.72.clone.1..sunk, s32[]{:T(128)} %constant.72.clone.1..sunk, s32[]{:T(128)} %constant.72.clone.1..sunk) | dynamic-update-slice | bytes 2097156 | tf_op jit(solution)/shard_map/while/body/jit(dynamic_update_index_in_dim)/dynamic_update_slice | solution.py:212
  627.6 17.8 %dynamic_update_slice.29 = bf16[2,1024,2,128]{1,0,3,2:T(2,128)(2,1)} dynamic-update-slice(bf16[2,1024,2,128]{1,0,3,2:T(2,128)(2,1)} %get-tuple-element.557, bf16[1,1024,2,128]{1,0,3,2:T(2,128)(2,1)} %copy.201, s32[]{:T(128)S(6)} %copy.220, s32[]{:T(128)} %constant.72.clone.1..sunk, s32[]{:T(128)} %constant.72.clone.1..sunk, s32[]{:T(128)} %constant.72.clone.1..sunk) | dynamic-update-slice | bytes 1048580 | tf_op jit(solution)/shard_map/while/body/jit(dynamic_update_index_in_dim)/dynamic_update_slice | solution.py:212
  661.7 18.8 %dynamic_update_slice.28 = f32[2,1024,2,128]{1,0,3,2:T(2,128)} dynamic-update-slice(f32[2,1024,2,128]{1,0,3,2:T(2,128)} %get-tuple-element.556, f32[1,1024,2,128]{1,0,3,2:T(1,128)} %copy.200, s32[]{:T(128)S(6)} %copy.220, s32[]{:T(128)} %constant.72.clone.1..sunk, s32[]{:T(128)} %constant.72.clone.1..sunk, s32[]{:T(128)} %constant.72.clone.1..sunk) | dynamic-update-slice | bytes 2097156 | tf_op jit(solution)/shard_map/while/body/jit(dynamic_update_index_in_dim)/dynamic_update_slice | solution.py:212
  680.5 18.8 %dynamic_update_slice.27 = f32[2,1024,2,128]{1,0,3,2:T(2,128)} dynamic-update-slice(f32[2,1024,2,128]{1,0,3,2:T(2,128)} %get-tuple-element.555, f32[1,1024,2,128]{1,0,3,2:T(1,128)} %copy.199, s32[]{:T(128)S(6)} %copy.220, s32[]{:T(128)} %constant.72.clone.1..sunk, s32[]{:T(128)} %constant.72.clone.1..sunk, s32[]{:T(128)} %constant.72.clone.1..sunk) | dynamic-update-slice | bytes 2097156 | tf_op jit(solution)/shard_map/while/body/jit(dynamic_update_index_in_dim)/dynamic_update_slice | solution.py:212
  737.8 20.8 %fusion.75 = bf16[2048,2,684]{0,2,1:T(8,128)(2,1)} fusion(bf16[2048,2048]{1,0:T(8,128)(2,1)} %all-gather.10.cloned.1.call-done, f32[2048,1,684]{0,2,1:T(8,128)} %get-tuple-element.338, f32[2048,1,684]{0,2,1:T(8,128)} %get-tuple-element.328), kind=kOutput, calls=%fused_computation.115 | convolution fusion | flops 11484020736 | bytes 25198592 | tf_op jit(solution)/shard_map/id,icf->dcf/dot_general | solution.py:186
  777.8 11.8 all-reduce.3
  802.8 46.2 %all-reduce.2 = (f32[2048]{0:T(1024)}, f32[2048]{0:T(1024)}, f32[2,2048]{1,0:T(2,128)}, f32[2,2048]{1,0:T(2,128)}) all-reduce(f32[2048]{0:T(1024)S(1)} %copy-done.36, f32[2048]{0:T(1024)S(1)} %copy-done.33, f32[2,2048]{1,0:T(2,128)S(1)} %pad_maximum_fusion.1, ...), channel_id=1, replica_groups=mesh['dp'=4,'tp'=8] {'dp','tp'}, use_global_device_ids=true, to_apply=%region_25.26 | all-reduce | flops 12288 | bytes 98304 | tf_op jit(solution)/shard_map/psum | solution.py:257
  852.9 380.0 %all-reduce.7.cloned.1.call-done = (bf16[2048,2,684]{0,2,1:T(8,128)(2,1)}, bf16[2048,768]{1,0:T(8,128)(2,1)}, bf16[256,2048]{1,0:T(8,128)(2,1)}, bf16[684,2048]{1,0:T(8,128)(2,1)}) async-done(((bf16[2048,2,684]{0,2,1:T(8,128)(2,1)}, bf16[2048,768]{1,0:T(8,128)(2,1)}, bf16[256,2048]{1,0:T(8,128)(2,1)}, bf16[684,2048]{1,0:T(8,128)(2,1)}), (bf16[2048,2,684]{0,2,1:T(8,128)(2,1)}, bf16[2048,768]{1,0:T(8,128)(2,1)}, ...) | async-done | bytes 12599312 | tf_op jit(solution)/shard_map/psum | solution.py:253
  1235.7 26.6 %copy.137 = f32[2048,2,684]{0,1,2:T(2,128)} copy(bf16[2048,2,684]{0,2,1:T(8,128)(2,1)} %get-tuple-element.317) | data formatting | bytes 16809984
  (261 shorter events, 286.0 us)
Async XLA Ops:
  7.2 63.5 %copy-start = (bf16[2048,768]{1,0:T(8,128)(2,1)S(1)}, bf16[2048,768]{1,0:T(8,128)(2,1)}, u32[]{:S(2)}) copy-start(bf16[2048,768]{1,0:T(8,128)(2,1)} %param.25) | copy-start | bytes 9437188
  7.2 63.4 %copy-start.46 = (f32[768]{0:T(1024)S(1)}, f32[768]{0:T(1024)}, u32[]{:S(2)}) copy-start(f32[768]{0:T(1024)} %param.26) | copy-start | bytes 9220
  7.2 63.4 %all-gather.6.cloned.1.call-start = ((), (), s32[]{:S(2)}) async-start(), calls=%async_computation.4 | async-start | bytes 9437184 | tf_op jit(solution)/shard_map/all_gather | solution.py:131
  8.9 173.9 %copy-start.31 = (f32[256]{0:T(256)}, f32[256]{0:T(256)S(1)}, u32[]{:S(2)}) copy-start(f32[256]{0:T(256)S(1)} %broadcast_multiply_fusion.2) | copy-start | bytes 3076
  10.5 172.2 %copy-start.37 = (f32[256]{0:T(256)}, f32[256]{0:T(256)S(1)}, u32[]{:S(2)}) copy-start(f32[256]{0:T(256)S(1)} %fusion.112) | copy-start | bytes 3076
  11.4 171.4 %copy-start.27 = (f32[1,2048]{1,0:T(1,128)}, f32[1,2048]{1,0:T(1,128)S(1)}, u32[]{:S(2)}) copy-start(f32[1,2048]{1,0:T(1,128)S(1)} %get-tuple-element.359) | copy-start | bytes 24580
  14.9 167.9 %all-gather.8.cloned.1.call-start = ((), (), s32[]{:S(2)}) async-start(), calls=%async_computation.5 | async-start | bytes 9437184 | tf_op jit(solution)/shard_map/all_gather | solution.py:149
  15.6 178.9 %all-gather.12.cloned.1.call-start = ((), (), s32[]{:S(2)}) async-start(), calls=%async_computation.8 | async-start | bytes 9437184 | tf_op jit(solution)/shard_map/all_gather | solution.py:176
  16.4 234.9 %all-gather.10.cloned.1.call-start = ((), (), s32[]{:S(2)}) async-start(), calls=%async_computation.6 | async-start | bytes 9437184 | tf_op jit(solution)/shard_map/all_gather | solution.py:157
  149.4 33.3 %copy-start.43 = (f32[2048]{0:T(1024)S(1)}, f32[2048]{0:T(1024)}, u32[]{:S(2)}) copy-start(f32[2048]{0:T(1024)} %param.28) | copy-start | bytes 24580
  192.2 194.0 %reduce-scatter.6.cloned.1.call-start = ((), (), s32[]{:S(2)}) async-start(), calls=%async_computation.9 | async-start | bytes 9437184 | tf_op jit(solution)/shard_map/reduce_scatter | solution.py:193
  192.3 58.9 %copy-start.45 = (f32[2,684]{1,0:T(2,128)S(1)}, f32[2,684]{1,0:T(2,128)}, u32[]{:S(2)}) copy-start(f32[2,684]{1,0:T(2,128)} %param.30) | copy-start | bytes 16420
  314.8 146.4 %reduce-scatter.4.cloned.1.call-start = ((), (), s32[]{:S(2)}) async-start(), calls=%async_computation.7 | async-start | bytes 9437184 | tf_op jit(solution)/shard_map/reduce_scatter | solution.py:167
  326.6 134.7 %copy-start.44 = (f32[2048]{0:T(1024)S(1)}, f32[2048]{0:T(1024)}, u32[]{:S(2)}) copy-start(f32[2048]{0:T(1024)} %param.32) | copy-start | bytes 24580
  326.6 197.5 %all-gather.14.cloned.1.call-start = ((), (), s32[]{:S(2)}) async-start(), calls=%async_computation.10 | async-start | bytes 9437184 | tf_op jit(solution)/shard_map/all_gather | solution.py:204
  466.3 64.8 %copy-start.39 = (f32[256]{0:T(256)}, f32[256]{0:T(256)S(1)}, u32[]{:S(2)}) copy-start(f32[256]{0:T(256)S(1)} %negate_multiply_fusion.2) | copy-start | bytes 3076
  469.5 328.8 %reduce-scatter.8.cloned.1.call-start = ((), (), s32[]{:S(2)}) async-start(), calls=%async_computation.11 | async-start | bytes 9437184 | tf_op jit(solution)/shard_map/reduce_scatter | solution.py:240
  726.9 506.0 %all-reduce.7.cloned.1.call-start = ((), (), s32[]{:S(2)}) async-start(), calls=%async_computation.12 | async-start | bytes 25296896 | tf_op jit(solution)/shard_map/psum | solution.py:253
  727.0 31.6 %slice-start.2 = ((s8[8388608]{0:T(1024)(128)(4,1)}), s8[4194304]{0:T(1024)(128)(4,1)S(1)}, s32[]{:S(2)}) async-start(s8[8388608]{0:T(1024)(128)(4,1)} %bitcast.266), calls=%async_computation.15 | async-start | bytes 8388608
  772.7 25.6 %copy-start.28 = (f32[1,2048]{1,0:T(1,128)S(1)}, f32[1,2048]{1,0:T(1,128)}, u32[]{:S(2)}) copy-start(f32[1,2048]{1,0:T(1,128)} %copy-done.27) | copy-start | bytes 24580
  772.7 25.6 %copy-start.32 = (f32[256]{0:T(256)S(1)}, f32[256]{0:T(256)}, u32[]{:S(2)}) copy-start(f32[256]{0:T(256)} %copy-done.31) | copy-start | bytes 3076
  772.7 25.6 %copy-start.40 = (f32[256]{0:T(256)S(1)}, f32[256]{0:T(256)}, u32[]{:S(2)}) copy-start(f32[256]{0:T(256)} %copy-done.39) | copy-start | bytes 3076
  777.7 25.1 %copy-start.33 = (f32[2048]{0:T(1024)S(1)}, f32[2048]{0:T(1024)}, u32[]{:S(2)}) copy-start(f32[2048]{0:T(1024)} %get-tuple-element.268) | copy-start | bytes 24580
  1235.7 26.6 %copy-start.24 = (bf16[684,2048]{1,0:T(8,128)(2,1)S(1)}, bf16[684,2048]{1,0:T(8,128)(2,1)}, u32[]{:S(2)}) copy-start(bf16[684,2048]{1,0:T(8,128)(2,1)} %get-tuple-element.320) | copy-start | bytes 8404996
  (45 other events, 334.3 us)
Sparse Core Ops, SparseCore 0:
  15.0 55.6 all-gather.5
  72.5 54.3 all-gather.7
  128.8 65.6 all-gather.11
  196.8 54.3 all-gather.9
  315.0 71.2 reduce-scatter.5
  389.9 71.2 reduce-scatter.3
  469.6 54.4 all-gather.13
  727.1 71.1 reduce-scatter.7
  801.4 431.4 all-reduce.6
where the time goes:
time: 1300 us; the launch traced here: 1280 us
  waiting for transfers between devices  655 us (50%)
  local copies, waits for them, and re-layouts  215 us (17%)
  matrix products  187 us (14%)
  other arithmetic  116 us (9%)
  blocking collectives  86.5 us (7%)
  between operations  14.9 us (1%)
    psum x1, waiting for transfers between devices, local(): lax.psum(expand_weight_grad.astype(jnp.bfloat16), 'dp').astype(jnp.float32)  380 us
    dynamic_update_slice x12, local copies, waits for them, and re-layouts, local(): lax.map(attend_backward, (queries, keys_low, values_low, grad_mixed, log_...  123 us
    reduce_scatter x1, waiting for transfers between devices, local(): lax.psum_scatter(jnp.dot(hidden_low, shrink_weight, preferred_element_typ...  71.1 us
    reduce_scatter x1, waiting for transfers between devices, local(): lax.psum_scatter(jnp.einsum('icf,dcf->id', grad_block, expand_weight, pre...  59.6 us
    all_gather x1, waiting for transfers between devices, local(): lax.all_gather(grad_attention, 'tp', axis=0, tiled=True)  50.9 us
    psum x1, blocking collectives, local(): lax.psum((jnp.stack([first_gain_grad, second_gain_grad]), jnp.stack([firs...  46.2 us
    all_gather x1, waiting for transfers between devices, local(): lax.all_gather(second_low, 'tp', axis=0, tiled=True)  45.5 us
    all_gather x1, waiting for transfers between devices, local(): lax.all_gather(first_low, 'tp', axis=0, tiled=True)  36.8 us
  transfers between devices with their start and end apart: 9, of which 8 were waited for; matrix products, arithmetic and copies ran while one was open for 15% of the time, Pallas kernels for 0%

commit v1 on v0

v1 whole, which is shorter than its diff:
```python
import functools

import jax
import jax.numpy as jnp
from jax import lax
from jax.experimental import pallas as pl
from jax.experimental.pallas import tpu as pltpu
from jax.sharding import PartitionSpec as P

HEAD_DIM = 128
FF_USED = 5461
LAYERS = 24
SEQ_LEN = 1024
BLOCK = 256

epsilon = 1e-05
rope_base = 10000.0
masked_score = -1e30
F32 = jnp.float32
BF16 = jnp.bfloat16
ROWS = (((1,), (1,)), ((), ()))
COLS = (((0,), (0,)), ((), ()))


def dot(left, right, dims):
    return lax.dot_general(left, right, dims, preferred_element_type=F32)


def normalize(values):
    average = jnp.mean(values, axis=-1, keepdims=True)
    centred = values - average
    variance = jnp.mean(centred * centred, axis=-1, keepdims=True)
    scale = lax.rsqrt(variance + epsilon)
    return centred * scale, scale


def normalize_back(grad, gains, hat, scale):
    pulled = grad * gains
    grad_in = scale * (
        pulled
        - jnp.mean(pulled, axis=-1, keepdims=True)
        - hat * jnp.mean(pulled * hat, axis=-1, keepdims=True)
    )
    return grad_in, jnp.sum(grad * hat, axis=0), jnp.sum(grad, axis=0)


def rotary_tables(places):
    half_dim = HEAD_DIM // 2
    exponents = lax.iota(F32, half_dim) * (-2.0 / HEAD_DIM)
    rates = jnp.power(rope_base, exponents)
    angles = places.astype(F32)[..., None] * rates
    cosine, sine = jnp.cos(angles), jnp.sin(angles)
    return jnp.concatenate([cosine, cosine], -1), jnp.concatenate([-sine, sine], -1)


def line_steps(part, count, axis):
    here = lax.axis_index(axis)
    half = count // 2
    for k in range(half - 1):
        got = yield part, [(k, k + 1), (count - 1 - k, count - 2 - k)]
        part = (part.astype(F32) + got.astype(F32)).astype(BF16)
    if count > 1:
        got = yield part, [(half - 1, half), (half, half - 1)]
        part = (part.astype(F32) + got.astype(F32)).astype(BF16)
    for k in range(half - 1):
        got = yield part, [(half - 1 - k, half - 2 - k), (half + k, half + k + 1)]
        outer = (here == half - 2 - k) | (here == half + k + 1)
        part = jnp.where(outer, got, part)
    return part


class Line:
    def __init__(self, count, axis):
        self.count, self.axis = count, axis
        self.waiting, self.moving, self.sums, self.marks = [], [], {}, []

    def add(self, name, part):
        self.waiting.append((name, part.astype(BF16)))

    def turn(self, *inputs):
        sends = []
        if self.waiting:
            name, part = self.waiting.pop(0)
            self.moving.append((name, line_steps(part, self.count, self.axis), None))
        for name, steps, got in self.moving:
            try:
                part, pairs = steps.send(got)
                sends.append((name, steps, part, pairs))
            except StopIteration as done:
                self.sums[name] = done.value
        parts = [part for _, _, part, _ in sends]
        inputs, parts, _ = lax.optimization_barrier((inputs, parts, self.marks))
        self.moving = [
            (name, steps, lax.ppermute(part, self.axis, pairs))
            for (name, steps, _, pairs), part in zip(sends, parts)
        ]
        self.marks = [got for _, _, got in self.moving]
        return inputs

    def made(self, *values):
        self.marks.extend(values)


def swap_sum(values, count, axis):
    bit = 1
    while bit < count:
        values = values + lax.ppermute(values, axis, [(i, i ^ bit) for i in range(count)])
        bit *= 2
    return values


def turned(values, cosine, sine):
    return values * cosine + pltpu.roll(values, HEAD_DIM // 2, 1) * sine


def attend_forward_kernel(bounds, projected, cosine, sine, low, high, packed, mixed, peaks, values_t):
    seq = pl.program_id(0)
    score_scale = HEAD_DIM ** (-0.5)
    packed[:, :HEAD_DIM] = turned(projected[:, :HEAD_DIM], cosine[...], sine[...]).astype(BF16)
    packed[:, HEAD_DIM : 2 * HEAD_DIM] = turned(
        projected[:, HEAD_DIM : 2 * HEAD_DIM], cosine[...], sine[...]
    ).astype(BF16)
    packed[:, 2 * HEAD_DIM :] = projected[:, 2 * HEAD_DIM :].astype(BF16)
    for b in range(SEQ_LEN // BLOCK):
        values_t[b] = projected[b * BLOCK : (b + 1) * BLOCK, 2 * HEAD_DIM :].T.astype(BF16)

    def queries_block(b, _):
        start = pl.multiple_of(b * BLOCK, BLOCK)
        queries = packed[pl.ds(start, BLOCK), :HEAD_DIM]
        first = low[0, 0, pl.ds(start, BLOCK)][None, :]
        last = high[0, 0, pl.ds(start, BLOCK)][None, :]

        def keys_block(j, carry):
            peak, total, gathered = carry
            keys = packed[pl.ds(pl.multiple_of(j * BLOCK, BLOCK), BLOCK), HEAD_DIM : 2 * HEAD_DIM]
            scores = dot(keys, queries, ROWS) * score_scale
            place = lax.broadcasted_iota(jnp.int32, (BLOCK, BLOCK), 0) + j * BLOCK
            scores = jnp.where((place >= first) & (place <= last), scores, masked_score)
            new_peak = jnp.maximum(peak, jnp.max(scores, axis=0, keepdims=True))
            shifted = jnp.exp(scores - new_peak)
            fade = jnp.exp(peak - new_peak)
            total = total * fade + jnp.sum(shifted, axis=0, keepdims=True)
            gathered = gathered * fade + jnp.dot(
                values_t[j], shifted.astype(BF16), preferred_element_type=F32
            )
            return new_peak, total, gathered

        peak, total, gathered = lax.fori_loop(
            bounds[seq, b, 0],
            bounds[seq, b, 1],
            keys_block,
            (
                jnp.full((1, BLOCK), masked_score, F32),
                jnp.zeros((1, BLOCK), F32),
                jnp.zeros((HEAD_DIM, BLOCK), F32),
            ),
        )
        mixed[pl.ds(start, BLOCK), :] = (gathered / total).T.astype(BF16)
        peaks[0, 0, 0, pl.ds(start, BLOCK)] = (peak + jnp.log(total))[0]
        return 0

    lax.fori_loop(0, SEQ_LEN // BLOCK, queries_block, 0)


def attend_forward(projected, cosine, sine, low, high, bounds):
    seq_count, heads = cosine.shape[0], projected.shape[1] // (3 * HEAD_DIM)
    rows = seq_count * SEQ_LEN
    per_head = pl.BlockSpec((SEQ_LEN, 3 * HEAD_DIM), lambda s, h, *_: (s, h))
    table = pl.BlockSpec((None, SEQ_LEN, HEAD_DIM), lambda s, h, *_: (s, 0, 0))
    line = pl.BlockSpec((1, 1, SEQ_LEN), lambda s, h, *_: (s, 0, 0))
    return pl.pallas_call(
        attend_forward_kernel,
        grid_spec=pltpu.PrefetchScalarGridSpec(
            num_scalar_prefetch=1,
            grid=(seq_count, heads),
            in_specs=[per_head, table, table, line, line],
            out_specs=[
                per_head,
                pl.BlockSpec((SEQ_LEN, HEAD_DIM), lambda s, h, *_: (s, h)),
                pl.BlockSpec((1, 1, 1, SEQ_LEN), lambda s, h, *_: (s, h, 0, 0)),
            ],
            scratch_shapes=[pltpu.VMEM((SEQ_LEN // BLOCK, HEAD_DIM, BLOCK), BF16)],
        ),
        out_shape=[
            jax.ShapeDtypeStruct(projected.shape, BF16),
            jax.ShapeDtypeStruct((rows, heads * HEAD_DIM), BF16),
            jax.ShapeDtypeStruct((seq_count, heads, 1, SEQ_LEN), F32),
        ],
        compiler_params=pltpu.CompilerParams(vmem_limit_bytes=40 << 20),
        cost_estimate=pl.CostEstimate(
            flops=4 * rows * SEQ_LEN * HEAD_DIM * heads,
            bytes_accessed=rows * heads * HEAD_DIM * 20,
            transcendentals=rows * SEQ_LEN * heads,
        ),
        name="attend_forward",
    )(bounds, projected, cosine, sine, low[:, None], high[:, None])


def attend_backward_kernel(
    bounds, packed, mixed, grad_mixed, peaks, cosine, sine, low, high, grad, keys_t, inner, grad_queries_t, grad_keys, grad_values
):
    seq = pl.program_id(0)
    score_scale = HEAD_DIM ** (-0.5)
    for b in range(SEQ_LEN // BLOCK):
        part = slice(b * BLOCK, (b + 1) * BLOCK)
        keys_t[b] = packed[part, HEAD_DIM : 2 * HEAD_DIM].astype(F32).T.astype(BF16)
        both = grad_mixed[part, :].astype(F32) * mixed[part, :].astype(F32)
        inner[b] = jnp.sum(both.T, axis=0, keepdims=True)
    grad_keys[...] = jnp.zeros_like(grad_keys)
    grad_values[...] = jnp.zeros_like(grad_values)

    def queries_block(b, _):
        start = pl.multiple_of(b * BLOCK, BLOCK)
        queries = packed[pl.ds(start, BLOCK), :HEAD_DIM]
        pulled = grad_mixed[pl.ds(start, BLOCK), :]
        first = low[0, 0, pl.ds(start, BLOCK)][None, :]
        last = high[0, 0, pl.ds(start, BLOCK)][None, :]
        peak = peaks[0, 0, 0, pl.ds(start, BLOCK)][None, :]
        inner_sum = inner[b]

        def keys_block(j, total):
            part = pl.ds(pl.multiple_of(j * BLOCK, BLOCK), BLOCK)
            keys = packed[part, HEAD_DIM : 2 * HEAD_DIM]
            values = packed[part, 2 * HEAD_DIM :]
            scores = dot(keys, queries, ROWS) * score_scale
            place = lax.broadcasted_iota(jnp.int32, (BLOCK, BLOCK), 0) + j * BLOCK
            scores = jnp.where((place >= first) & (place <= last), scores, masked_score)
            probs = jnp.exp(scores - peak)
            grad_probs = dot(values, pulled, ROWS)
            grad_scores = (probs * (grad_probs - inner_sum)).astype(BF16)
            grad_values[part, :] += jnp.dot(probs.astype(BF16), pulled, preferred_element_type=F32)
            grad_keys[part, :] += jnp.dot(grad_scores, queries, preferred_element_type=F32)
            return total + jnp.dot(keys_t[j], grad_scores, preferred_element_type=F32)

        total = lax.fori_loop(
            bounds[seq, b, 0], bounds[seq, b, 1], keys_block, jnp.zeros((HEAD_DIM, BLOCK), F32)
        )
        grad_queries = total.T * score_scale
        rows = pl.ds(start, BLOCK)
        grad[rows, :HEAD_DIM] = turned(grad_queries, cosine[rows, :], -sine[rows, :]).astype(BF16)
        return 0

    lax.fori_loop(0, SEQ_LEN // BLOCK, queries_block, 0)
    grad[:, HEAD_DIM : 2 * HEAD_DIM] = turned(
        grad_keys[...] * score_scale, cosine[...], -sine[...]
    ).astype(BF16)
    grad[:, 2 * HEAD_DIM :] = grad_values[...].astype(BF16)


def attend_backward(packed, mixed, grad_mixed, peaks, cosine, sine, low, high, bounds):
    seq_count, heads = cosine.shape[0], packed.shape[1] // (3 * HEAD_DIM)
    rows = seq_count * SEQ_LEN
    per_head = pl.BlockSpec((SEQ_LEN, 3 * HEAD_DIM), lambda s, h, *_: (s, h))
    single = pl.BlockSpec((SEQ_LEN, HEAD_DIM), lambda s, h, *_: (s, h))
    table = pl.BlockSpec((None, SEQ_LEN, HEAD_DIM), lambda s, h, *_: (s, 0, 0))
    line = pl.BlockSpec((1, 1, SEQ_LEN), lambda s, h, *_: (s, 0, 0))
    blocks = SEQ_LEN // BLOCK
    return pl.pallas_call(
        attend_backward_kernel,
        grid_spec=pltpu.PrefetchScalarGridSpec(
            num_scalar_prefetch=1,
            grid=(seq_count, heads),
            in_specs=[
                per_head,
                single,
                single,
                pl.BlockSpec((1, 1, 1, SEQ_LEN), lambda s, h, *_: (s, h, 0, 0)),
                table,
                table,
                line,
                line,
            ],
            out_specs=per_head,
            scratch_shapes=[
                pltpu.VMEM((blocks, HEAD_DIM, BLOCK), BF16),
                pltpu.VMEM((blocks, 1, BLOCK), F32),
                pltpu.VMEM((blocks, HEAD_DIM, BLOCK), F32),
                pltpu.VMEM((SEQ_LEN, HEAD_DIM), F32),
                pltpu.VMEM((SEQ_LEN, HEAD_DIM), F32),
            ],
        ),
        out_shape=jax.ShapeDtypeStruct(packed.shape, BF16),
        compiler_params=pltpu.CompilerParams(vmem_limit_bytes=40 << 20),
        cost_estimate=pl.CostEstimate(
            flops=10 * rows * SEQ_LEN * HEAD_DIM * heads,
            bytes_accessed=rows * heads * HEAD_DIM * 20,
            transcendentals=rows * SEQ_LEN * heads,
        ),
        name="attend_backward",
    )(bounds, packed, mixed, grad_mixed, peaks, cosine, sine, low[:, None], high[:, None])


def feed_kernel(units, second, cotangent, expand, shrink, columns, hidden, grads):
    step = 176 if units % 176 == 0 else units
    for at in range(0, units, step):
        part = slice(at, at + step)
        upper = slice(units + at, units + at + step)
        gate = dot(expand[part, :], second[...], ROWS) + columns[part, 0:1]
        up = dot(expand[upper, :], second[...], ROWS) + columns[part, 1:2]
        grad_hidden = dot(shrink[part, :], cotangent[...], ROWS) * columns[part, 2:3]
        normal = 0.5 * (1.0 + lax.erf(gate * (0.5**0.5)))
        density = jnp.exp(-0.5 * gate * gate) * (0.5 / jnp.pi) ** 0.5
        gelu = gate * normal
        hidden[part, :] = (gelu * up * columns[part, 2:3]).astype(BF16)
        grads[part, :] = (grad_hidden * up * (normal + gate * density)).astype(BF16)
        grads[upper, :] = (grad_hidden * gelu).astype(BF16)


def feed(second, cotangent, expand, shrink, columns):
    rows, width = second.shape
    units = shrink.shape[0]
    tile = 256
    tokens = pl.BlockSpec((tile, width), lambda i: (i, 0))
    whole = lambda a: pl.BlockSpec(a.shape, lambda i: (0, 0), pipeline_mode=pl.Buffered(1))
    return pl.pallas_call(
        functools.partial(feed_kernel, units),
        grid=(rows // tile,),
        in_specs=[tokens, tokens, whole(expand), whole(shrink), whole(columns)],
        out_specs=[
            pl.BlockSpec((units, tile), lambda i: (0, i)),
            pl.BlockSpec((2 * units, tile), lambda i: (0, i)),
        ],
        out_shape=[
            jax.ShapeDtypeStruct((units, rows), BF16),
            jax.ShapeDtypeStruct((2 * units, rows), BF16),
        ],
        compiler_params=pltpu.CompilerParams(vmem_limit_bytes=50 << 20),
        cost_estimate=pl.CostEstimate(
            flops=6 * rows * width * units,
            bytes_accessed=4 * rows * width + 6 * units * (rows + width),
            transcendentals=2 * rows * units,
        ),
        name="feed",
    )(second, cotangent, expand, shrink, columns)


def weave_kernel(gate, up, out):
    out[:, 0, :] = gate[...].astype(F32)
    out[:, 1, :] = up[...].astype(F32)


def weave(gate, up):
    rows, width = gate.shape
    tile = 256
    part = pl.BlockSpec((rows, tile), lambda j: (0, j))
    return pl.pallas_call(
        weave_kernel,
        grid=(width // tile,),
        in_specs=[part, part],
        out_specs=pl.BlockSpec((rows, 2, tile), lambda j: (0, 0, j)),
        out_shape=jax.ShapeDtypeStruct((rows, 2, width), F32),
        compiler_params=pltpu.CompilerParams(vmem_limit_bytes=40 << 20),
        cost_estimate=pl.CostEstimate(flops=0, bytes_accessed=12 * rows * width, transcendentals=0),
        name="weave",
    )(gate, up)


def cuts(total, pieces):
    step = -(-total // pieces)
    step = -(-step // 16) * 16
    return [(at, min(at + step, total)) for at in range(0, total, step)]


def local(
    dp,
    tp,
    tokens,
    segment_ids,
    prefix_lengths,
    positions,
    norm_gains,
    norm_offsets,
    input_weight,
    input_offset,
    output_weight,
    output_offset,
    expand_weight,
    expand_offset,
    shrink_weight,
    shrink_offset,
    cotangent,
):
    residual_scale = (2.0 * LAYERS) ** 0.5
    seq_count = segment_ids.shape[0]
    group_rows = seq_count * SEQ_LEN
    width = tokens.shape[1]
    units_used = expand_weight.shape[2]
    units = -(-units_used // 176) * 176
    heads_width = output_weight.shape[0]
    gather = lambda a: lax.all_gather(a, "tp", axis=0, tiled=True)
    scatter = lambda a: lax.psum_scatter(a, "tp", scatter_dimension=0, tiled=True).astype(F32)

    pad = ((0, units - units_used), (0, 0))
    turned_expand = jnp.transpose(expand_weight, (2, 1, 0))
    expand = jnp.concatenate(
        [jnp.pad(turned_expand[:, 0], pad), jnp.pad(turned_expand[:, 1], pad)], axis=0
    )
    shrink = jnp.pad(shrink_weight, pad)
    unit_index = lax.axis_index("tp") * units_used + lax.iota(jnp.int32, units_used)
    keep_units = (unit_index < FF_USED).astype(F32)
    columns = jnp.pad(jnp.stack([expand_offset[0], expand_offset[1], keep_units], axis=1), pad)

    row_at = lax.broadcasted_iota(jnp.int32, positions.shape, 1)
    low = row_at - positions
    matches = segment_ids[:, :, None] == lax.iota(jnp.int32, prefix_lengths.shape[1])
    own_prefix = jnp.sum(jnp.where(matches, prefix_lengths[:, None, :], 0), axis=2)
    high = jnp.maximum(row_at, low + own_prefix - 1)
    bounds = jnp.stack(
        [
            jnp.min(low.reshape(seq_count, -1, BLOCK), axis=2) // BLOCK,
            jnp.max(high.reshape(seq_count, -1, BLOCK), axis=2) // BLOCK + 1,
        ],
        axis=2,
    )
    cosine, sine = rotary_tables(positions)

    first_hat, first_scale = normalize(tokens.astype(F32))
    first_norm = first_hat * norm_gains[0] + norm_offsets[0]
    first_all = gather(first_norm.astype(BF16))
    cotangent_all = gather(cotangent)
    full_output = gather(output_weight)
    projected = jnp.dot(first_all, input_weight, preferred_element_type=F32) + input_offset
    packed, mixed, peaks = attend_forward(projected, cosine, sine, low, high, bounds)
    own_heads = lax.all_to_all(mixed, "tp", split_axis=0, concat_axis=1, tiled=True)
    attention = jnp.dot(own_heads, full_output, preferred_element_type=F32) + output_offset
    middle = residual_scale * first_norm + attention
    second_hat, second_scale = normalize(middle)
    second_norm = second_hat * norm_gains[1] + norm_offsets[1]
    second_all = gather(second_norm.astype(BF16))
    hidden, grads = feed(second_all, cotangent_all, expand, shrink, columns)

    line = Line(dp, "dp")
    mul = lambda a, b: jnp.dot(a, b, preferred_element_type=F32).astype(BF16)
    unit_cuts = cuts(units_used, 3)
    width_cuts = cuts(width, 3)
    shrink_part = [None] * 3
    expand_part = [[None] * 3, [None] * 3]
    a, b = unit_cuts[0]
    line.add("s0", mul(hidden[a:b], cotangent_all))

    hidden, cotangent_all, grads, expand = line.turn(hidden, cotangent_all, grads, expand)
    for k in (1, 2):
        a, b = unit_cuts[k]
        line.add("s%d" % k, mul(hidden[a:b], cotangent_all))
    grad_second_part = dot(grads, expand, COLS).astype(BF16)
    line.made(line.waiting[0][1], line.waiting[1][1], grad_second_part)

    grads, second_all, hidden, shrink, grad_second_part = line.turn(
        grads, second_all, hidden, shrink, grad_second_part
    )
    grad_second_sum = scatter(grad_second_part)
    for k in range(3):
        a, b = unit_cuts[k]
        line.add("g%d" % k, mul(grads[a:b], second_all))
    shrink_sum_part = dot(hidden, shrink, COLS).astype(BF16)
    line.made(shrink_sum_part, *[p for _, p in line.waiting[-3:]])

    grads, second_all, shrink_sum_part, cotangent = line.turn(
        grads, second_all, shrink_sum_part, cotangent
    )
    shrink_sum = scatter(shrink_sum_part)
    for k in range(3):
        a, b = unit_cuts[k]
        line.add("u%d" % k, mul(grads[units + a : units + b], second_all))
    expand_offset_grad = jnp.sum(grads.astype(F32), axis=1).reshape(2, units)[:, :units_used]
    grad_output = cotangent.astype(F32)
    shrink_offset_grad = jnp.sum(grad_output, axis=0)
    line.made(expand_offset_grad, shrink_offset_grad, *[p for _, p in line.waiting[-3:]])

    line.turn()

    grad_second_sum, full_output = line.turn(grad_second_sum, full_output)
    grad_second = residual_scale * grad_output + grad_second_sum
    grad_middle, second_gain_grad, second_offset_grad = normalize_back(
        grad_second, norm_gains[1], second_hat, second_scale
    )
    grad_attention = grad_middle.astype(BF16)
    output_offset_grad = jnp.sum(grad_attention.astype(F32), axis=0)
    grad_own = dot(grad_attention, full_output, ROWS).astype(BF16)
    grad_mixed = lax.all_to_all(grad_own, "tp", split_axis=1, concat_axis=0, tiled=True)
    attention_all = gather(grad_attention)
    line.made(grad_mixed, second_gain_grad, second_offset_grad, output_offset_grad)

    grad_mixed, packed, mixed = line.turn(grad_mixed, packed, mixed)
    grad_projected = attend_backward(
        packed, mixed, grad_mixed, peaks, cosine, sine, low, high, bounds
    )
    line.made(grad_projected)

    grad_projected, first_all, input_weight = line.turn(grad_projected, first_all, input_weight)
    grad_first_part = dot(grad_projected, input_weight, ROWS).astype(BF16)
    input_offset_grad = jnp.sum(grad_projected.astype(F32), axis=0)
    line.made(grad_first_part, input_offset_grad)

    grad_projected, first_all, grad_first_part = line.turn(grad_projected, first_all, grad_first_part)
    grad_first_sum = scatter(grad_first_part)
    for k in range(3):
        a, b = width_cuts[k]
        line.add("i%d" % k, dot(first_all[:, a:b], grad_projected, COLS))
    line.made(*[p for _, p in line.waiting[-3:]])

    attention_all, mixed = line.turn(attention_all, mixed)
    line.add("o", dot(mixed, attention_all, COLS))
    line.made(line.waiting[-1][1])

    shrink_sum, second_hat = line.turn(shrink_sum, second_hat)
    layer_out = (
        residual_scale * (second_hat * norm_gains[1] + norm_offsets[1]) + shrink_sum + shrink_offset
    )
    shrink_grad = jnp.concatenate([line.sums["s%d" % k] for k in range(3)]).astype(F32)
    line.made(layer_out, shrink_grad)
    while "u2" not in line.sums:
        line.turn()
    expand_grad = weave(
        jnp.concatenate([line.sums["g%d" % k] for k in range(3)]),
        jnp.concatenate([line.sums["u%d" % k] for k in range(3)]),
    )
    line.made(expand_grad)

    grad_first_sum, grad_middle = line.turn(grad_first_sum, grad_middle)
    grad_first = residual_scale * grad_middle + grad_first_sum
    tokens_grad, first_gain_grad, first_offset_grad = normalize_back(
        grad_first, norm_gains[0], first_hat, first_scale
    )
    line.made(tokens_grad, first_gain_grad, first_offset_grad)
    while line.waiting or line.moving:
        line.turn()

    whole_sums = swap_sum(
        jnp.stack(
            [
                first_gain_grad,
                second_gain_grad,
                first_offset_grad,
                second_offset_grad,
                output_offset_grad,
                shrink_offset_grad,
            ]
        ),
        tp,
        "tp",
    )
    whole_sums = swap_sum(whole_sums, dp, "dp")
    group_sums = swap_sum(
        jnp.concatenate([expand_offset_grad.reshape(-1), input_offset_grad]), dp, "dp"
    )
    return (
        layer_out,
        tokens_grad,
        jnp.concatenate([line.sums["i%d" % k] for k in range(3)]).astype(F32),
        group_sums[2 * units_used :],
        line.sums["o"].astype(F32),
        whole_sums[4],
        jnp.transpose(expand_grad, (2, 1, 0)),
        group_sums[: 2 * units_used].reshape(2, units_used),
        shrink_grad,
        whole_sums[5],
        whole_sums[0:2],
        whole_sums[2:4],
    )


def solution(mesh):
    in_specs = (
        P(("dp", "tp"), None),
        P("dp", None),
        P("dp", None),
        P("dp", None),
        P(),
        P(),
        P(None, "tp"),
        P("tp"),
        P("tp", None),
        P(),
        P(None, None, "tp"),
        P(None, "tp"),
        P("tp", None),
        P(),
        P(("dp", "tp"), None),
    )
    out_specs = (
        P(("dp", "tp"), None),
        P(("dp", "tp"), None),
        P(None, "tp"),
        P("tp"),
        P("tp", None),
        P(),
        P(None, None, "tp"),
        P(None, "tp"),
        P("tp", None),
        P(),
        P(),
        P(),
    )
    return jax.shard_map(
        functools.partial(local, mesh.shape["dp"], mesh.shape["tp"]),
        mesh=mesh,
        in_specs=in_specs,
        out_specs=out_specs,
        check_vma=False,
    )
```

time: 1300 us -> 845 us (0.65)
  waiting for transfers between devices: 655 us -> 334 us
  local copies, waits for them, and re-layouts: 215 us -> 27.5 us
  starting transfers between devices: 0.37 us -> 99.2 us
  Pallas kernels: 0 us -> 97.3 us
  blocking collectives: 86.5 us -> 0 us
  matrix products: 187 us -> 145 us
    psum x1 -> x0, waiting for transfers between devices: 380 us -> none  [local(): lax.psum(expand_weight_grad.astype(jnp.bfloat16), 'dp').astype(jnp.float32)]
    ppermute x0 -> x46, waiting for transfers between devices: none -> 171 us  [the longest x39 147 us: turn(): lax.ppermute(part, self.axis, pairs)]
    reduce_scatter x3, waiting for transfers between devices: 138 us -> 0.01 us  [local(): lax.psum_scatter(a, 'tp', scatter_dimension=0, tiled=True).astype(F32)]
    dynamic_update_slice x16 -> x0, local copies, waits for them, and re-layouts: 131 us -> none  [the longest x12 123 us: local(): lax.map(attend_backward, (queries, keys_low, values_low, grad_mixed, log_...]
    pallas_call x0 -> x4, Pallas kernels: none -> 97.3 us  [the longest x1 40 us: feed(): pl.pallas_call(functools.partial(feed_kernel, units), grid=(rows // tile,...]
    ppermute x0 -> x46, starting transfers between devices: none -> 88.7 us  [the longest x39 85.1 us: turn(): lax.ppermute(part, self.axis, pairs)]
    psum x2 -> x0, blocking collectives: 58 us -> none  [the longest x1 46.2 us: local(): lax.psum((jnp.stack([first_gain_grad, second_gain_grad]), jnp.stack([firs...]
    dot_general x26 -> x19, matrix products: 187 us -> 145 us  [the longest x8 65 us: dot(): return lax.dot_general(left, right, dims, preferred_element_type=F32)]
  transfers between devices with their start and end apart: 9 -> 56, of which waited for: 8 -> 27; matrix products, arithmetic and copies ran while one was open for 15% -> 31% of each run, Pallas kernels for 0% -> 7%
where the time goes in v1:
time: 845 us; the launch traced here: 833 us
  waiting for transfers between devices  334 us (40%)
  matrix products  145 us (17%)
  other arithmetic  114 us (13%)
  starting transfers between devices  99.2 us (12%)
  Pallas kernels  97.3 us (12%)
  local copies, waits for them, and re-layouts  27.5 us (3%)
  between operations  15.7 us (2%)
    all_gather x5, waiting for transfers between devices, local(): gather = lambda a: lax.all_gather(a, 'tp', axis=0, tiled=True)  154 us
    ppermute x39, waiting for transfers between devices, turn(): lax.ppermute(part, self.axis, pairs)  147 us
    ppermute x39, starting transfers between devices, turn(): lax.ppermute(part, self.axis, pairs)  85.1 us
    dot_general x8, matrix products, dot(): return lax.dot_general(left, right, dims, preferred_element_type=F32)  65 us
    dot_general x9, matrix products, local(): mul = lambda a, b: jnp.dot(a, b, preferred_element_type=F32).astype(BF16)  64.2 us
    convert_element_type x26, other arithmetic, line_steps(): part = (part.astype(F32) + got.astype(F32)).astype(BF16)  45 us
    pallas_call x1, Pallas kernels, feed(): pl.pallas_call(functools.partial(feed_kernel, units), grid=(rows // tile,...  40 us
    pallas_call x1, Pallas kernels, attend_backward(): pl.pallas_call(attend_backward_kernel, grid_spec=pltpu.PrefetchScalarGrid...  26.6 us
  transfers between devices with their start and end apart: 56, of which 27 were waited for; matrix products, arithmetic and copies ran while one was open for 31% of the time, Pallas kernels for 7%

profile of v1, /device:TPU:2, one launch (start us, length us, event | category | flops | bytes accessed | tf_op | source)
XLA Modules:
  0.0 833.0 jit_solution(6825220407057607312)
XLA Ops:
  20.1 47.8 %all-gather.6.cloned.1.call-done = bf16[2048,2048]{1,0:T(8,128)(2,1)} async-done(((bf16[256,2048]{1,0:T(8,128)(2,1)}), bf16[2048,2048]{1,0:T(8,128)(2,1)}) %all-gather.6.cloned.1.call-update) | async-done | bytes 8388624 | tf_op jit(solution)/shard_map/all_gather | solution.py:390
  67.9 9.2 %broadcast_add_fusion.projected = f32[2048,768]{1,0:T(8,128)S(1)} fusion(f32[768]{0:T(1024)S(1)} %copy-done.81, bf16[2048,2048]{1,0:T(8,128)(2,1)} %all-gather.6.cloned.1.call-done, bf16[2048,768]{1,0:T(8,128)(2,1)S(1)} %copy-done), kind=kOutput, calls=%fused_computation.22 | convolution fusion | flops 6444023808 | bytes 17828864 | tf_op jit(solution)/shard_map/dot_general | solution.py:422
  77.1 23.8 %attend_forward.1 = (bf16[2048,768]{1,0:T(8,128)(2,1)S(1)}, bf16[2048,256]{1,0:T(8,128)(2,1)S(1)}, f32[2,2,1,1024]{3,2,1,0:T(1,128)S(1)}) custom-call(s32[2,4,2]{2,1,0:T(4,128)S(1)} %pad_add_fusion.bounds, f32[2048,768]{1,0:T(8,128)S(1)} %broadcast_add_fusion.projected, f32[2,1024,128]{2,1,0:T(8,128)S(1)} %copy-done.5, f32[2,1024,128]{2,1,0:T(8,128)S(1)} %copy-done.7, ...), custom_call_target="tpu_custom_call" | custom-call | flops 2147483648 | bytes 10485760 | tf_op jit(solution)/shard_map/attend_forward/pallas_call | solution.py:171
  111.0 24.5 %all-gather.8.cloned.1.call-done = bf16[2048,2048]{1,0:T(8,128)(2,1)} async-done(((bf16[256,2048]{1,0:T(8,128)(2,1)}), bf16[2048,2048]{1,0:T(8,128)(2,1)}) %all-gather.8.cloned.1.call-update) | async-done | bytes 8388624 | tf_op jit(solution)/shard_map/all_gather | solution.py:390
  153.8 12.4 %fusion.2.expand = bf16[1408,2048]{1,0:T(8,128)(2,1)} fusion(bf16[684,2048]{1,0:T(8,128)(2,1)S(1)} %get-tuple-element.175, bf16[684,2048]{1,0:T(8,128)(2,1)S(1)} %get-tuple-element.174), kind=kLoop, calls=%fused_computation.9 | loop fusion | flops 23068672 | bytes 11370496 | tf_op jit(solution)/shard_map/concatenate | solution.py:395
  166.3 25.6 %all-gather.12.cloned.1.call-done.cotangent = bf16[2048,2048]{1,0:T(8,128)(2,1)} async-done(((bf16[256,2048]{1,0:T(8,128)(2,1)}), bf16[2048,2048]{1,0:T(8,128)(2,1)}) %all-gather.12.cloned.1.call-update) | async-done | bytes 8388624 | tf_op jit(solution)/shard_map/all_gather | solution.py:390
  191.8 56.2 %all-gather.10.cloned.1.call-done.second = bf16[2048,2048]{1,0:T(8,128)(2,1)} async-done(((bf16[256,2048]{1,0:T(8,128)(2,1)}), bf16[2048,2048]{1,0:T(8,128)(2,1)}) %all-gather.10.cloned.1.call-update) | async-done | bytes 8388624 | tf_op jit(solution)/shard_map/all_gather | solution.py:390
  248.0 40.0 %feed.1 = (bf16[704,2048]{1,0:T(8,128)(2,1)S(1)}, bf16[1408,2048]{1,0:T(8,128)(2,1)}) custom-call(bf16[2048,2048]{1,0:T(8,128)(2,1)} %all-gather.10.cloned.1.call-done.second, bf16[2048,2048]{1,0:T(8,128)(2,1)} %all-gather.12.cloned.1.call-done.cotangent, bf16[1408,2048]{1,0:T(8,128)(2,1)} %fusion.2.expand, bf16[704,2048]{1,0:T(8,128)(2,1)} %pad.16.shrink, ...), custom_call_target="tpu_custom_call" | custom-call | flops 17716740096 | bytes 34078720 | tf_op jit(solution)/shard_map/feed/pallas_call | solution.py:315
  288.0 7.6 fusion.49
  300.0 15.6 %convolution_convert_fusion.2 = bf16[2048,2048]{1,0:T(8,128)(2,1)} fusion(bf16[1408,2048]{1,0:T(8,128)(2,1)S(1)} %copy-done.29, bf16[1408,2048]{1,0:T(8,128)(2,1)S(1)} %copy-done.30), kind=kOutput, calls=%fused_computation.7 | convolution fusion | flops 11815354368 | bytes 19922944 | tf_op jit(solution)/shard_map/dot_general | solution.py:26
  336.5 8.0 fusion.44
  344.5 7.8 fusion.46
  352.3 9.5 %convolution_convert_fusion.1 = bf16[2048,2048]{1,0:T(8,128)(2,1)} fusion(bf16[704,2048]{1,0:T(8,128)(2,1)S(1)} %copy-done.21, bf16[704,2048]{1,0:T(8,128)(2,1)S(1)} %copy-done.47), kind=kOutput, calls=%fused_computation.6 | convolution fusion | flops 5909774336 | bytes 14155776 | tf_op jit(solution)/shard_map/dot_general | solution.py:26
  404.4 13.2 %collective-permute-done.5 = bf16[240,2048]{1,0:T(8,128)(2,1)S(1)} collective-permute-done((bf16[240,2048]{1,0:T(8,128)(2,1)}, bf16[240,2048]{1,0:T(8,128)(2,1)S(1)}, u32[]{:S(2)}, u32[]{:S(2)}) %collective-permute-start.5) | collective-permute-done | bytes 983072 | tf_op jit(solution)/shard_map/ppermute | solution.py:94
  425.0 17.6 %collective-permute-done.7 = bf16[240,2048]{1,0:T(8,128)(2,1)S(1)} collective-permute-done((bf16[240,2048]{1,0:T(8,128)(2,1)S(1)}, bf16[240,2048]{1,0:T(8,128)(2,1)S(1)}, u32[]{:S(2)}, u32[]{:S(2)}) %collective-permute-start.7) | collective-permute-done | bytes 983072 | tf_op jit(solution)/shard_map/ppermute | solution.py:94
  499.1 26.6 %attend_backward.1 = bf16[2048,768]{1,0:T(8,128)(2,1)S(1)} custom-call(s32[2,4,2]{2,1,0:T(4,128)S(1)} %copy-done.16, bf16[2048,768]{1,0:T(8,128)(2,1)S(1)} %copy-done.18, bf16[2048,256]{1,0:T(8,128)(2,1)S(1)} %copy-done.3, bf16[2048,256]{1,0:T(8,128)(2,1)} %bitcast.16.grad_mixed, f32[2,2,1,1024]{3,2,1,0:T(1,128)S(1)} %get-tuple-element.120.peaks, ...), custom_call_target="tpu_custom_call" | custom-call | flops 5368709120 | bytes 10485760 | tf_op jit(solution)/shard_map/attend_backward/pallas_call | solution.py:258
  535.8 9.0 %convolution_convert_fusion = bf16[2048,2048]{1,0:T(8,128)(2,1)} fusion(bf16[2048,768]{1,0:T(8,128)(2,1)S(1)} %attend_backward.1, bf16[2048,768]{1,0:T(8,128)(2,1)S(1)} %copy-done), kind=kOutput, calls=%fused_computation.5 | convolution fusion | flops 6446645248 | bytes 14680064 | tf_op jit(solution)/shard_map/dot_general | solution.py:26
  620.4 8.1 collective-permute-done.23
  640.7 15.6 %collective-permute-done.25 = bf16[688,768]{1,0:T(8,128)(2,1)S(1)} collective-permute-done((bf16[688,768]{1,0:T(8,128)(2,1)S(1)}, bf16[688,768]{1,0:T(8,128)(2,1)S(1)}, u32[]{:S(2)}, u32[]{:S(2)}) %collective-permute-start.25) | collective-permute-done | bytes 1056800 | tf_op jit(solution)/shard_map/ppermute | solution.py:94
  670.7 9.2 %collective-permute-done.27 = bf16[688,768]{1,0:T(8,128)(2,1)} collective-permute-done((bf16[688,768]{1,0:T(8,128)(2,1)}, bf16[688,768]{1,0:T(8,128)(2,1)}, u32[]{:S(2)}, u32[]{:S(2)}) %collective-permute-start.27) | collective-permute-done | bytes 1056800 | tf_op jit(solution)/shard_map/ppermute | solution.py:94
  726.3 14.8 %collective-permute-done.35 = bf16[256,2048]{1,0:T(8,128)(2,1)S(1)} collective-permute-done((bf16[256,2048]{1,0:T(8,128)(2,1)}, bf16[256,2048]{1,0:T(8,128)(2,1)S(1)}, u32[]{:S(2)}, u32[]{:S(2)}) %collective-permute-start.35) | collective-permute-done | bytes 1048608 | tf_op jit(solution)/shard_map/ppermute | solution.py:94
  752.2 19.4 %collective-permute-done.38 = f32[2136]{0:T(1024)S(1)} collective-permute-done((f32[2136]{0:T(1024)S(1)}, f32[2136]{0:T(1024)S(1)}, u32[]{:S(2)}, u32[]{:S(2)}) %collective-permute-start.38) | collective-permute-done | bytes 8576 | tf_op jit(solution)/shard_map/ppermute | solution.py:107
  781.4 18.1 %collective-permute-done.36 = bf16[672,768]{1,0:T(8,128)(2,1)S(1)} collective-permute-done((bf16[672,768]{1,0:T(8,128)(2,1)}, bf16[672,768]{1,0:T(8,128)(2,1)S(1)}, u32[]{:S(2)}, u32[]{:S(2)}) %collective-permute-start.36) | collective-permute-done | bytes 1032224 | tf_op jit(solution)/shard_map/ppermute | solution.py:94
  806.0 18.5 %collective-permute-done.40 = bf16[256,2048]{1,0:T(8,128)(2,1)S(1)} collective-permute-done((bf16[256,2048]{1,0:T(8,128)(2,1)S(1)}, bf16[256,2048]{1,0:T(8,128)(2,1)S(1)}, u32[]{:S(2)}, u32[]{:S(2)}) %collective-permute-start.40) | collective-permute-done | bytes 1048608 | tf_op jit(solution)/shard_map/ppermute | solution.py:94
  (399 shorter events, 359.3 us)
Async XLA Ops:
  7.2 60.7 %all-gather.6.cloned.1.call-start = ((), (), s32[]{:S(2)}) async-start(), calls=%async_computation.5 | async-start | bytes 9437184 | tf_op jit(solution)/shard_map/all_gather | solution.py:390
  12.1 123.4 %all-gather.8.cloned.1.call-start = ((), (), s32[]{:S(2)}) async-start(), calls=%async_computation.6 | async-start | bytes 9437184 | tf_op jit(solution)/shard_map/all_gather | solution.py:390
  12.9 179.0 %all-gather.12.cloned.1.call-start = ((), (), s32[]{:S(2)}) async-start(), calls=%async_computation.8 | async-start | bytes 9437184 | tf_op jit(solution)/shard_map/all_gather | solution.py:390
  105.9 29.6 %all-to-all-start = ((bf16[8,256,256]{1,2,0:T(8,128)(2,1)}), bf16[8,256,256]{1,2,0:T(8,128)(2,1)}, u32[]{:S(2)}, u32[]{:S(2)}) async-start(bf16[8,256,256]{1,2,0:T(8,128)(2,1)} %copy.77), calls=%async_computation | async-start | bytes 2097152 | tf_op jit(solution)/shard_map/all_to_all | solution.py:424
  110.5 137.5 %all-gather.10.cloned.1.call-start = ((), (), s32[]{:S(2)}) async-start(), calls=%async_computation.7 | async-start | bytes 9437184 | tf_op jit(solution)/shard_map/all_gather | solution.py:390
  144.8 299.1 %reduce-scatter.6.cloned.1.call-start = ((), (), s32[]{:S(2)}) async-start(), calls=%async_computation.10 | async-start | bytes 9437184 | tf_op jit(solution)/shard_map/reduce_scatter | solution.py:391
  295.6 33.2 %collective-permute-start = (bf16[240,2048]{1,0:T(8,128)(2,1)}, bf16[240,2048]{1,0:T(8,128)(2,1)}, u32[]{:S(2)}, u32[]{:S(2)}) collective-permute-start(bf16[240,2048]{1,0:T(8,128)(2,1)} %fusion.49), channel_id=1, source_target_pairs={{0,8},{24,16},{1,9},{25,17},{2,10},{26,18},{3,11},{27,19},{4,12},{... | collective-permute-start | bytes 2949128 | tf_op jit(solution)/shard_map/ppermute | solution.py:94
  331.7 235.5 %reduce-scatter.4.cloned.1.call-start = ((), (), s32[]{:S(2)}) async-start(), calls=%async_computation.9 | async-start | bytes 9437184 | tf_op jit(solution)/shard_map/reduce_scatter | solution.py:391
  331.7 36.9 %collective-permute-start.1 = (bf16[240,2048]{1,0:T(8,128)(2,1)}, bf16[240,2048]{1,0:T(8,128)(2,1)}, u32[]{:S(2)}, u32[]{:S(2)}) collective-permute-start(bf16[240,2048]{1,0:T(8,128)(2,1)} %fusion.26), channel_id=1, source_target_pairs={{8,16},{16,8},{9,17},{17,9},{10,18},{18,10},{11,19},{19,11},{12,20... | collective-permute-start | bytes 2949128 | tf_op jit(solution)/shard_map/ppermute | solution.py:94
  333.4 37.9 %collective-permute-start.2 = (bf16[240,2048]{1,0:T(8,128)(2,1)}, bf16[240,2048]{1,0:T(8,128)(2,1)}, u32[]{:S(2)}, u32[]{:S(2)}) collective-permute-start(bf16[240,2048]{1,0:T(8,128)(2,1)} %convolution_convert_fusion.7), channel_id=1, source_target_pairs={{0,8},{24,16},{1,9},{25,17},{2,10},{26,18},{3,11},{27,19},{4,12},{... | collective-permute-start | bytes 2949128 | tf_op jit(solution)/shard_map/ppermute | solution.py:94
  373.9 225.4 %all-gather.14.cloned.1.call-start = ((), (), s32[]{:S(2)}) async-start(), calls=%async_computation.11 | async-start | bytes 9437184 | tf_op jit(solution)/shard_map/all_gather | solution.py:390
  373.9 27.5 %collective-permute-start.3 = (bf16[204,2048]{1,0:T(8,128)(2,1)}, bf16[204,2048]{1,0:T(8,128)(2,1)}, u32[]{:S(2)}, u32[]{:S(2)}) collective-permute-start(bf16[204,2048]{1,0:T(8,128)(2,1)} %convolution_convert_fusion.9), channel_id=1, source_target_pairs={{0,8},{24,16},{1,9},{25,17},{2,10},{26,18},{3,11},{27,19},{4,12},{... | collective-permute-start | bytes 2506760 | tf_op jit(solution)/shard_map/ppermute | solution.py:94
  391.9 25.8 %collective-permute-start.5 = (bf16[240,2048]{1,0:T(8,128)(2,1)}, bf16[240,2048]{1,0:T(8,128)(2,1)S(1)}, u32[]{:S(2)}, u32[]{:S(2)}) collective-permute-start(bf16[240,2048]{1,0:T(8,128)(2,1)} %add_convert_fusion.17), channel_id=1, source_target_pairs={{8,0},{16,24},{9,1},{17,25},{10,2},{18,26},{11,3},{19,27},{12,4},{... | collective-permute-start | bytes 2949128 | tf_op jit(solution)/shard_map/ppermute | solution.py:94
  452.1 28.6 %collective-permute-start.11 = (bf16[204,2048]{1,0:T(8,128)(2,1)}, bf16[204,2048]{1,0:T(8,128)(2,1)}, u32[]{:S(2)}, u32[]{:S(2)}) collective-permute-start(bf16[204,2048]{1,0:T(8,128)(2,1)} %add_convert_fusion.21), channel_id=1, source_target_pairs={{8,0},{16,24},{9,1},{17,25},{10,2},{18,26},{11,3},{19,27},{12,4},{... | collective-permute-start | bytes 2506760 | tf_op jit(solution)/shard_map/ppermute | solution.py:94
  472.2 195.4 %reduce-scatter.8.cloned.1.call-start = ((), (), s32[]{:S(2)}) async-start(), calls=%async_computation.12 | async-start | bytes 9437184 | tf_op jit(solution)/shard_map/reduce_scatter | solution.py:391
  487.6 38.1 %collective-permute-start.13 = (bf16[204,2048]{1,0:T(8,128)(2,1)}, bf16[204,2048]{1,0:T(8,128)(2,1)S(1)}, u32[]{:S(2)}, u32[]{:S(2)}) collective-permute-start(bf16[204,2048]{1,0:T(8,128)(2,1)} %fusion.52), channel_id=1, source_target_pairs={{0,8},{24,16},{1,9},{25,17},{2,10},{26,18},{3,11},{27,19},{4,12},{... | collective-permute-start | bytes 2506760 | tf_op jit(solution)/shard_map/ppermute | solution.py:94
  491.0 35.9 %collective-permute-start.12 = (bf16[240,2048]{1,0:T(8,128)(2,1)}, bf16[240,2048]{1,0:T(8,128)(2,1)S(1)}, u32[]{:S(2)}, u32[]{:S(2)}) collective-permute-start(bf16[240,2048]{1,0:T(8,128)(2,1)} %fusion.30), channel_id=1, source_target_pairs={{8,16},{16,8},{9,17},{17,9},{10,18},{18,10},{11,19},{19,11},{12,20... | collective-permute-start | bytes 2949128 | tf_op jit(solution)/shard_map/ppermute | solution.py:94
  491.7 37.3 %collective-permute-start.14 = (bf16[240,2048]{1,0:T(8,128)(2,1)}, bf16[240,2048]{1,0:T(8,128)(2,1)}, u32[]{:S(2)}, u32[]{:S(2)}) collective-permute-start(bf16[240,2048]{1,0:T(8,128)(2,1)} %add_convert_fusion.14), channel_id=1, source_target_pairs={{8,0},{16,24},{9,1},{17,25},{10,2},{18,26},{11,3},{19,27},{12,4},{... | collective-permute-start | bytes 2949128 | tf_op jit(solution)/shard_map/ppermute | solution.py:94
  570.4 28.9 %collective-permute-start.20 = (bf16[204,2048]{1,0:T(8,128)(2,1)}, bf16[204,2048]{1,0:T(8,128)(2,1)}, u32[]{:S(2)}, u32[]{:S(2)}) collective-permute-start(bf16[204,2048]{1,0:T(8,128)(2,1)} %add_convert_fusion.20), channel_id=1, source_target_pairs={{8,0},{16,24},{9,1},{17,25},{10,2},{18,26},{11,3},{19,27},{12,4},{... | collective-permute-start | bytes 2506760 | tf_op jit(solution)/shard_map/ppermute | solution.py:94
  631.5 26.0 %collective-permute-start.26 = (bf16[240,2048]{1,0:T(8,128)(2,1)S(1)}, bf16[240,2048]{1,0:T(8,128)(2,1)S(1)}, u32[]{:S(2)}, u32[]{:S(2)}) collective-permute-start(bf16[240,2048]{1,0:T(8,128)(2,1)S(1)} %add_convert_fusion.9), channel_id=1, source_target_pairs={{8,0},{16,24},{9,1},{17,25},{10,2},{18,26},{11,3},{19,27},{12,4},{... | collective-permute-start | bytes 2949128 | tf_op jit(solution)/shard_map/ppermute | solution.py:94
  714.2 26.8 %collective-permute-start.35 = (bf16[256,2048]{1,0:T(8,128)(2,1)}, bf16[256,2048]{1,0:T(8,128)(2,1)S(1)}, u32[]{:S(2)}, u32[]{:S(2)}) collective-permute-start(bf16[256,2048]{1,0:T(8,128)(2,1)} %convolution_convert_fusion.3), channel_id=1, source_target_pairs={{0,8},{24,16},{1,9},{25,17},{2,10},{26,18},{3,11},{27,19},{4,12},{... | collective-permute-start | bytes 3145736 | tf_op jit(solution)/shard_map/ppermute | solution.py:94
  717.8 27.7 %collective-permute-start.33 = (bf16[688,768]{1,0:T(8,128)(2,1)}, bf16[688,768]{1,0:T(8,128)(2,1)}, u32[]{:S(2)}, u32[]{:S(2)}) collective-permute-start(bf16[688,768]{1,0:T(8,128)(2,1)} %add_convert_fusion), channel_id=1, source_target_pairs={{8,0},{16,24},{9,1},{17,25},{10,2},{18,26},{11,3},{19,27},{12,4},{... | collective-permute-start | bytes 3170312 | tf_op jit(solution)/shard_map/ppermute | solution.py:94
  745.5 34.0 %collective-permute-start.39 = (bf16[256,2048]{1,0:T(8,128)(2,1)}, bf16[256,2048]{1,0:T(8,128)(2,1)}, u32[]{:S(2)}, u32[]{:S(2)}) collective-permute-start(bf16[256,2048]{1,0:T(8,128)(2,1)} %add_convert_fusion.5), channel_id=1, source_target_pairs={{8,16},{16,8},{9,17},{17,9},{10,18},{18,10},{11,19},{19,11},{12,20... | collective-permute-start | bytes 3145736 | tf_op jit(solution)/shard_map/ppermute | solution.py:94
  773.1 26.4 %collective-permute-start.36 = (bf16[672,768]{1,0:T(8,128)(2,1)}, bf16[672,768]{1,0:T(8,128)(2,1)S(1)}, u32[]{:S(2)}, u32[]{:S(2)}) collective-permute-start(bf16[672,768]{1,0:T(8,128)(2,1)} %add_convert_fusion.7), channel_id=1, source_target_pairs={{8,0},{16,24},{9,1},{17,25},{10,2},{18,26},{11,3},{19,27},{12,4},{... | collective-permute-start | bytes 3096584 | tf_op jit(solution)/shard_map/ppermute | solution.py:94
  (116 other events, 2015.4 us)
Sparse Core Ops, SparseCore 0:
  12.2 55.6 all-gather.5
  69.8 65.6 all-gather.7
  137.4 54.4 all-gather.11
  193.6 54.3 all-gather.9
  331.8 70.2 reduce-scatter.5
  406.4 75.5 reduce-scatter.3
  483.8 60.0 all-gather.13
  560.0 70.4 reduce-scatter.7

commit v2 on v1

--- a/solution.py
+++ b/solution.py
@@ -290,6 +290,150 @@
     )(bounds, packed, mixed, grad_mixed, peaks, cosine, sine, low[:, None], high[:, None])
 
 
+class Ring:
+    def __init__(self, count, rows, buffer, sems):
+        self.chips, self.rows, self.buffer = count // 2, rows, buffer
+        self.ring_send, self.ring_recv, self.core_send, self.core_recv = sems
+        me = lax.axis_index("tp")
+        self.core, self.chip = me % 2, me // 2
+        self.spot = self.place(self.chip)
+        self.way = 1 - 2 * self.core
+        self.next = self.place((self.spot + self.way + self.chips) % self.chips) * 2 + self.core
+        self.last = self.place((self.spot - self.way + self.chips) % self.chips) * 2 + self.core
+        self.me, self.mate = me, me + self.way
+
+    def place(self, spot):
+        turn = self.chips // 2
+        return spot + (spot // turn) * (self.chips - 1 + turn - 2 * spot)
+
+    def origin(self, hop):
+        return self.place((self.spot - hop * self.way + hop * self.chips) % self.chips) * 2 + self.core
+
+    def mates_origin(self, hop):
+        spot = (self.spot + hop * self.way + hop * self.chips) % self.chips
+        return self.place(spot) * 2 + 1 - self.core
+
+    def part(self, device, half):
+        size = self.rows // 2
+        return pl.ds(pl.multiple_of(device * self.rows + half * size, size), size)
+
+    def copy(self, device, half, send, recv, to):
+        part = self.buffer.at[self.part(device, half), :]
+        return pltpu.make_async_remote_copy(
+            src_ref=part,
+            dst_ref=part,
+            send_sem=send,
+            recv_sem=recv,
+            device_id={"tp": to},
+            device_id_type=pl.DeviceIdType.MESH,
+        )
+
+    def greet(self):
+        barrier = pltpu.get_barrier_semaphore()
+        for other in (self.next, self.last, self.mate):
+            pl.semaphore_signal(
+                barrier, inc=1, device_id={"tp": other}, device_id_type=pl.DeviceIdType.MESH
+            )
+        return barrier
+
+    def along(self, hop, half, device):
+        return self.copy(device, half, self.ring_send.at[hop, half], self.ring_recv.at[hop, half], self.next)
+
+    def across(self, hop, half, device):
+        return self.copy(device, half, self.core_send.at[hop, half], self.core_recv.at[hop, half], self.mate)
+
+    def begin(self):
+        for half in range(2):
+            self.along(0, half, self.me).start()
+            self.across(0, half, self.me).start()
+
+    def advance(self, hop):
+        device = self.origin(hop)
+        for half in range(2):
+            self.along(hop - 1, half, device).wait_recv()
+            if hop < self.chips - 1:
+                self.along(hop, half, device).start()
+            self.across(hop, half, device).start()
+
+    def from_mate(self, hop):
+        device = self.mates_origin(hop)
+        for half in range(2):
+            self.across(hop, half, device).wait_recv()
+
+    def finish(self):
+        for half in range(2):
+            for hop in range(self.chips):
+                if hop < self.chips - 1:
+                    self.along(hop, half, self.me).wait_send()
+                self.across(hop, half, self.me).wait_send()
+
+
+def ring_sems(count):
+    chips = count // 2
+    return [pltpu.SemaphoreType.DMA((chips, 2))] * 4
+
+
+def project_kernel(count, tokens, gains, offsets, weight, bias, projected, gathered, buffer, *rest):
+    sems, out_sem = rest[:4], rest[4]
+    rows = tokens.shape[0]
+    ring = Ring(count, rows, buffer, sems)
+    barrier = ring.greet()
+    hat, _ = normalize(tokens[...].astype(F32))
+    own = pl.ds(pl.multiple_of(ring.me * rows, rows), rows)
+    buffer[own, :] = (hat * gains[...] + offsets[...]).astype(BF16)
+    pl.semaphore_wait(barrier, 3)
+    ring.begin()
+
+    def keep(device):
+        part = pl.ds(pl.multiple_of(device * rows, rows), rows)
+        return pltpu.make_async_copy(buffer.at[part, :], gathered.at[part, :], out_sem.at[device])
+
+    def work(device):
+        part = pl.ds(pl.multiple_of(device * rows, rows), rows)
+        keep(device).start()
+        projected[part, :] = (
+            jnp.dot(buffer[part, :], weight[...], preferred_element_type=F32) + bias[...]
+        )
+
+    work(ring.me)
+    ring.from_mate(0)
+    work(ring.mate)
+    for hop in range(1, ring.chips):
+        ring.advance(hop)
+        work(ring.origin(hop))
+        ring.from_mate(hop)
+        work(ring.mates_origin(hop))
+    ring.finish()
+    for device in range(count):
+        keep(device).wait()
+
+
+def project(count, tokens, gains, offsets, weight, bias):
+    rows, width = tokens.shape
+    columns = weight.shape[1]
+    total = rows * count
+    vmem = pl.BlockSpec(memory_space=pltpu.VMEM)
+    return pl.pallas_call(
+        functools.partial(project_kernel, count),
+        in_specs=[vmem] * 5,
+        out_specs=[vmem, pl.BlockSpec(memory_space=pl.ANY)],
+        out_shape=[
+            jax.ShapeDtypeStruct((total, columns), F32),
+            jax.ShapeDtypeStruct((total, width), BF16),
+        ],
+        scratch_shapes=[pltpu.VMEM((total, width), BF16)]
+        + ring_sems(count)
+        + [pltpu.SemaphoreType.DMA((count,))],
+        compiler_params=pltpu.CompilerParams(
+            collective_id=0, has_side_effects=True, vmem_limit_bytes=48 << 20
+        ),
+        cost_estimate=pl.CostEstimate(
+            flops=2 * total * width * columns, bytes_accessed=total * width * 8, transcendentals=0
+        ),
+        name="project",
+    )(tokens, gains, offsets, weight, bias[None])
+
+
 def feed_kernel(units, second, cotangent, expand, shrink, columns, hidden, grads):
     step = 176 if units % 176 == 0 else units
     for at in range(0, units, step):
@@ -416,10 +560,11 @@
 
     first_hat, first_scale = normalize(tokens.astype(F32))
     first_norm = first_hat * norm_gains[0] + norm_offsets[0]
-    first_all = gather(first_norm.astype(BF16))
     cotangent_all = gather(cotangent)
     full_output = gather(output_weight)
-    projected = jnp.dot(first_all, input_weight, preferred_element_type=F32) + input_offset
+    projected, first_all = project(
+        tp, tokens, norm_gains[:1], norm_offsets[:1], input_weight, input_offset
+    )
     packed, mixed, peaks = attend_forward(projected, cosine, sine, low, high, bounds)
     own_heads = lax.all_to_all(mixed, "tp", split_axis=0, concat_axis=1, tiled=True)
     attention = jnp.dot(own_heads, full_output, preferred_element_type=F32) + output_offset

time: 845 us -> 797 us (0.943)
  waiting for transfers between devices: 334 us -> 240 us
  Pallas kernels: 97.3 us -> 170 us
  other arithmetic: 114 us -> 97.2 us
  matrix products: 145 us -> 134 us
    all_gather x5 -> x4, waiting for transfers between devices: 154 us -> 35.3 us  [local(): gather = lambda a: lax.all_gather(a, 'tp', axis=0, tiled=True)]
    pallas_call x0 -> x1, Pallas kernels: none -> 77.9 us  [project(): pl.pallas_call(functools.partial(project_kernel, count), in_specs=[vmem]...]
    all_to_all x1, waiting for transfers between devices: 0.01 us -> 20.1 us  [local(): lax.all_to_all(mixed, 'tp', split_axis=0, concat_axis=1, tiled=True)]
    dot_general x1 -> x0, matrix products: 9.19 us -> none  [local(): jnp.dot(first_all, input_weight, preferred_element_type=F32) + input_offset]
    unnamed x169 -> x159, local copies, waits for them, and re-layouts: 17.9 us -> 17 us
  transfers between devices with their start and end apart: 56 -> 55, of which waited for: 27 -> 24; matrix products, arithmetic and copies ran while one was open for 31% -> 30% of each run, Pallas kernels for 7% -> 17%
where the time goes in v2:
time: 797 us; the launch traced here: 788 us
  waiting for transfers between devices  240 us (30%)
  Pallas kernels  170 us (21%)
  matrix products  134 us (17%)
  starting transfers between devices  106 us (13%)
  other arithmetic  97.2 us (12%)
  local copies, waits for them, and re-layouts  24.9 us (3%)
  between operations  15.9 us (2%)
    ppermute x39, waiting for transfers between devices, turn(): lax.ppermute(part, self.axis, pairs)  149 us
    ppermute x39, starting transfers between devices, turn(): lax.ppermute(part, self.axis, pairs)  92.9 us
    pallas_call x1, Pallas kernels, project(): pl.pallas_call(functools.partial(project_kernel, count), in_specs=[vmem]...  77.9 us
    dot_general x8, matrix products, dot(): return lax.dot_general(left, right, dims, preferred_element_type=F32)  64.2 us
    dot_general x9, matrix products, local(): mul = lambda a, b: jnp.dot(a, b, preferred_element_type=F32).astype(BF16)  63 us
    pallas_call x1, Pallas kernels, feed(): pl.pallas_call(functools.partial(feed_kernel, units), grid=(rows // tile,...  40 us
    convert_element_type x26, other arithmetic, line_steps(): part = (part.astype(F32) + got.astype(F32)).astype(BF16)  38.3 us
    all_gather x4, waiting for transfers between devices, local(): gather = lambda a: lax.all_gather(a, 'tp', axis=0, tiled=True)  35.3 us
  transfers between devices with their start and end apart: 55, of which 24 were waited for; matrix products, arithmetic and copies ran while one was open for 30% of the time, Pallas kernels for 17%

profile of v2, /device:TPU:2, one launch (start us, length us, event | category | flops | bytes accessed | tf_op | source)
XLA Modules:
  0.0 788.3 jit_solution(3578021619697050045)
XLA Ops:
  16.3 77.9 %project.1 = (f32[2048,768]{1,0:T(8,128)}, bf16[2048,2048]{1,0:T(8,128)(2,1)}) custom-call(bf16[256,2048]{1,0:T(8,128)(2,1)S(1)} %copy-done, f32[1,2048]{1,0:T(1,128)S(1)} %get-tuple-element.202.gains, f32[1,2048]{1,0:T(1,128)S(1)} %get-tuple-element.184.offsets, bf16[2048,768]{1,0:T(8,128)(2,1)S(1)} %copy-done.17, f32[1,768]{1,0:T(1,128)S(1)} %broadcast_in_dim.20.bias), custom_call_target="tpu_custom_call" | custom-call | flops 6442450944 | bytes 33554432 | tf_op jit(solution)/shard_map/project/pallas_call | solution.py:416
  97.0 21.5 %attend_forward.1 = (bf16[2048,768]{1,0:T(8,128)(2,1)S(1)}, bf16[2048,256]{1,0:T(8,128)(2,1)S(1)}, f32[2,2,1,1024]{3,2,1,0:T(1,128)S(1)}) custom-call(s32[2,4,2]{2,1,0:T(4,128)S(1)} %pad_add_fusion.bounds, f32[2048,768]{1,0:T(8,128)S(1)} %copy-done.2, f32[2,1024,128]{2,1,0:T(8,128)S(1)} %get-tuple-element.203.cosine, ...), custom_call_target="tpu_custom_call" | custom-call | flops 2147483648 | bytes 10485760 | tf_op jit(solution)/shard_map/attend_forward/pallas_call | solution.py:171
  127.0 20.1 %all-to-all-done = bf16[8,256,256]{1,2,0:T(8,128)(2,1)S(1)} async-done(((bf16[8,256,256]{1,2,0:T(8,128)(2,1)}), bf16[8,256,256]{1,2,0:T(8,128)(2,1)S(1)}, u32[]{:S(2)}, u32[]{:S(2)}) %all-to-all-start) | async-done | bytes 1048608 | tf_op jit(solution)/shard_map/all_to_all | solution.py:569
  164.0 12.4 %fusion.2.expand = bf16[1408,2048]{1,0:T(8,128)(2,1)} fusion(bf16[684,2048]{1,0:T(8,128)(2,1)S(1)} %get-tuple-element.179, bf16[684,2048]{1,0:T(8,128)(2,1)S(1)} %get-tuple-element.178), kind=kLoop, calls=%fused_computation.9 | loop fusion | flops 23068672 | bytes 11370496 | tf_op jit(solution)/shard_map/concatenate | solution.py:539
  176.4 35.3 %all-gather.7.cloned.1.call-done.second = bf16[2048,2048]{1,0:T(8,128)(2,1)} async-done(((bf16[256,2048]{1,0:T(8,128)(2,1)}), bf16[2048,2048]{1,0:T(8,128)(2,1)}) %all-gather.7.cloned.1.call-update) | async-done | bytes 8388624 | tf_op jit(solution)/shard_map/all_gather | solution.py:534
  211.7 40.0 %feed.1 = (bf16[704,2048]{1,0:T(8,128)(2,1)S(1)}, bf16[1408,2048]{1,0:T(8,128)(2,1)}) custom-call(bf16[2048,2048]{1,0:T(8,128)(2,1)} %all-gather.7.cloned.1.call-done.second, bf16[2048,2048]{1,0:T(8,128)(2,1)} %all-gather.9.cloned.1.call-done.cotangent, bf16[1408,2048]{1,0:T(8,128)(2,1)} %fusion.2.expand, bf16[704,2048]{1,0:T(8,128)(2,1)} %pad.16.shrink, ...), custom_call_target="tpu_custom_call" | custom-call | flops 17716740096 | bytes 34078720 | tf_op jit(solution)/shard_map/feed/pallas_call | solution.py:459
  262.9 15.6 %convolution_convert_fusion.2 = bf16[2048,2048]{1,0:T(8,128)(2,1)} fusion(bf16[1408,2048]{1,0:T(8,128)(2,1)S(1)} %copy-done.29, bf16[1408,2048]{1,0:T(8,128)(2,1)S(1)} %copy-done.30), kind=kOutput, calls=%fused_computation.7 | convolution fusion | flops 11815354368 | bytes 19922944 | tf_op jit(solution)/shard_map/dot_general | solution.py:26
  298.1 7.9 %fusion.43 = bf16[240,2048]{1,0:T(8,128)(2,1)} fusion(bf16[2048,2048]{1,0:T(8,128)(2,1)} %all-gather.7.cloned.1.call-done.second, bf16[1408,2048]{1,0:T(8,128)(2,1)} %get-tuple-element.104), kind=kOutput, calls=%fused_computation.109 | convolution fusion | flops 2013265920 | bytes 10354688 | tf_op jit(solution)/shard_map/dot_general | solution.py:578
  306.0 7.8 fusion.45
  313.8 9.5 %convolution_convert_fusion.1 = bf16[2048,2048]{1,0:T(8,128)(2,1)} fusion(bf16[704,2048]{1,0:T(8,128)(2,1)S(1)} %copy-done.23, bf16[704,2048]{1,0:T(8,128)(2,1)S(1)} %copy-done.47), kind=kOutput, calls=%fused_computation.6 | convolution fusion | flops 5909774336 | bytes 14155776 | tf_op jit(solution)/shard_map/dot_general | solution.py:26
  337.4 7.1 convolution_convert_fusion.5
  364.5 14.1 %collective-permute-done.5 = bf16[240,2048]{1,0:T(8,128)(2,1)S(1)} collective-permute-done((bf16[240,2048]{1,0:T(8,128)(2,1)S(1)}, bf16[240,2048]{1,0:T(8,128)(2,1)S(1)}, u32[]{:S(2)}, u32[]{:S(2)}) %collective-permute-start.5) | collective-permute-done | bytes 983072 | tf_op jit(solution)/shard_map/ppermute | solution.py:94
  385.6 17.6 %collective-permute-done.7 = bf16[240,2048]{1,0:T(8,128)(2,1)S(1)} collective-permute-done((bf16[240,2048]{1,0:T(8,128)(2,1)S(1)}, bf16[240,2048]{1,0:T(8,128)(2,1)S(1)}, u32[]{:S(2)}, u32[]{:S(2)}) %collective-permute-start.7) | collective-permute-done | bytes 983072 | tf_op jit(solution)/shard_map/ppermute | solution.py:94
  440.5 8.7 %all-to-all-done.1 = bf16[256,8,256]{2,0,1:T(8,128)(2,1)} async-done(((bf16[256,8,256]{2,0,1:T(8,128)(2,1)}), bf16[256,8,256]{2,0,1:T(8,128)(2,1)}, u32[]{:S(2)}, u32[]{:S(2)}) %all-to-all-start.1) | async-done | bytes 1048608 | tf_op jit(solution)/shard_map/all_to_all | solution.py:625
  455.7 23.9 %attend_backward.1 = bf16[2048,768]{1,0:T(8,128)(2,1)S(1)} custom-call(s32[2,4,2]{2,1,0:T(4,128)S(1)} %copy-done.16, bf16[2048,768]{1,0:T(8,128)(2,1)S(1)} %copy-done.20, bf16[2048,256]{1,0:T(8,128)(2,1)S(1)} %get-tuple-element.142.mixed, bf16[2048,256]{1,0:T(8,128)(2,1)} %bitcast.16.grad_mixed, f32[2,2,1,1024]{3,2,1,0:T(1,128)S(1)} %get-tuple-element.123.peaks, ...), custom_call_target="tpu_custom_call" | custom-call | flops 5368709120 | bytes 10485760 | tf_op jit(solution)/shard_map/attend_backward/pallas_call | solution.py:258
  483.7 9.1 %collective-permute-start.16 = (bf16[240,2048]{1,0:T(8,128)(2,1)}, bf16[240,2048]{1,0:T(8,128)(2,1)}, u32[]{:S(2)}, u32[]{:S(2)}) collective-permute-start(bf16[240,2048]{1,0:T(8,128)(2,1)} %convolution_convert_fusion.5), channel_id=1, source_target_pairs={{0,8},{24,16},{1,9},{25,17},{2,10},{26,18},{3,11},{27,19},{4,12},{... | collective-permute-start | bytes 2949128 | tf_op jit(solution)/shard_map/ppermute | solution.py:94
  494.2 9.0 %convolution_convert_fusion = bf16[2048,2048]{1,0:T(8,128)(2,1)} fusion(bf16[2048,768]{1,0:T(8,128)(2,1)S(1)} %attend_backward.1, bf16[2048,768]{1,0:T(8,128)(2,1)S(1)} %copy-done.18), kind=kOutput, calls=%fused_computation.5 | convolution fusion | flops 6446645248 | bytes 14680064 | tf_op jit(solution)/shard_map/dot_general | solution.py:26
  578.1 8.1 %collective-permute-done.23 = bf16[240,2048]{1,0:T(8,128)(2,1)S(1)} collective-permute-done((bf16[240,2048]{1,0:T(8,128)(2,1)S(1)}, bf16[240,2048]{1,0:T(8,128)(2,1)S(1)}, u32[]{:S(2)}, u32[]{:S(2)}) %collective-permute-start.23) | collective-permute-done | bytes 983072 | tf_op jit(solution)/shard_map/ppermute | solution.py:94
  598.3 14.6 %collective-permute-done.25 = bf16[688,768]{1,0:T(8,128)(2,1)S(1)} collective-permute-done((bf16[688,768]{1,0:T(8,128)(2,1)S(1)}, bf16[688,768]{1,0:T(8,128)(2,1)S(1)}, u32[]{:S(2)}, u32[]{:S(2)}) %collective-permute-start.25) | collective-permute-done | bytes 1056800 | tf_op jit(solution)/shard_map/ppermute | solution.py:94
  625.8 9.8 %collective-permute-done.27 = bf16[688,768]{1,0:T(8,128)(2,1)} collective-permute-done((bf16[688,768]{1,0:T(8,128)(2,1)}, bf16[688,768]{1,0:T(8,128)(2,1)}, u32[]{:S(2)}, u32[]{:S(2)}) %collective-permute-start.27) | collective-permute-done | bytes 1056800 | tf_op jit(solution)/shard_map/ppermute | solution.py:94
  682.1 15.7 %collective-permute-done.35 = bf16[256,2048]{1,0:T(8,128)(2,1)S(1)} collective-permute-done((bf16[256,2048]{1,0:T(8,128)(2,1)}, bf16[256,2048]{1,0:T(8,128)(2,1)S(1)}, u32[]{:S(2)}, u32[]{:S(2)}) %collective-permute-start.35) | collective-permute-done | bytes 1048608 | tf_op jit(solution)/shard_map/ppermute | solution.py:94
  709.0 19.1 %collective-permute-done.38 = f32[2136]{0:T(1024)S(1)} collective-permute-done((f32[2136]{0:T(1024)S(1)}, f32[2136]{0:T(1024)S(1)}, u32[]{:S(2)}, u32[]{:S(2)}) %collective-permute-start.38) | collective-permute-done | bytes 8576 | tf_op jit(solution)/shard_map/ppermute | solution.py:107
  737.0 18.0 %collective-permute-done.36 = bf16[672,768]{1,0:T(8,128)(2,1)S(1)} collective-permute-done((bf16[672,768]{1,0:T(8,128)(2,1)S(1)}, bf16[672,768]{1,0:T(8,128)(2,1)S(1)}, u32[]{:S(2)}, u32[]{:S(2)}) %collective-permute-start.36) | collective-permute-done | bytes 1032224 | tf_op jit(solution)/shard_map/ppermute | solution.py:94
  761.5 18.3 %collective-permute-done.40 = bf16[256,2048]{1,0:T(8,128)(2,1)S(1)} collective-permute-done((bf16[256,2048]{1,0:T(8,128)(2,1)S(1)}, bf16[256,2048]{1,0:T(8,128)(2,1)S(1)}, u32[]{:S(2)}, u32[]{:S(2)}) %collective-permute-start.40) | collective-permute-done | bytes 1048608 | tf_op jit(solution)/shard_map/ppermute | solution.py:94
  (385 shorter events, 331.1 us)
Async XLA Ops:
  7.2 139.9 %all-gather.5.cloned.1.call-start = ((), (), s32[]{:S(2)}) async-start(), calls=%async_computation.5 | async-start | bytes 9437184 | tf_op jit(solution)/shard_map/all_gather | solution.py:534
  8.0 168.4 %all-gather.9.cloned.1.call-start = ((), (), s32[]{:S(2)}) async-start(), calls=%async_computation.7 | async-start | bytes 9437184 | tf_op jit(solution)/shard_map/all_gather | solution.py:534
  121.5 25.6 %all-to-all-start = ((bf16[8,256,256]{1,2,0:T(8,128)(2,1)}), bf16[8,256,256]{1,2,0:T(8,128)(2,1)S(1)}, u32[]{:S(2)}, u32[]{:S(2)}) async-start(bf16[8,256,256]{1,2,0:T(8,128)(2,1)} %copy.77), calls=%async_computation | async-start | bytes 2097152 | tf_op jit(solution)/shard_map/all_to_all | solution.py:569
  126.4 85.3 %all-gather.7.cloned.1.call-start = ((), (), s32[]{:S(2)}) async-start(), calls=%async_computation.6 | async-start | bytes 9437184 | tf_op jit(solution)/shard_map/all_gather | solution.py:534
  156.0 247.6 %reduce-scatter.6.cloned.1.call-start = ((), (), s32[]{:S(2)}) async-start(), calls=%async_computation.9 | async-start | bytes 9437184 | tf_op jit(solution)/shard_map/reduce_scatter | solution.py:535
  258.4 33.3 %collective-permute-start = (bf16[240,2048]{1,0:T(8,128)(2,1)S(1)}, bf16[240,2048]{1,0:T(8,128)(2,1)}, u32[]{:S(2)}, u32[]{:S(2)}) collective-permute-start(bf16[240,2048]{1,0:T(8,128)(2,1)S(1)} %fusion.48), channel_id=1, source_target_pairs={{0,8},{24,16},{1,9},{25,17},{2,10},{26,18},{3,11},{27,19},{4,12},{... | collective-permute-start | bytes 2949128 | tf_op jit(solution)/shard_map/ppermute | solution.py:94
  293.3 232.4 %reduce-scatter.4.cloned.1.call-start = ((), (), s32[]{:S(2)}) async-start(), calls=%async_computation.8 | async-start | bytes 9437184 | tf_op jit(solution)/shard_map/reduce_scatter | solution.py:535
  293.4 36.8 %collective-permute-start.1 = (bf16[240,2048]{1,0:T(8,128)(2,1)S(1)}, bf16[240,2048]{1,0:T(8,128)(2,1)}, u32[]{:S(2)}, u32[]{:S(2)}) collective-permute-start(bf16[240,2048]{1,0:T(8,128)(2,1)S(1)} %fusion.25), channel_id=1, source_target_pairs={{8,16},{16,8},{9,17},{17,9},{10,18},{18,10},{11,19},{19,11},{12,20... | collective-permute-start | bytes 2949128 | tf_op jit(solution)/shard_map/ppermute | solution.py:94
  295.0 36.7 %collective-permute-start.2 = (bf16[240,2048]{1,0:T(8,128)(2,1)}, bf16[240,2048]{1,0:T(8,128)(2,1)}, u32[]{:S(2)}, u32[]{:S(2)}) collective-permute-start(bf16[240,2048]{1,0:T(8,128)(2,1)} %convolution_convert_fusion.7), channel_id=1, source_target_pairs={{0,8},{24,16},{1,9},{25,17},{2,10},{26,18},{3,11},{27,19},{4,12},{... | collective-permute-start | bytes 2949128 | tf_op jit(solution)/shard_map/ppermute | solution.py:94
  335.1 222.9 %all-gather.11.cloned.1.call-start = ((), (), s32[]{:S(2)}) async-start(), calls=%async_computation.10 | async-start | bytes 9437184 | tf_op jit(solution)/shard_map/all_gather | solution.py:534
  335.2 26.1 %collective-permute-start.3 = (bf16[204,2048]{1,0:T(8,128)(2,1)}, bf16[204,2048]{1,0:T(8,128)(2,1)}, u32[]{:S(2)}, u32[]{:S(2)}) collective-permute-start(bf16[204,2048]{1,0:T(8,128)(2,1)} %convolution_convert_fusion.9), channel_id=1, source_target_pairs={{0,8},{24,16},{1,9},{25,17},{2,10},{26,18},{3,11},{27,19},{4,12},{... | collective-permute-start | bytes 2506760 | tf_op jit(solution)/shard_map/ppermute | solution.py:94
  353.1 25.5 %collective-permute-start.5 = (bf16[240,2048]{1,0:T(8,128)(2,1)S(1)}, bf16[240,2048]{1,0:T(8,128)(2,1)S(1)}, u32[]{:S(2)}, u32[]{:S(2)}) collective-permute-start(bf16[240,2048]{1,0:T(8,128)(2,1)S(1)} %add_convert_fusion.17), channel_id=1, source_target_pairs={{8,0},{16,24},{9,1},{17,25},{10,2},{18,26},{11,3},{19,27},{12,4},{... | collective-permute-start | bytes 2949128 | tf_op jit(solution)/shard_map/ppermute | solution.py:94
  411.8 28.7 %collective-permute-start.11 = (bf16[204,2048]{1,0:T(8,128)(2,1)}, bf16[204,2048]{1,0:T(8,128)(2,1)}, u32[]{:S(2)}, u32[]{:S(2)}) collective-permute-start(bf16[204,2048]{1,0:T(8,128)(2,1)} %add_convert_fusion.21), channel_id=1, source_target_pairs={{8,0},{16,24},{9,1},{17,25},{10,2},{18,26},{11,3},{19,27},{12,4},{... | collective-permute-start | bytes 2506760 | tf_op jit(solution)/shard_map/ppermute | solution.py:94
  431.3 191.4 %reduce-scatter.8.cloned.1.call-start = ((), (), s32[]{:S(2)}) async-start(), calls=%async_computation.11 | async-start | bytes 9437184 | tf_op jit(solution)/shard_map/reduce_scatter | solution.py:535
  449.2 30.5 %collective-permute-start.13 = (bf16[204,2048]{1,0:T(8,128)(2,1)}, bf16[204,2048]{1,0:T(8,128)(2,1)S(1)}, u32[]{:S(2)}, u32[]{:S(2)}) collective-permute-start(bf16[204,2048]{1,0:T(8,128)(2,1)} %fusion.51), channel_id=1, source_target_pairs={{0,8},{24,16},{1,9},{25,17},{2,10},{26,18},{3,11},{27,19},{4,12},{... | collective-permute-start | bytes 2506760 | tf_op jit(solution)/shard_map/ppermute | solution.py:94
  451.7 28.3 %collective-permute-start.12 = (bf16[240,2048]{1,0:T(8,128)(2,1)}, bf16[240,2048]{1,0:T(8,128)(2,1)S(1)}, u32[]{:S(2)}, u32[]{:S(2)}) collective-permute-start(bf16[240,2048]{1,0:T(8,128)(2,1)} %fusion.29), channel_id=1, source_target_pairs={{8,16},{16,8},{9,17},{17,9},{10,18},{18,10},{11,19},{19,11},{12,20... | collective-permute-start | bytes 2949128 | tf_op jit(solution)/shard_map/ppermute | solution.py:94
  452.4 29.6 %collective-permute-start.14 = (bf16[240,2048]{1,0:T(8,128)(2,1)}, bf16[240,2048]{1,0:T(8,128)(2,1)S(1)}, u32[]{:S(2)}, u32[]{:S(2)}) collective-permute-start(bf16[240,2048]{1,0:T(8,128)(2,1)} %add_convert_fusion.14), channel_id=1, source_target_pairs={{8,0},{16,24},{9,1},{17,25},{10,2},{18,26},{11,3},{19,27},{12,4},{... | collective-permute-start | bytes 2949128 | tf_op jit(solution)/shard_map/ppermute | solution.py:94
  483.7 28.8 %collective-permute-start.16 = (bf16[240,2048]{1,0:T(8,128)(2,1)}, bf16[240,2048]{1,0:T(8,128)(2,1)}, u32[]{:S(2)}, u32[]{:S(2)}) collective-permute-start(bf16[240,2048]{1,0:T(8,128)(2,1)} %convolution_convert_fusion.5), channel_id=1, source_target_pairs={{0,8},{24,16},{1,9},{25,17},{2,10},{26,18},{3,11},{27,19},{4,12},{... | collective-permute-start | bytes 2949128 | tf_op jit(solution)/shard_map/ppermute | solution.py:94
  528.9 29.2 %collective-permute-start.20 = (bf16[204,2048]{1,0:T(8,128)(2,1)}, bf16[204,2048]{1,0:T(8,128)(2,1)}, u32[]{:S(2)}, u32[]{:S(2)}) collective-permute-start(bf16[204,2048]{1,0:T(8,128)(2,1)} %add_convert_fusion.20), channel_id=1, source_target_pairs={{8,0},{16,24},{9,1},{17,25},{10,2},{18,26},{11,3},{19,27},{12,4},{... | collective-permute-start | bytes 2506760 | tf_op jit(solution)/shard_map/ppermute | solution.py:94
  668.8 29.0 %collective-permute-start.35 = (bf16[256,2048]{1,0:T(8,128)(2,1)}, bf16[256,2048]{1,0:T(8,128)(2,1)S(1)}, u32[]{:S(2)}, u32[]{:S(2)}) collective-permute-start(bf16[256,2048]{1,0:T(8,128)(2,1)} %convolution_convert_fusion.3), channel_id=1, source_target_pairs={{0,8},{24,16},{1,9},{25,17},{2,10},{26,18},{3,11},{27,19},{4,12},{... | collective-permute-start | bytes 3145736 | tf_op jit(solution)/shard_map/ppermute | solution.py:94
  674.5 27.7 %collective-permute-start.33 = (bf16[688,768]{1,0:T(8,128)(2,1)}, bf16[688,768]{1,0:T(8,128)(2,1)}, u32[]{:S(2)}, u32[]{:S(2)}) collective-permute-start(bf16[688,768]{1,0:T(8,128)(2,1)} %add_convert_fusion), channel_id=1, source_target_pairs={{8,0},{16,24},{9,1},{17,25},{10,2},{18,26},{11,3},{19,27},{12,4},{... | collective-permute-start | bytes 3170312 | tf_op jit(solution)/shard_map/ppermute | solution.py:94
  702.2 33.2 %collective-permute-start.39 = (bf16[256,2048]{1,0:T(8,128)(2,1)S(1)}, bf16[256,2048]{1,0:T(8,128)(2,1)}, u32[]{:S(2)}, u32[]{:S(2)}) collective-permute-start(bf16[256,2048]{1,0:T(8,128)(2,1)S(1)} %add_convert_fusion.5), channel_id=1, source_target_pairs={{8,16},{16,8},{9,17},{17,9},{10,18},{18,10},{11,19},{19,11},{12,20... | collective-permute-start | bytes 3145736 | tf_op jit(solution)/shard_map/ppermute | solution.py:94
  704.0 25.4 %collective-permute-start.44 = (f32[6,2048]{1,0:T(8,128)S(1)}, f32[6,2048]{1,0:T(8,128)S(1)}, u32[]{:S(2)}, u32[]{:S(2)}) collective-permute-start(f32[6,2048]{1,0:T(8,128)S(1)} %add.277), channel_id=1, source_target_pairs={{0,8},{8,0},{16,24},{24,16},{1,9},{9,1},{17,25},{25,17},{2,10},{10... | collective-permute-start | bytes 147464 | tf_op jit(solution)/shard_map/ppermute | solution.py:107
  729.5 25.5 %collective-permute-start.36 = (bf16[672,768]{1,0:T(8,128)(2,1)S(1)}, bf16[672,768]{1,0:T(8,128)(2,1)S(1)}, u32[]{:S(2)}, u32[]{:S(2)}) collective-permute-start(bf16[672,768]{1,0:T(8,128)(2,1)S(1)} %add_convert_fusion.7), channel_id=1, source_target_pairs={{8,0},{16,24},{9,1},{17,25},{10,2},{18,26},{11,3},{19,27},{12,4},{... | collective-permute-start | bytes 3096584 | tf_op jit(solution)/shard_map/ppermute | solution.py:94
  (110 other events, 1957.5 us)
Sparse Core Ops, SparseCore 0:
  9.9 72.8 all-gather.4
  84.7 65.5 all-gather.8
  156.1 55.5 all-gather.6
  293.4 70.2 reduce-scatter.5
  368.0 80.8 reduce-scatter.3
  450.6 55.7 all-gather.10
  517.6 69.0 reduce-scatter.7

commit v3 on v2

--- a/solution.py
+++ b/solution.py
@@ -12,6 +12,8 @@
 LAYERS = 24
 SEQ_LEN = 1024
 BLOCK = 256
+TILE = 512
+UNITS = 176
 
 epsilon = 1e-05
 rope_base = 10000.0
@@ -19,6 +21,7 @@
 F32 = jnp.float32
 BF16 = jnp.bfloat16
 ROWS = (((1,), (1,)), ((), ()))
+MESH = pl.DeviceIdType.MESH
 COLS = (((0,), (0,)), ((), ()))
 
 
@@ -51,54 +54,6 @@
     angles = places.astype(F32)[..., None] * rates
     cosine, sine = jnp.cos(angles), jnp.sin(angles)
     return jnp.concatenate([cosine, cosine], -1), jnp.concatenate([-sine, sine], -1)
-
-
-def line_steps(part, count, axis):
-    here = lax.axis_index(axis)
-    half = count // 2
-    for k in range(half - 1):
-        got = yield part, [(k, k + 1), (count - 1 - k, count - 2 - k)]
-        part = (part.astype(F32) + got.astype(F32)).astype(BF16)
-    if count > 1:
-        got = yield part, [(half - 1, half), (half, half - 1)]
-        part = (part.astype(F32) + got.astype(F32)).astype(BF16)
-    for k in range(half - 1):
-        got = yield part, [(half - 1 - k, half - 2 - k), (half + k, half + k + 1)]
-        outer = (here == half - 2 - k) | (here == half + k + 1)
-        part = jnp.where(outer, got, part)
-    return part
-
-
-class Line:
-    def __init__(self, count, axis):
-        self.count, self.axis = count, axis
-        self.waiting, self.moving, self.sums, self.marks = [], [], {}, []
-
-    def add(self, name, part):
-        self.waiting.append((name, part.astype(BF16)))
-
-    def turn(self, *inputs):
-        sends = []
-        if self.waiting:
-            name, part = self.waiting.pop(0)
-            self.moving.append((name, line_steps(part, self.count, self.axis), None))
-        for name, steps, got in self.moving:
-            try:
-                part, pairs = steps.send(got)
-                sends.append((name, steps, part, pairs))
-            except StopIteration as done:
-                self.sums[name] = done.value
-        parts = [part for _, _, part, _ in sends]
-        inputs, parts, _ = lax.optimization_barrier((inputs, parts, self.marks))
-        self.moving = [
-            (name, steps, lax.ppermute(part, self.axis, pairs))
-            for (name, steps, _, pairs), part in zip(sends, parts)
-        ]
-        self.marks = [got for _, _, got in self.moving]
-        return inputs
-
-    def made(self, *values):
-        self.marks.extend(values)
 
 
 def swap_sum(values, count, axis):
@@ -325,14 +280,14 @@
             send_sem=send,
             recv_sem=recv,
             device_id={"tp": to},
-            device_id_type=pl.DeviceIdType.MESH,
+            device_id_type=MESH,
         )
 
     def greet(self):
         barrier = pltpu.get_barrier_semaphore()
         for other in (self.next, self.last, self.mate):
             pl.semaphore_signal(
-                barrier, inc=1, device_id={"tp": other}, device_id_type=pl.DeviceIdType.MESH
+                barrier, inc=1, device_id={"tp": other}, device_id_type=MESH
             )
         return barrier
 
@@ -434,75 +389,934 @@
     )(tokens, gains, offsets, weight, bias[None])
 
 
-def feed_kernel(units, second, cotangent, expand, shrink, columns, hidden, grads):
-    step = 176 if units % 176 == 0 else units
-    for at in range(0, units, step):
-        part = slice(at, at + step)
-        upper = slice(units + at, units + at + step)
-        gate = dot(expand[part, :], second[...], ROWS) + columns[part, 0:1]
-        up = dot(expand[upper, :], second[...], ROWS) + columns[part, 1:2]
-        grad_hidden = dot(shrink[part, :], cotangent[...], ROWS) * columns[part, 2:3]
-        normal = 0.5 * (1.0 + lax.erf(gate * (0.5**0.5)))
-        density = jnp.exp(-0.5 * gate * gate) * (0.5 / jnp.pi) ** 0.5
-        gelu = gate * normal
-        hidden[part, :] = (gelu * up * columns[part, 2:3]).astype(BF16)
-        grads[part, :] = (grad_hidden * up * (normal + gate * density)).astype(BF16)
-        grads[upper, :] = (grad_hidden * gelu).astype(BF16)
-
-
-def feed(second, cotangent, expand, shrink, columns):
-    rows, width = second.shape
-    units = shrink.shape[0]
+class Scatter:
+    def __init__(self, ring, give, take, passing, total, sems):
+        self.ring, self.give, self.take, self.passing, self.total = ring, give, take, passing, total
+        self.give_send, self.give_recv, self.pass_send, self.pass_recv, self.again = sems
+
+    def handed(self, far, half):
+        size = self.ring.rows // 2
+        part = pl.ds(half * size, size)
+        return pltpu.make_async_remote_copy(
+            src_ref=self.give.at[far % 2, part, :],
+            dst_ref=self.take.at[far, part, :],
+            send_sem=self.give_send.at[far, half],
+            recv_sem=self.give_recv.at[far, half],
+            device_id={"tp": self.ring.mate},
+            device_id_type=MESH,
+        )
+
+    def passed(self, far, half):
+        size = self.ring.rows // 2
+        part = pl.ds(half * size, size)
+        return pltpu.make_async_remote_copy(
+            src_ref=self.passing.at[far, part, :],
+            dst_ref=self.passing.at[far - 1, part, :],
+            send_sem=self.pass_send.at[far, half],
+            recv_sem=self.pass_recv.at[far - 1, half],
+            device_id={"tp": self.ring.next},
+            device_id_type=MESH,
+        )
+
+    def run(self, make, beside=lambda far: None):
+        ring = self.ring
+        chips, size = ring.chips, ring.rows // 2
+        for far in reversed(range(chips)):
+            if far < chips - 2:
+                for half in range(2):
+                    self.handed(far + 2, half).wait_send()
+            make(ring.origin(far) + ring.way, self.give.at[far % 2])
+            for half in range(2):
+                self.handed(far, half).start()
+            make(ring.origin(chips - far), self.total)
+            beside(far)
+            for half in range(2):
+                self.handed(far, half).wait_recv()
+                if far < chips - 1:
+                    self.passed(far + 1, half).wait_recv()
+
+                @pl.loop(0, size // 16)
+                def _(row):
+                    part = pl.ds(pl.multiple_of(half * size + row * 16, 16), 16)
+                    value = self.total[part, :] + self.take[far, part, :].astype(F32)
+                    if far < chips - 1:
+                        value = value + self.passing[far, part, :].astype(F32)
+                    if far > 0:
+                        self.passing[far, part, :] = value.astype(BF16)
+                    else:
+                        self.total[part, :] = value
+
+                if far > 0:
+                    self.passed(far, half).start()
+        for half in range(2):
+            for far in range(chips):
+                if far < 2:
+                    self.handed(far, half).wait_send()
+                if far > 0:
+                    self.passed(far, half).wait_send()
+
+    def release(self):
+        for other in (self.ring.last, self.ring.mate):
+            pl.semaphore_signal(self.again, inc=1, device_id={"tp": other}, device_id_type=MESH)
+        pl.semaphore_wait(self.again, 2)
+
+
+def scatter_space(count, rows, width):
+    chips = count // 2
+    return [
+        pltpu.VMEM((2, rows, width), BF16),
+        pltpu.VMEM((chips, rows, width), BF16),
+        pltpu.VMEM((chips, rows, width), BF16),
+        pltpu.VMEM((rows, width), F32),
+    ]
+
+
+def scatter_sems(count):
+    return [pltpu.SemaphoreType.DMA((count // 2, 2))] * 4 + [pltpu.SemaphoreType.REGULAR]
+
+
+SLOTS = 4
+LANDINGS = 3
+PIECE = 128
+
+
+class Line:
+    def __init__(self, count, pieces, held, came, crossed, sems):
+        self.pieces, self.held, self.came, self.crossed = pieces, held, came, crossed
+        (
+            self.load_sem,
+            self.keep_sem,
+            self.in_send,
+            self.in_recv,
+            self.mid_send,
+            self.mid_recv,
+            self.out_send,
+            self.out_recv,
+            self.in_free,
+            self.mid_free,
+        ) = sems
+        here = lax.axis_index("dp")
+        half = count // 2
+        side = here // half
+        self.count, self.half = count, half
+        self.inner, self.outer = here + 1 - 2 * side, here - 1 + 2 * side
+        self.depth = here + side * (count - 1 - 2 * here)
+        self.end, self.middle = self.depth == 0, self.depth == half - 1
+
+    def greet(self, barrier):
+        pl.semaphore_signal(barrier, inc=1, device_id={"dp": self.inner}, device_id_type=MESH)
+
+        @pl.when(self.depth > 0)
+        def _():
+            pl.semaphore_signal(barrier, inc=1, device_id={"dp": self.outer}, device_id_type=MESH)
+
+    def met(self, barrier, others):
+        @pl.when(self.depth == 0)
+        def _():
+            pl.semaphore_wait(barrier, others + 1)
+
+        @pl.when(self.depth > 0)
+        def _():
+            pl.semaphore_wait(barrier, others + 2)
+
+    def rows(self, k):
+        return self.pieces[k][0].shape[0]
+
+    def sent(self, source, target, send, recv, to):
+        return pltpu.make_async_remote_copy(
+            src_ref=source,
+            dst_ref=target,
+            send_sem=send,
+            recv_sem=recv,
+            device_id={"dp": to},
+            device_id_type=MESH,
+        )
+
+    def inward(self, k, source):
+        landing = self.came.at[k % LANDINGS, pl.ds(0, self.rows(k)), :]
+        return self.sent(source, landing, self.in_send.at[k], self.in_recv.at[k], self.inner)
+
+    def across(self, k):
+        part = pl.ds(0, self.rows(k))
+        return self.sent(
+            self.held.at[k % SLOTS, part, :],
+            self.crossed.at[k % LANDINGS, part, :],
+            self.mid_send.at[k],
+            self.mid_recv.at[k],
+            self.inner,
+        )
+
+    def outward(self, k, source):
+        return self.sent(source, self.pieces[k][1], self.out_send.at[k], self.out_recv.at[k], self.outer)
+
+    def slot(self, k):
+        return self.held.at[k % SLOTS, pl.ds(0, self.rows(k)), :]
+
+    def load(self, k):
+        return pltpu.make_async_copy(self.pieces[k][0], self.slot(k), self.load_sem.at[k])
+
+    def keep(self, k):
+        return pltpu.make_async_copy(self.slot(k), self.pieces[k][1], self.keep_sem.at[k])
+
+    def begin(self, k):
+        @pl.when(self.end)
+        def _():
+            if k >= LANDINGS:
+                pl.semaphore_wait(self.in_free, 1)
+            self.inward(k, self.pieces[k][0]).start()
+
+    def free(self, k):
+        @pl.when(self.middle)
+        def _():
+            self.outward(k, self.slot(k)).wait_send()
+            self.keep(k).wait()
+
+        if self.half > 2:
+
+            @pl.when((self.depth > 0) & (self.depth < self.half - 1))
+            def _():
+                self.inward(k, self.slot(k)).wait_send()
+
+    def ready(self, k):
+        if k >= SLOTS:
+            self.free(k - SLOTS)
+
+        @pl.when(self.depth > 0)
+        def _():
+            self.load(k).start()
+
+    def add(self, k, other):
+        slot = self.held.at[k % SLOTS]
+
+        @pl.loop(0, self.rows(k) // 16)
+        def _(row):
+            part = pl.ds(pl.multiple_of(row * 16, 16), 16)
+            slot[part, :] = (
+                slot[part, :].astype(F32) + other[k % LANDINGS, part, :].astype(F32)
+            ).astype(BF16)
+
+    def join(self, k):
+        @pl.when(self.depth > 0)
+        def _():
+            self.load(k).wait()
+            self.inward(k, self.slot(k)).wait_recv()
+            self.add(k, self.came)
+            if k + LANDINGS < len(self.pieces):
+                pl.semaphore_signal(
+                    self.in_free, inc=1, device_id={"dp": self.outer}, device_id_type=MESH
+                )
+
+        @pl.when(self.middle)
+        def _():
+            if k >= LANDINGS:
+                pl.semaphore_wait(self.mid_free, 1)
+            self.across(k).start()
+
+        if self.half > 2:
+
+            @pl.when((self.depth > 0) & (self.depth < self.half - 1))
+            def _():
+                if k >= LANDINGS:
+                    pl.semaphore_wait(self.in_free, 1)
+                self.inward(k, self.slot(k)).start()
+
+    def close(self, k):
+        @pl.when(self.middle)
+        def _():
+            self.across(k).wait_recv()
+            self.across(k).wait_send()
+            self.add(k, self.crossed)
+            if k + LANDINGS < len(self.pieces):
+                pl.semaphore_signal(
+                    self.mid_free, inc=1, device_id={"dp": self.inner}, device_id_type=MESH
+                )
+            self.outward(k, self.slot(k)).start()
+            self.keep(k).start()
+
+    def spread(self, k):
+        @pl.when(self.depth < self.half - 1)
+        def _():
+            self.outward(k, self.pieces[k][1]).wait_recv()
+
+        if self.half > 2:
+
+            @pl.when((self.depth > 0) & (self.depth < self.half - 1))
+            def _():
+                self.outward(k, self.pieces[k][1]).start()
+
+    def finish(self):
+        total = len(self.pieces)
+        for k in range(max(0, total - SLOTS), total):
+            self.free(k)
+        for k in range(total):
+
+            @pl.when(self.end)
+            def _():
+                self.inward(k, self.pieces[k][0]).wait_send()
+
+            if self.half > 2:
+
+                @pl.when((self.depth > 0) & (self.depth < self.half - 1))
+                def _():
+                    self.outward(k, self.pieces[k][1]).wait_send()
+
+
+def line_space(width):
+    return [
+        pltpu.VMEM((SLOTS, PIECE, width), BF16),
+        pltpu.VMEM((LANDINGS, PIECE, width), BF16),
+        pltpu.VMEM((LANDINGS, PIECE, width), BF16),
+    ]
+
+
+def line_sems(pieces):
+    return [pltpu.SemaphoreType.DMA((pieces,))] * 8 + [pltpu.SemaphoreType.REGULAR] * 2
+
+
+def piece_rows(start, total):
+    return [(start + at, min(PIECE, total - at)) for at in range(0, total, PIECE)]
+
+
+def middle_kernel(
+    count,
+    mixed,
+    weight,
+    tokens,
+    gains,
+    offsets,
+    output_offset,
+    gate_weight,
+    up_weight,
+    columns,
+    hidden,
+    gate_factor,
+    up_factor,
+    gathered,
+    middle,
+    buffer,
+    give,
+    take,
+    passing,
+    total,
+    *rest,
+):
+    rows = tokens.shape[0]
+    residual_scale = (2.0 * LAYERS) ** 0.5
+    ring = Ring(count, rows, buffer, rest[:4])
+    scatter = Scatter(ring, give, take, passing, total, rest[4:9])
+    out_sem = rest[9]
+    pl.semaphore_wait(ring.greet(), 3)
+
+    def make(device, target):
+        part = pl.ds(pl.multiple_of(device * rows, rows), rows)
+
+        @pl.loop(0, weight.shape[1] // TILE)
+        def _(tile):
+            cut = pl.ds(pl.multiple_of(tile * TILE, TILE), TILE)
+            target[:, cut] = jnp.dot(
+                mixed[part, :], weight[:, cut], preferred_element_type=F32
+            ).astype(target.dtype)
+
+    scatter.run(make)
+    hat, _ = normalize(tokens[...].astype(F32))
+    first = hat * gains[0:1, :] + offsets[0:1, :]
+    middle[...] = residual_scale * first + (total[...] + output_offset[...])
+    hat, _ = normalize(middle[...])
+    own = pl.ds(pl.multiple_of(ring.me * rows, rows), rows)
+    buffer[own, :] = (hat * gains[1:2, :] + offsets[1:2, :]).astype(BF16)
+    ring.begin()
+
+    def keep(device):
+        part = pl.ds(pl.multiple_of(device * rows, rows), rows)
+        return pltpu.make_async_copy(buffer.at[part, :], gathered.at[part, :], out_sem.at[device])
+
+    def work(device):
+        part = pl.ds(pl.multiple_of(device * rows, rows), rows)
+        keep(device).start()
+
+        @pl.loop(0, columns.shape[0] // UNITS)
+        def _(step):
+            own = pl.ds(pl.multiple_of(step * UNITS, UNITS), UNITS)
+            gate = dot(gate_weight[own, :], buffer[part, :], ROWS) + columns[own, 0:1]
+            up = dot(up_weight[own, :], buffer[part, :], ROWS) + columns[own, 1:2]
+            up = up * columns[own, 2:3]
+            normal = 0.5 * (1.0 + lax.erf(gate * (0.5**0.5)))
+            density = jnp.exp(-0.5 * gate * gate) * (0.5 / jnp.pi) ** 0.5
+            gelu = gate * normal
+            hidden[own, part] = (gelu * up).astype(BF16)
+            gate_factor[own, part] = (up * (normal + gate * density)).astype(BF16)
+            up_factor[own, part] = (gelu * columns[own, 2:3]).astype(BF16)
+
+    work(ring.me)
+    ring.from_mate(0)
+    work(ring.mate)
+    for hop in range(1, ring.chips):
+        ring.advance(hop)
+        work(ring.origin(hop))
+        ring.from_mate(hop)
+        work(ring.mates_origin(hop))
+    ring.finish()
+    for device in range(count):
+        keep(device).wait()
+
+
+def attention_to_feed(
+    count, mixed, weight, tokens, gains, offsets, output_offset, gate_weight, up_weight, columns
+):
+    rows, width = tokens.shape
+    units = columns.shape[0]
+    total = rows * count
+    vmem = pl.BlockSpec(memory_space=pltpu.VMEM)
+    return pl.pallas_call(
+        functools.partial(middle_kernel, count),
+        in_specs=[vmem] * 9,
+        out_specs=[vmem] * 3 + [pl.BlockSpec(memory_space=pl.ANY), vmem],
+        out_shape=[jax.ShapeDtypeStruct((units, total), BF16)] * 3
+        + [jax.ShapeDtypeStruct((total, width), BF16), jax.ShapeDtypeStruct((rows, width), F32)],
+        scratch_shapes=[pltpu.VMEM((total, width), BF16)]
+        + scatter_space(count, rows, width)
+        + ring_sems(count)
+        + scatter_sems(count)
+        + [pltpu.SemaphoreType.DMA((count,))],
+        compiler_params=pltpu.CompilerParams(
+            collective_id=1, has_side_effects=True, vmem_limit_bytes=58 << 20
+        ),
+        cost_estimate=pl.CostEstimate(
+            flops=4 * total * width * units,
+            bytes_accessed=total * width * 8,
+            transcendentals=2 * total * units,
+        ),
+        name="attention_to_feed",
+    )(
+        mixed, weight, tokens, gains, offsets, output_offset[None], gate_weight, up_weight, columns
+    )
+
+
+class Stage:
+    def __init__(self, slots, sem):
+        self.slots, self.sem, self.copies, self.waited = slots, sem, [], set()
+
+    def settle(self, index):
+        if index not in self.waited:
+            self.copies[index].wait()
+            self.waited.add(index)
+
+    def emit(self, work, size, target):
+        index = len(self.copies)
+        if index >= 2:
+            self.settle(index - 2)
+        slot = self.slots.at[index % 2, pl.ds(0, size), :]
+
+        @pl.loop(0, slot.shape[1] // TILE)
+        def _(tile):
+            cut = pl.ds(pl.multiple_of(tile * TILE, TILE), TILE)
+            slot[:, cut] = work(cut).astype(BF16)
+
+        copy = pltpu.make_async_copy(slot, target, self.sem.at[index])
+        copy.start()
+        self.copies.append(copy)
+        return index
+
+    def finish(self):
+        for index in range(len(self.copies)):
+            self.settle(index)
+
+
+def back_kernel(
+    count,
+    line_count,
+    used,
+    hidden,
+    shrink,
+    gate_weight,
+    up_weight,
+    output_weight,
+    mixed,
+    middle,
+    cotangent,
+    gains,
+    cotangent_all,
+    second_all,
+    gate_factor,
+    up_factor,
+    grad_mixed,
+    grad_middle,
+    sums,
+    unit_sums,
+    shrink_part,
+    expand_part,
+    output_part,
+    shrink_whole,
+    grads,
+    buffer,
+    factors,
+    staged,
+    *rest,
+):
+    rows, width = middle.shape
+    units = hidden.shape[0]
+    tokens = buffer.shape[0]
+    sems = rest[7:]
+    big_sem, factor_sem, stage_sem = sems[19:22]
+    residual_scale = (2.0 * LAYERS) ** 0.5
+    ring = Ring(count, rows, buffer, sems[:4])
+    scatter = Scatter(ring, *rest[:4], sems[4:9])
+    stage = Stage(staged, stage_sem)
+    parts = piece_rows(0, used)
+    pieces = [
+        (shrink_part.at[pl.ds(a, n), :], shrink_whole.at[pl.ds(a, n), :]) for a, n in parts
+    ]
+    line = Line(line_count, pieces, *rest[4:7], sems[9:19])
+    barrier = ring.greet()
+    line.greet(barrier)
+    load = pltpu.make_async_copy(cotangent_all, buffer, big_sem.at[0])
+    load.start()
+
+    def factor(block, slot):
+        cut = pl.ds(pl.multiple_of(block * BLOCK, BLOCK), BLOCK)
+        return [
+            pltpu.make_async_copy(from_.at[:, cut], factors.at[slot, c], factor_sem.at[slot, c])
+            for c, from_ in enumerate((gate_factor, up_factor))
+        ]
+
+    for copy in factor(0, 0):
+        copy.start()
+    line.met(barrier, 3)
+    load.wait()
+
+    def shrink_work(a, n):
+        return lambda cut: jnp.dot(
+            hidden[a : a + n, :], buffer[:, cut], preferred_element_type=F32
+        )
+
+    for k, (a, n) in enumerate(parts):
+        stage.emit(shrink_work(a, n), n, pieces[k][0])
+        if k > 0:
+            stage.settle(k - 1)
+            if k == 1:
+                line.ready(0)
+            if k <= LANDINGS:
+                line.begin(k - 1)
+    stage.settle(len(parts) - 1)
+
+    @pl.loop(0, tokens // BLOCK)
+    def _(block):
+        slot = block % 2
+        for copy in factor(block, slot):
+            copy.wait()
+
+        @pl.when(block + 1 < tokens // BLOCK)
+        def _():
+            for copy in factor(block + 1, 1 - slot):
+                copy.start()
+
+        cut = pl.ds(pl.multiple_of(block * BLOCK, BLOCK), BLOCK)
+
+        @pl.loop(0, units // UNITS)
+        def _(step):
+            own = pl.ds(pl.multiple_of(step * UNITS, UNITS), UNITS)
+            grad_hidden = dot(shrink[own, :], buffer[cut, :], ROWS)
+            grads[0, own, cut] = (grad_hidden * factors[slot, 0, own, :].astype(F32)).astype(BF16)
+            grads[1, own, cut] = (grad_hidden * factors[slot, 1, own, :].astype(F32)).astype(BF16)
+
+    load = pltpu.make_async_copy(second_all, buffer, big_sem.at[1])
+    load.start()
+    acts = []
+    for t in range(len(pieces) + 1):
+        if t < len(pieces):
+            acts.append(functools.partial(line.join, t))
+            if t + 1 < len(pieces):
+                acts.append(functools.partial(line.ready, t + 1))
+        if t > 0:
+            acts.append(functools.partial(line.close, t - 1))
+        if t + LANDINGS < len(pieces):
+            acts.append(functools.partial(line.begin, t + LANDINGS))
+    expands = []
+    for c in range(2):
+        for a, n in parts:
+            expands.append((c, a, n))
+
+    def expand_work(c, a, n):
+        return lambda cut: jnp.dot(
+            grads[c, a : a + n, :], buffer[:, cut], preferred_element_type=F32
+        )
+
+    def emit_expands(many):
+        for _ in range(min(many, len(expands))):
+            c, a, n = expands.pop(0)
+            stage.emit(expand_work(c, a, n), n, expand_part.at[pl.ds(c * units + a, n), :])
+
+    def serve(many):
+        for _ in range(min(many, len(acts))):
+            acts.pop(0)()
+
+    def make(device, target):
+        part = pl.ds(pl.multiple_of(device * rows, rows), rows)
+
+        @pl.loop(0, width // TILE)
+        def _(tile):
+            cut = pl.ds(pl.multiple_of(tile * TILE, TILE), TILE)
+            target[:, cut] = (
+                dot(grads[0, :, part], gate_weight[:, cut], COLS)
+                + dot(grads[1, :, part], up_weight[:, cut], COLS)
+            ).astype(target.dtype)
+
+    def beside(far):
+        serve(3)
+        if far == ring.chips - 1:
+            load.wait()
+        emit_expands(-(-2 * len(parts) // (ring.chips - 1)))
+
+    scatter.run(make, beside)
+    emit_expands(len(expands))
+    grad_output = cotangent[...].astype(F32)
+    hat, scale = normalize(middle[...])
+    grad_in, gain, offset = normalize_back(
+        residual_scale * grad_output + scatter.total[...], gains[1:2, :], hat, scale
+    )
+    grad_middle[...] = grad_in
+    scatter.release()
+    own = pl.ds(pl.multiple_of(ring.me * rows, rows), rows)
+    buffer[own, :] = grad_in.astype(BF16)
+    ring.begin()
+    sums[0:1, :] = gain[None]
+    sums[1:2, :] = offset[None]
+    sums[2:3, :] = jnp.sum(grad_middle[...].astype(BF16).astype(F32), axis=0, keepdims=True)
+    sums[3:4, :] = jnp.sum(cotangent[...].astype(F32), axis=0, keepdims=True)
+    sums[4:8, :] = jnp.zeros((4, width), F32)
+
+    def work(device):
+        part = pl.ds(pl.multiple_of(device * rows, rows), rows)
+        grad_mixed[part, :] = dot(buffer[part, :], output_weight[...], ROWS).astype(BF16)
+
+    work(ring.me)
+    ring.from_mate(0)
+    work(ring.mate)
+    for c in range(2):
+        unit_sums[c] = jnp.dot(
+            grads[c], jnp.ones((tokens, 128), BF16), preferred_element_type=F32
+        )
+    serve(3)
+    for hop in range(1, ring.chips):
+        ring.advance(hop)
+        work(ring.origin(hop))
+        ring.from_mate(hop)
+        work(ring.mates_origin(hop))
+        serve(3)
+    for a, n in piece_rows(0, mixed.shape[1]):
+        stage.emit(
+            lambda cut: dot(mixed[:, a : a + n], buffer[:, cut], COLS),
+            n,
+            output_part.at[pl.ds(a, n), :],
+        )
+    ring.finish()
+    serve(len(acts))
+    for k in range(len(pieces)):
+        line.spread(k)
+    line.finish()
+    stage.finish()
+
+
+def back(
+    count,
+    line_count,
+    used,
+    hidden,
+    shrink,
+    gate_weight,
+    up_weight,
+    output_weight,
+    mixed,
+    middle,
+    cotangent,
+    gains,
+    cotangent_all,
+    second_all,
+    gate_factor,
+    up_factor,
+):
+    rows, width = middle.shape
+    units, total = hidden.shape
+    heads = mixed.shape[1]
+    vmem, any_ = pl.BlockSpec(memory_space=pltpu.VMEM), pl.BlockSpec(memory_space=pl.ANY)
+    pieces = len(piece_rows(0, used))
+    return pl.pallas_call(
+        functools.partial(back_kernel, count, line_count, used),
+        in_specs=[vmem] * 9 + [any_] * 4,
+        out_specs=[vmem] * 4 + [any_] * 4,
+        out_shape=[
+            jax.ShapeDtypeStruct((total, heads), BF16),
+            jax.ShapeDtypeStruct((rows, width), F32),
+            jax.ShapeDtypeStruct((8, width), F32),
+            jax.ShapeDtypeStruct((2, units, 128), F32),
+            jax.ShapeDtypeStruct((used, width), BF16),
+            jax.ShapeDtypeStruct((2 * units, width), BF16),
+            jax.ShapeDtypeStruct((heads, width), BF16),
+            jax.ShapeDtypeStruct((used, width), BF16),
+        ],
+        scratch_shapes=[
+            pltpu.VMEM((2, units, total), BF16),
+            pltpu.VMEM((total, width), BF16),
+            pltpu.VMEM((2, 2, units, BLOCK), BF16),
+            pltpu.VMEM((2, PIECE, width), BF16),
+        ]
+        + scatter_space(count, rows, width)
+        + line_space(width)
+        + ring_sems(count)
+        + scatter_sems(count)
+        + line_sems(pieces)
+        + [
+            pltpu.SemaphoreType.DMA((2,)),
+            pltpu.SemaphoreType.DMA((2, 2)),
+            pltpu.SemaphoreType.DMA((3 * pieces + heads // PIECE,)),
+        ],
+        compiler_params=pltpu.CompilerParams(
+            collective_id=2, has_side_effects=True, vmem_limit_bytes=60 << 20
+        ),
+        cost_estimate=pl.CostEstimate(
+            flops=18 * total * width * units, bytes_accessed=total * width * 8, transcendentals=0
+        ),
+        name="back",
+    )(
+        hidden,
+        shrink,
+        gate_weight,
+        up_weight,
+        output_weight,
+        mixed,
+        middle,
+        cotangent,
+        gains,
+        cotangent_all,
+        second_all,
+        gate_factor,
+        up_factor,
+    )
+
+
+def tail_kernel(
+    count,
+    line_count,
+    used,
+    grad_projected,
+    input_weight,
+    hidden,
+    shrink,
+    middle,
+    tokens,
+    grad_middle,
+    gains,
+    offsets,
+    shrink_offset,
+    first_all,
+    expand_part,
+    output_part,
+    layer_out,
+    tokens_grad,
+    sums,
+    input_sums,
+    input_part,
+    expand_whole,
+    output_whole,
+    input_whole,
+    first,
+    staged,
+    *rest,
+):
+    rows, width = middle.shape
+    units = hidden.shape[0]
+    sems = rest[7:]
+    big_sem, stage_sem = sems[15:17]
+    residual_scale = (2.0 * LAYERS) ** 0.5
+    ring = Ring(count, rows, None, [None] * 4)
+    scatter = Scatter(ring, *rest[:4], sems[:5])
+    stage = Stage(staged, stage_sem)
+    pieces = [
+        (expand_part.at[pl.ds(c * units + a, n), :], expand_whole.at[pl.ds(c * units + a, n), :])
+        for c in range(2)
+        for a, n in piece_rows(0, used)
+    ] + [
+        (output_part.at[pl.ds(a, n), :], output_whole.at[pl.ds(a, n), :])
+        for a, n in piece_rows(0, output_part.shape[0])
+    ]
+    early = len(pieces)
+    lasts = piece_rows(0, grad_projected.shape[1])
+    pieces += [(input_part.at[pl.ds(a, n), :], input_whole.at[pl.ds(a, n), :]) for a, n in lasts]
+    line = Line(line_count, pieces, *rest[4:7], sems[5:15])
+    barrier = ring.greet()
+    line.greet(barrier)
+    load = pltpu.make_async_copy(first_all, first, big_sem.at[0])
+    load.start()
+    line.ready(0)
+    line.met(barrier, 3)
+    for k in range(LANDINGS):
+        line.begin(k)
+    turns = iter(range(len(pieces) + 1))
+
+    def turn():
+        t = next(turns, None)
+        if t is None:
+            return
+        if t < len(pieces):
+            line.join(t)
+            if t + 1 < len(pieces):
+                line.ready(t + 1)
+        if t > 0:
+            line.close(t - 1)
+        if t + LANDINGS < len(pieces):
+            line.begin(t + LANDINGS)
+
+    def make(device, target):
+        part = pl.ds(pl.multiple_of(device * rows, rows), rows)
+
+        @pl.loop(0, width // TILE)
+        def _(tile):
+            cut = pl.ds(pl.multiple_of(tile * TILE, TILE), TILE)
+            target[:, cut] = dot(grad_projected[part, :], input_weight[cut, :], ROWS).astype(
+                target.dtype
+            )
+
+    scatter.run(make, lambda far: turn())
+    hat, scale = normalize(tokens[...].astype(F32))
+    grad_in, gain, offset = normalize_back(
+        residual_scale * grad_middle[...] + scatter.total[...], gains[0:1, :], hat, scale
+    )
+    tokens_grad[...] = grad_in
+    sums[0:1, :] = gain[None]
+    sums[1:2, :] = offset[None]
+    sums[2:8, :] = jnp.zeros((6, width), F32)
+    scatter.release()
+    load.wait()
+
+    def input_work(a, n):
+        return lambda cut: dot(grad_projected[:, a : a + n], first[:, cut], COLS)
+
+    turn()
+    for a, n in lasts:
+        stage.emit(input_work(a, n), n, input_part.at[pl.ds(a, n), :])
+    input_sums[...] = jnp.dot(
+        jnp.ones((16, grad_projected.shape[0]), BF16),
+        grad_projected[...],
+        preferred_element_type=F32,
+    )
+    stage.finish()
+    turn()
+
+    def make_out(device, target):
+        part = pl.ds(pl.multiple_of(device * rows, rows), rows)
+
+        @pl.loop(0, width // TILE)
+        def _(tile):
+            cut = pl.ds(pl.multiple_of(tile * TILE, TILE), TILE)
+            target[:, cut] = dot(hidden[:, part], shrink[:, cut], COLS).astype(target.dtype)
+
+    scatter.run(make_out, lambda far: turn())
+    hat, _ = normalize(middle[...])
+    layer_out[...] = (
+        residual_scale * (hat * gains[1:2, :] + offsets[1:2, :])
+        + scatter.total[...]
+        + shrink_offset[...]
+    )
+    for _ in range(len(pieces) + 1):
+        turn()
+    for k in range(len(pieces)):
+        line.spread(k)
+    line.finish()
+
+
+def tail(
+    count,
+    line_count,
+    used,
+    grad_projected,
+    input_weight,
+    hidden,
+    shrink,
+    middle,
+    tokens,
+    grad_middle,
+    gains,
+    offsets,
+    shrink_offset,
+    first_all,
+    expand_part,
+    output_part,
+):
+    rows, width = middle.shape
+    units, total = hidden.shape
+    columns = grad_projected.shape[1]
+    heads = output_part.shape[0]
+    vmem, any_ = pl.BlockSpec(memory_space=pltpu.VMEM), pl.BlockSpec(memory_space=pl.ANY)
+    lasts = len(piece_rows(0, columns))
+    pieces = 2 * len(piece_rows(0, used)) + len(piece_rows(0, heads)) + lasts
+    return pl.pallas_call(
+        functools.partial(tail_kernel, count, line_count, used),
+        in_specs=[vmem] * 10 + [any_] * 3,
+        out_specs=[vmem] * 4 + [any_] * 4,
+        out_shape=[
+            jax.ShapeDtypeStruct((rows, width), F32),
+            jax.ShapeDtypeStruct((rows, width), F32),
+            jax.ShapeDtypeStruct((8, width), F32),
+            jax.ShapeDtypeStruct((16, columns), F32),
+            jax.ShapeDtypeStruct((columns, width), BF16),
+            jax.ShapeDtypeStruct((2 * units, width), BF16),
+            jax.ShapeDtypeStruct((heads, width), BF16),
+            jax.ShapeDtypeStruct((columns, width), BF16),
+        ],
+        scratch_shapes=[pltpu.VMEM((total, width), BF16), pltpu.VMEM((2, PIECE, width), BF16)]
+        + scatter_space(count, rows, width)
+        + line_space(width)
+        + scatter_sems(count)
+        + line_sems(pieces)
+        + [pltpu.SemaphoreType.DMA((1,)), pltpu.SemaphoreType.DMA((lasts,))],
+        compiler_params=pltpu.CompilerParams(
+            collective_id=3, has_side_effects=True, vmem_limit_bytes=60 << 20
+        ),
+        cost_estimate=pl.CostEstimate(
+            flops=4 * total * width * (columns + units),
+            bytes_accessed=total * width * 8,
+            transcendentals=0,
+        ),
+        name="tail",
+    )(
+        grad_projected,
+        input_weight,
+        hidden,
+        shrink,
+        middle,
+        tokens,
+        grad_middle,
+        gains,
+        offsets,
+        shrink_offset[None],
+        first_all,
+        expand_part,
+        output_part,
+    )
+
+
+def weave_kernel(gate, up, out):
+    rows = out.shape[0]
+    out[:, 0, :] = gate[:rows, :].astype(F32)
+    out[:, 1, :] = up[:rows, :].astype(F32)
+
+
+def weave(both, rows):
+    units, width = both.shape[0] // 2, both.shape[1]
     tile = 256
-    tokens = pl.BlockSpec((tile, width), lambda i: (i, 0))
-    whole = lambda a: pl.BlockSpec(a.shape, lambda i: (0, 0), pipeline_mode=pl.Buffered(1))
-    return pl.pallas_call(
-        functools.partial(feed_kernel, units),
-        grid=(rows // tile,),
-        in_specs=[tokens, tokens, whole(expand), whole(shrink), whole(columns)],
-        out_specs=[
-            pl.BlockSpec((units, tile), lambda i: (0, i)),
-            pl.BlockSpec((2 * units, tile), lambda i: (0, i)),
-        ],
-        out_shape=[
-            jax.ShapeDtypeStruct((units, rows), BF16),
-            jax.ShapeDtypeStruct((2 * units, rows), BF16),
-        ],
-        compiler_params=pltpu.CompilerParams(vmem_limit_bytes=50 << 20),
-        cost_estimate=pl.CostEstimate(
-            flops=6 * rows * width * units,
-            bytes_accessed=4 * rows * width + 6 * units * (rows + width),
-            transcendentals=2 * rows * units,
-        ),
-        name="feed",
-    )(second, cotangent, expand, shrink, columns)
-
-
-def weave_kernel(gate, up, out):
-    out[:, 0, :] = gate[...].astype(F32)
-    out[:, 1, :] = up[...].astype(F32)
-
-
-def weave(gate, up):
-    rows, width = gate.shape
-    tile = 256
-    part = pl.BlockSpec((rows, tile), lambda j: (0, j))
     return pl.pallas_call(
         weave_kernel,
         grid=(width // tile,),
-        in_specs=[part, part],
+        in_specs=[
+            pl.BlockSpec((units, tile), lambda j: (0, j)),
+            pl.BlockSpec((units, tile), lambda j: (1, j)),
+        ],
         out_specs=pl.BlockSpec((rows, 2, tile), lambda j: (0, 0, j)),
         out_shape=jax.ShapeDtypeStruct((rows, 2, width), F32),
         compiler_params=pltpu.CompilerParams(vmem_limit_bytes=40 << 20),
         cost_estimate=pl.CostEstimate(flops=0, bytes_accessed=12 * rows * width, transcendentals=0),
         name="weave",
-    )(gate, up)
-
-
-def cuts(total, pieces):
-    step = -(-total // pieces)
-    step = -(-step // 16) * 16
-    return [(at, min(at + step, total)) for at in range(0, total, step)]
+    )(both, both)
 
 
 def local(
@@ -524,21 +1338,14 @@
     shrink_offset,
     cotangent,
 ):
-    residual_scale = (2.0 * LAYERS) ** 0.5
     seq_count = segment_ids.shape[0]
-    group_rows = seq_count * SEQ_LEN
-    width = tokens.shape[1]
     units_used = expand_weight.shape[2]
-    units = -(-units_used // 176) * 176
-    heads_width = output_weight.shape[0]
-    gather = lambda a: lax.all_gather(a, "tp", axis=0, tiled=True)
-    scatter = lambda a: lax.psum_scatter(a, "tp", scatter_dimension=0, tiled=True).astype(F32)
+    units = -(-units_used // UNITS) * UNITS
+    used = -(-units_used // 16) * 16
 
     pad = ((0, units - units_used), (0, 0))
     turned_expand = jnp.transpose(expand_weight, (2, 1, 0))
-    expand = jnp.concatenate(
-        [jnp.pad(turned_expand[:, 0], pad), jnp.pad(turned_expand[:, 1], pad)], axis=0
-    )
+    gate_weight, up_weight = jnp.pad(turned_expand[:, 0], pad), jnp.pad(turned_expand[:, 1], pad)
     shrink = jnp.pad(shrink_weight, pad)
     unit_index = lax.axis_index("tp") * units_used + lax.iota(jnp.int32, units_used)
     keep_units = (unit_index < FF_USED).astype(F32)
@@ -558,150 +1365,83 @@
     )
     cosine, sine = rotary_tables(positions)
 
-    first_hat, first_scale = normalize(tokens.astype(F32))
-    first_norm = first_hat * norm_gains[0] + norm_offsets[0]
-    cotangent_all = gather(cotangent)
-    full_output = gather(output_weight)
     projected, first_all = project(
         tp, tokens, norm_gains[:1], norm_offsets[:1], input_weight, input_offset
     )
+    waiting, first_all = lax.optimization_barrier((cotangent, first_all))
+    cotangent_all = lax.all_gather(waiting, "tp", axis=0, tiled=True)
     packed, mixed, peaks = attend_forward(projected, cosine, sine, low, high, bounds)
-    own_heads = lax.all_to_all(mixed, "tp", split_axis=0, concat_axis=1, tiled=True)
-    attention = jnp.dot(own_heads, full_output, preferred_element_type=F32) + output_offset
-    middle = residual_scale * first_norm + attention
-    second_hat, second_scale = normalize(middle)
-    second_norm = second_hat * norm_gains[1] + norm_offsets[1]
-    second_all = gather(second_norm.astype(BF16))
-    hidden, grads = feed(second_all, cotangent_all, expand, shrink, columns)
-
-    line = Line(dp, "dp")
-    mul = lambda a, b: jnp.dot(a, b, preferred_element_type=F32).astype(BF16)
-    unit_cuts = cuts(units_used, 3)
-    width_cuts = cuts(width, 3)
-    shrink_part = [None] * 3
-    expand_part = [[None] * 3, [None] * 3]
-    a, b = unit_cuts[0]
-    line.add("s0", mul(hidden[a:b], cotangent_all))
-
-    hidden, cotangent_all, grads, expand = line.turn(hidden, cotangent_all, grads, expand)
-    for k in (1, 2):
-        a, b = unit_cuts[k]
-        line.add("s%d" % k, mul(hidden[a:b], cotangent_all))
-    grad_second_part = dot(grads, expand, COLS).astype(BF16)
-    line.made(line.waiting[0][1], line.waiting[1][1], grad_second_part)
-
-    grads, second_all, hidden, shrink, grad_second_part = line.turn(
-        grads, second_all, hidden, shrink, grad_second_part
-    )
-    grad_second_sum = scatter(grad_second_part)
-    for k in range(3):
-        a, b = unit_cuts[k]
-        line.add("g%d" % k, mul(grads[a:b], second_all))
-    shrink_sum_part = dot(hidden, shrink, COLS).astype(BF16)
-    line.made(shrink_sum_part, *[p for _, p in line.waiting[-3:]])
-
-    grads, second_all, shrink_sum_part, cotangent = line.turn(
-        grads, second_all, shrink_sum_part, cotangent
-    )
-    shrink_sum = scatter(shrink_sum_part)
-    for k in range(3):
-        a, b = unit_cuts[k]
-        line.add("u%d" % k, mul(grads[units + a : units + b], second_all))
-    expand_offset_grad = jnp.sum(grads.astype(F32), axis=1).reshape(2, units)[:, :units_used]
-    grad_output = cotangent.astype(F32)
-    shrink_offset_grad = jnp.sum(grad_output, axis=0)
-    line.made(expand_offset_grad, shrink_offset_grad, *[p for _, p in line.waiting[-3:]])
-
-    line.turn()
-
-    grad_second_sum, full_output = line.turn(grad_second_sum, full_output)
-    grad_second = residual_scale * grad_output + grad_second_sum
-    grad_middle, second_gain_grad, second_offset_grad = normalize_back(
-        grad_second, norm_gains[1], second_hat, second_scale
-    )
-    grad_attention = grad_middle.astype(BF16)
-    output_offset_grad = jnp.sum(grad_attention.astype(F32), axis=0)
-    grad_own = dot(grad_attention, full_output, ROWS).astype(BF16)
-    grad_mixed = lax.all_to_all(grad_own, "tp", split_axis=1, concat_axis=0, tiled=True)
-    attention_all = gather(grad_attention)
-    line.made(grad_mixed, second_gain_grad, second_offset_grad, output_offset_grad)
-
-    grad_mixed, packed, mixed = line.turn(grad_mixed, packed, mixed)
+    hidden, gate_factor, up_factor, second_all, middle = attention_to_feed(
+        tp,
+        mixed,
+        output_weight,
+        tokens,
+        norm_gains,
+        norm_offsets,
+        output_offset,
+        gate_weight,
+        up_weight,
+        columns,
+    )
+
+    grad_mixed, grad_middle, sums, unit_sums, _, expand_part, output_part, shrink_whole = back(
+        tp,
+        dp,
+        used,
+        hidden,
+        shrink,
+        gate_weight,
+        up_weight,
+        output_weight,
+        mixed,
+        middle,
+        cotangent,
+        norm_gains,
+        cotangent_all,
+        second_all,
+        gate_factor,
+        up_factor,
+    )
     grad_projected = attend_backward(
         packed, mixed, grad_mixed, peaks, cosine, sine, low, high, bounds
     )
-    line.made(grad_projected)
-
-    grad_projected, first_all, input_weight = line.turn(grad_projected, first_all, input_weight)
-    grad_first_part = dot(grad_projected, input_weight, ROWS).astype(BF16)
-    input_offset_grad = jnp.sum(grad_projected.astype(F32), axis=0)
-    line.made(grad_first_part, input_offset_grad)
-
-    grad_projected, first_all, grad_first_part = line.turn(grad_projected, first_all, grad_first_part)
-    grad_first_sum = scatter(grad_first_part)
-    for k in range(3):
-        a, b = width_cuts[k]
-        line.add("i%d" % k, dot(first_all[:, a:b], grad_projected, COLS))
-    line.made(*[p for _, p in line.waiting[-3:]])
-
-    attention_all, mixed = line.turn(attention_all, mixed)
-    line.add("o", dot(mixed, attention_all, COLS))
-    line.made(line.waiting[-1][1])
-
-    shrink_sum, second_hat = line.turn(shrink_sum, second_hat)
-    layer_out = (
-        residual_scale * (second_hat * norm_gains[1] + norm_offsets[1]) + shrink_sum + shrink_offset
-    )
-    shrink_grad = jnp.concatenate([line.sums["s%d" % k] for k in range(3)]).astype(F32)
-    line.made(layer_out, shrink_grad)
-    while "u2" not in line.sums:
-        line.turn()
-    expand_grad = weave(
-        jnp.concatenate([line.sums["g%d" % k] for k in range(3)]),
-        jnp.concatenate([line.sums["u%d" % k] for k in range(3)]),
-    )
-    line.made(expand_grad)
-
-    grad_first_sum, grad_middle = line.turn(grad_first_sum, grad_middle)
-    grad_first = residual_scale * grad_middle + grad_first_sum
-    tokens_grad, first_gain_grad, first_offset_grad = normalize_back(
-        grad_first, norm_gains[0], first_hat, first_scale
-    )
-    line.made(tokens_grad, first_gain_grad, first_offset_grad)
-    while line.waiting or line.moving:
-        line.turn()
-
-    whole_sums = swap_sum(
-        jnp.stack(
-            [
-                first_gain_grad,
-                second_gain_grad,
-                first_offset_grad,
-                second_offset_grad,
-                output_offset_grad,
-                shrink_offset_grad,
-            ]
-        ),
+    layer_out, tokens_grad, late_sums, input_sums, _, expand_whole, output_whole, input_whole = tail(
         tp,
-        "tp",
-    )
+        dp,
+        used,
+        grad_projected,
+        input_weight,
+        hidden,
+        shrink,
+        middle,
+        tokens,
+        grad_middle,
+        norm_gains,
+        norm_offsets,
+        shrink_offset,
+        first_all,
+        expand_part,
+        output_part,
+    )
+
+    whole_sums = swap_sum(jnp.concatenate([late_sums[:2], sums[:4]]), tp, "tp")
     whole_sums = swap_sum(whole_sums, dp, "dp")
     group_sums = swap_sum(
-        jnp.concatenate([expand_offset_grad.reshape(-1), input_offset_grad]), dp, "dp"
+        jnp.concatenate([unit_sums[:, :units_used, 0].reshape(-1), input_sums[0]]), dp, "dp"
     )
     return (
         layer_out,
         tokens_grad,
-        jnp.concatenate([line.sums["i%d" % k] for k in range(3)]).astype(F32),
+        input_whole.astype(F32).T,
         group_sums[2 * units_used :],
-        line.sums["o"].astype(F32),
+        output_whole.astype(F32),
         whole_sums[4],
-        jnp.transpose(expand_grad, (2, 1, 0)),
+        jnp.transpose(weave(expand_whole, units_used), (2, 1, 0)),
         group_sums[: 2 * units_used].reshape(2, units_used),
-        shrink_grad,
+        shrink_whole[:units_used].astype(F32),
         whole_sums[5],
-        whole_sums[0:2],
-        whole_sums[2:4],
+        jnp.stack([whole_sums[0], whole_sums[2]]),
+        jnp.stack([whole_sums[1], whole_sums[3]]),
     )
 
 

time: 797 us -> 683 us (0.86)
  Pallas kernels: 170 us -> 585 us
  waiting for transfers between devices: 240 us -> 6.17 us
  matrix products: 134 us -> 0 us
  starting transfers between devices: 106 us -> 3.78 us
  other arithmetic: 97.2 us -> 17 us
  local copies, waits for them, and re-layouts: 24.9 us -> 43.8 us
    pallas_call x2 -> x4, Pallas kernels: 46.9 us -> 493 us  [the longest x1 251 us: tail(): pl.pallas_call(functools.partial(tail_kernel, count, line_count, used), i...]
    ppermute x39 -> x0, waiting for transfers between devices: 149 us -> none  [turn(): lax.ppermute(part, self.axis, pairs)]
    dot_general x18 -> x0, matrix products: 134 us -> none  [the longest x8 64.2 us: dot(): return lax.dot_general(left, right, dims, preferred_element_type=F32)]
    ppermute x39 -> x0, starting transfers between devices: 92.9 us -> none  [turn(): lax.ppermute(part, self.axis, pairs)]
    convert_element_type x33 -> x2, other arithmetic: 55.4 us -> 4.8 us  [the longest x1 3.25 us: local(): shrink_whole[:units_used].astype(F32)]
    all_gather x4 -> x1, waiting for transfers between devices: 35.3 us -> 0.02 us  [local(): cotangent_all = lax.all_gather(waiting, 'tp', axis=0, tiled=True)]
    pallas_call x1, Pallas kernels: 77.9 us -> 43.6 us  [project(): pl.pallas_call(functools.partial(project_kernel, count), in_specs=[vmem]...]
    all_to_all x2 -> x0, waiting for transfers between devices: 28.8 us -> none  [the longest x1 20.1 us: local(): lax.all_to_all(mixed, 'tp', split_axis=0, concat_axis=1, tiled=True)]
  transfers between devices with their start and end apart: 55 -> 8, of which waited for: 24 -> 3; matrix products, arithmetic and copies ran while one was open for 30% -> 5% of each run, Pallas kernels for 17% -> 19%
where the time goes in v3:
time: 683 us; the launch traced here: 671 us
  Pallas kernels  585 us (86%)
  local copies, waits for them, and re-layouts  43.8 us (6%)
  other arithmetic  17 us (2%)
  between operations  14.8 us (2%)
    pallas_call x1, Pallas kernels, tail(): pl.pallas_call(functools.partial(tail_kernel, count, line_count, used), i...  251 us
    pallas_call x1, Pallas kernels, back(): pl.pallas_call(functools.partial(back_kernel, count, line_count, used), i...  142 us
    pallas_call x1, Pallas kernels, attention_to_feed(): pl.pallas_call(functools.partial(middle_kernel, count), in_specs=[vmem] *...  94.3 us
    pallas_call x1, Pallas kernels, project(): pl.pallas_call(functools.partial(project_kernel, count), in_specs=[vmem]...  43.6 us
    unnamed x44, local copies, waits for them, and re-layouts  29.5 us
    pallas_call x1, Pallas kernels, attend_backward(): pl.pallas_call(attend_backward_kernel, grid_spec=pltpu.PrefetchScalarGrid...  25.1 us
    pallas_call x1, Pallas kernels, attend_forward(): pl.pallas_call(attend_forward_kernel, grid_spec=pltpu.PrefetchScalarGridS...  23.3 us
  transfers between devices with their start and end apart: 8, of which 3 were waited for; matrix products, arithmetic and copies ran while one was open for 5% of the time, Pallas kernels for 19%

profile of v3, /device:TPU:2, one launch (start us, length us, event | category | flops | bytes accessed | tf_op | source)
XLA Modules:
  0.0 670.9 jit_solution(7338004541268625932)
XLA Ops:
  9.4 1.9 copy-done.1
  12.5 43.6 %project.1 = (f32[2048,768]{1,0:T(8,128)}, bf16[2048,2048]{1,0:T(8,128)(2,1)}) custom-call(bf16[256,2048]{1,0:T(8,128)(2,1)S(1)} %copy-done.4, f32[1,2048]{1,0:T(1,128)S(1)} %slice.57.gains, f32[1,2048]{1,0:T(1,128)S(1)} %slice.58.offsets, bf16[2048,768]{1,0:T(8,128)(2,1)S(1)} %copy-done.1, f32[1,768]{1,0:T(1,128)S(1)} %broadcast_in_dim.36.bias), custom_call_target="tpu_custom_call" | custom-call | flops 6442450944 | bytes 33554432 | tf_op jit(solution)/shard_map/project/pallas_call | solution.py:371
  57.0 5.3 copy.80
  62.4 1.8 pad.17.shrink
  64.6 1.8 pad.15.up_weight
  66.4 1.8 pad.14.gate_weight
  69.1 4.1 fusion
  73.8 23.3 %attend_forward.1 = (bf16[2048,768]{1,0:T(8,128)(2,1)S(1)}, bf16[2048,256]{1,0:T(8,128)(2,1)S(1)}, f32[2,2,1,1024]{3,2,1,0:T(1,128)S(1)}) custom-call(s32[2,4,2]{2,1,0:T(4,128)S(1)} %pad_add_fusion.bounds, f32[2048,768]{1,0:T(8,128)S(1)} %bitcast.23, f32[2,1024,128]{2,1,0:T(8,128)S(1)} %get-tuple-element.131.cosine, ...), custom_call_target="tpu_custom_call" | custom-call | flops 2147483648 | bytes 10485760 | tf_op jit(solution)/shard_map/attend_forward/pallas_call | solution.py:126
  97.1 1.7 copy-done.2
  99.7 94.3 %attention_to_feed.1 = (bf16[704,2048]{1,0:T(8,128)(2,1)}, bf16[704,2048]{1,0:T(8,128)(2,1)}, bf16[704,2048]{1,0:T(8,128)(2,1)}, bf16[2048,2048]{1,0:T(8,128)(2,1)}, f32[256,2048]{1,0:T(8,128)}) custom-call(bf16[2048,256]{1,0:T(8,128)(2,1)} %copy-done.5, bf16[256,2048]{1,0:T(8,128)(2,1)} %output_weight.1, bf16[256,2048]{1,0:T(8,128)(2,1)} %tokens.5, ...), custom_call_target="tpu_custom_call" | custom-call | flops 11811160064 | bytes 33554432 | tf_op jit(solution)/shard_map/attention_to_feed/pallas_call | solution.py:770
  194.1 141.6 %back.1 = (bf16[2048,256]{1,0:T(8,128)(2,1)}, f32[256,2048]{1,0:T(8,128)}, f32[8,2048]{1,0:T(8,128)}, f32[2,704,128]{2,1,0:T(8,128)}, bf16[688,2048]{1,0:T(8,128...) custom-call(bf16[704,2048]{1,0:T(8,128)(2,1)} %get-tuple-element.41.hidden, ...), custom_call_target="tpu_custom_call" | custom-call | flops 53150220288 | bytes 33554432 | tf_op jit(solution)/shard_map/back/pallas_call | solution.py:1043
  337.1 1.9 copy-done.3
  340.2 25.1 %attend_backward.1.grad_projected = bf16[2048,768]{1,0:T(8,128)(2,1)S(1)} custom-call(s32[2,4,2]{2,1,0:T(4,128)S(1)} %pad_add_fusion.bounds, bf16[2048,768]{1,0:T(8,128)(2,1)S(1)} %copy-done.3, bf16[2048,256]{1,0:T(8,128)(2,1)S(1)} %copy-done.6, bf16[2048,256]{1,0:T(8,128)(2,1)S(1)} %copy-done.8, f32[2,2,1,1024]{3,2,1,0:T(1,128)S(1)} %get-tuple-element.49.peaks, ...), custom_call_target="tpu_custom_call" | custom-call | flops 5368709120 | bytes 10485760 | tf_op jit(solution)/shard_map/attend_backward/pallas_call | solution.py:213
  365.4 1.7 copy-done.7
  367.0 250.5 %tail.1 = (f32[256,2048]{1,0:T(8,128)}, f32[256,2048]{1,0:T(8,128)}, f32[8,2048]{1,0:T(8,128)}, f32[16,768]{1,0:T(8,128)}, bf16[768,2048]{1,0:T(8,128)(2,1)}, /*...) custom-call(bf16[2048,768]{1,0:T(8,128)(2,1)} %copy-done.7, ...), custom_call_target="tpu_custom_call" | custom-call | flops 24696061952 | bytes 33554432 | tf_op jit(solution)/shard_map/tail/pallas_call | solution.py:1252
  620.4 3.7 collective-permute-done.3
  624.7 5.6 convert_bitcast_fusion
  630.5 2.1 collective-permute-start.1
  632.6 2.0 collective-permute-done.5
  635.0 3.2 slice_convert_fusion
  639.8 6.6 copy.78
  646.3 2.6 copy-done
  649.0 6.9 %weave.1 = f32[684,2,2048]{2,1,0:T(2,128)} custom-call(bf16[1408,2048]{1,0:T(8,128)(2,1)S(1)} %copy-done, bf16[1408,2048]{1,0:T(8,128)(2,1)S(1)} %copy-done), custom_call_target="tpu_custom_call" | custom-call | bytes 16809984 | tf_op jit(solution)/shard_map/weave/pallas_call | solution.py:1307
  659.1 3.1 copy.83
  (95 shorter events, 19.9 us)
Async XLA Ops:
  7.2 186.9 %all-gather.2.cloned.1.call-start = ((), (), s32[]{:S(2)}) async-start(), calls=%async_computation | async-start | bytes 9437184 | tf_op jit(solution)/shard_map/all_gather | solution.py:1372
  9.4 1.9 copy-start.1
  12.5 43.6 %copy-start.14 = (s32[2,1024]{1,0:T(2,128)S(1)}, s32[2,1024]{1,0:T(2,128)}, u32[]{:S(2)}) copy-start(s32[2,1024]{1,0:T(2,128)} %param.16) | copy-start | bytes 24580
  12.5 43.7 %copy-start.17 = (s32[2,4]{1,0:T(2,128)S(1)}, s32[2,4]{1,0:T(2,128)}, u32[]{:S(2)}) copy-start(s32[2,4]{1,0:T(2,128)} %param.17) | copy-start | bytes 100
  12.5 43.8 %copy-start.15 = (s32[2,1024]{1,0:T(2,128)S(1)}, s32[2,1024]{1,0:T(2,128)}, u32[]{:S(2)}) copy-start(s32[2,1024]{1,0:T(2,128)} %param.18) | copy-start | bytes 24580
  12.5 44.3 %copy-start.16 = (f32[2,684]{1,0:T(2,128)S(1)}, f32[2,684]{1,0:T(2,128)}, u32[]{:S(2)}) copy-start(f32[2,684]{1,0:T(2,128)} %param.26) | copy-start | bytes 16420
  57.0 5.3 copy-start.9
  66.4 7.4 %slice-start = ((s8[6291456]{0:T(1024)(128)(4,1)}), s8[4194304]{0:T(1024)(128)(4,1)S(1)}, s32[]{:S(2)}) async-start(s8[6291456]{0:T(1024)(128)(4,1)} %bitcast.22), calls=%async_computation.1 | async-start | bytes 8388608
  69.1 4.7 slice-start.1
  97.1 1.7 copy-start.2
  194.1 143.0 %copy-start.6 = (bf16[2048,256]{1,0:T(8,128)(2,1)S(1)}, bf16[2048,256]{1,0:T(8,128)(2,1)}, u32[]{:S(2)}) copy-start(bf16[2048,256]{1,0:T(8,128)(2,1)} %copy-done.5) | copy-start | bytes 3145732
  337.1 1.9 copy-start.3
  367.0 251.4 %copy-start.13 = (f32[8,2048]{1,0:T(8,128)S(1)}, f32[8,2048]{1,0:T(8,128)}, u32[]{:S(2)}) copy-start(f32[8,2048]{1,0:T(8,128)} %get-tuple-element.61) | copy-start | bytes 196612
  618.4 1.3 collective-permute-start.2
  619.8 4.3 collective-permute-start.3
  620.4 10.0 %collective-permute-start = (f32[2136]{0:T(1024)S(1)}, f32[2136]{0:T(1024)S(1)}, u32[]{:S(2)}, u32[]{:S(2)}) collective-permute-start(f32[2136]{0:T(1024)S(1)} %pad_maximum_fusion.6), channel_id=1, source_target_pairs={{0,8},{8,0},{16,24},{24,16},{1,9},{9,1},{17,25},{25,17},{2,10},{10... | collective-permute-start | bytes 25640 | tf_op jit(solution)/shard_map/ppermute | solution.py:62
  624.1 6.2 collective-permute-start.4
  624.7 10.3 %copy-start.10 = (bf16[688,2048]{1,0:T(8,128)(2,1)S(1)}, bf16[688,2048]{1,0:T(8,128)(2,1)}, u32[]{:S(2)}) copy-start(bf16[688,2048]{1,0:T(8,128)(2,1)} %get-tuple-element.63) | copy-start | bytes 8454148
  630.3 4.3 collective-permute-start.5
  630.5 25.4 %collective-permute-start.1 = (f32[2136]{0:T(1024)S(1)}, f32[2136]{0:T(1024)S(1)}, u32[]{:S(2)}, u32[]{:S(2)}) collective-permute-start(f32[2136]{0:T(1024)S(1)} %fusion.6), channel_id=1, source_target_pairs={{0,16},{8,24},{16,0},{24,8},{1,17},{9,25},{17,1},{25,9},{2,18},{10... | collective-permute-start | bytes 25640 | tf_op jit(solution)/shard_map/ppermute | solution.py:62
  634.6 22.6 %collective-permute-start.6 = (f32[6,2048]{1,0:T(8,128)S(1)}, f32[6,2048]{1,0:T(8,128)S(1)}, u32[]{:S(2)}, u32[]{:S(2)}) collective-permute-start(f32[6,2048]{1,0:T(8,128)S(1)} %add.81), channel_id=1, source_target_pairs={{0,16},{8,24},{16,0},{24,8},{1,17},{9,25},{17,1},{25,9},{2,18},{10... | collective-permute-start | bytes 147464 | tf_op jit(solution)/shard_map/ppermute | solution.py:62
  635.0 3.2 copy-start.12
  646.3 2.6 copy-start
  655.9 6.4 copy-start.11
  (4 other events, 5.1 us)
Sparse Core Ops, SparseCore 0:
  56.2 56.5 all-gather.1

commit v4 on v3

--- a/solution.py
+++ b/solution.py
@@ -54,14 +54,6 @@
     angles = places.astype(F32)[..., None] * rates
     cosine, sine = jnp.cos(angles), jnp.sin(angles)
     return jnp.concatenate([cosine, cosine], -1), jnp.concatenate([-sine, sine], -1)
-
-
-def swap_sum(values, count, axis):
-    bit = 1
-    while bit < count:
-        values = values + lax.ppermute(values, axis, [(i, i ^ bit) for i in range(count)])
-        bit *= 2
-    return values
 
 
 def turned(values, cosine, sine):
@@ -151,10 +143,9 @@
     )(bounds, projected, cosine, sine, low[:, None], high[:, None])
 
 
-def attend_backward_kernel(
-    bounds, packed, mixed, grad_mixed, peaks, cosine, sine, low, high, grad, keys_t, inner, grad_queries_t, grad_keys, grad_values
+def attend_back(
+    packed, mixed, grad_mixed, peaks, cosine, sine, low, high, grad, keys_t, inner, grad_keys, grad_values
 ):
-    seq = pl.program_id(0)
     score_scale = HEAD_DIM ** (-0.5)
     for b in range(SEQ_LEN // BLOCK):
         part = slice(b * BLOCK, (b + 1) * BLOCK)
@@ -164,13 +155,13 @@
     grad_keys[...] = jnp.zeros_like(grad_keys)
     grad_values[...] = jnp.zeros_like(grad_values)
 
-    def queries_block(b, _):
-        start = pl.multiple_of(b * BLOCK, BLOCK)
-        queries = packed[pl.ds(start, BLOCK), :HEAD_DIM]
-        pulled = grad_mixed[pl.ds(start, BLOCK), :]
-        first = low[0, 0, pl.ds(start, BLOCK)][None, :]
-        last = high[0, 0, pl.ds(start, BLOCK)][None, :]
-        peak = peaks[0, 0, 0, pl.ds(start, BLOCK)][None, :]
+    @pl.loop(0, SEQ_LEN // BLOCK)
+    def _(b):
+        rows = pl.ds(pl.multiple_of(b * BLOCK, BLOCK), BLOCK)
+        queries = packed[rows, :HEAD_DIM]
+        pulled = grad_mixed[rows, :]
+        first, last = low[:, rows], high[:, rows]
+        peak = peaks[:, rows]
         inner_sum = inner[b]
 
         def keys_block(j, total):
@@ -188,61 +179,15 @@
             return total + jnp.dot(keys_t[j], grad_scores, preferred_element_type=F32)
 
         total = lax.fori_loop(
-            bounds[seq, b, 0], bounds[seq, b, 1], keys_block, jnp.zeros((HEAD_DIM, BLOCK), F32)
+            0, SEQ_LEN // BLOCK, keys_block, jnp.zeros((HEAD_DIM, BLOCK), F32)
         )
         grad_queries = total.T * score_scale
-        rows = pl.ds(start, BLOCK)
         grad[rows, :HEAD_DIM] = turned(grad_queries, cosine[rows, :], -sine[rows, :]).astype(BF16)
-        return 0
-
-    lax.fori_loop(0, SEQ_LEN // BLOCK, queries_block, 0)
+
     grad[:, HEAD_DIM : 2 * HEAD_DIM] = turned(
         grad_keys[...] * score_scale, cosine[...], -sine[...]
     ).astype(BF16)
     grad[:, 2 * HEAD_DIM :] = grad_values[...].astype(BF16)
-
-
-def attend_backward(packed, mixed, grad_mixed, peaks, cosine, sine, low, high, bounds):
-    seq_count, heads = cosine.shape[0], packed.shape[1] // (3 * HEAD_DIM)
-    rows = seq_count * SEQ_LEN
-    per_head = pl.BlockSpec((SEQ_LEN, 3 * HEAD_DIM), lambda s, h, *_: (s, h))
-    single = pl.BlockSpec((SEQ_LEN, HEAD_DIM), lambda s, h, *_: (s, h))
-    table = pl.BlockSpec((None, SEQ_LEN, HEAD_DIM), lambda s, h, *_: (s, 0, 0))
-    line = pl.BlockSpec((1, 1, SEQ_LEN), lambda s, h, *_: (s, 0, 0))
-    blocks = SEQ_LEN // BLOCK
-    return pl.pallas_call(
-        attend_backward_kernel,
-        grid_spec=pltpu.PrefetchScalarGridSpec(
-            num_scalar_prefetch=1,
-            grid=(seq_count, heads),
-            in_specs=[
-                per_head,
-                single,
-                single,
-                pl.BlockSpec((1, 1, 1, SEQ_LEN), lambda s, h, *_: (s, h, 0, 0)),
-                table,
-                table,
-                line,
-                line,
-            ],
-            out_specs=per_head,
-            scratch_shapes=[
-                pltpu.VMEM((blocks, HEAD_DIM, BLOCK), BF16),
-                pltpu.VMEM((blocks, 1, BLOCK), F32),
-                pltpu.VMEM((blocks, HEAD_DIM, BLOCK), F32),
-                pltpu.VMEM((SEQ_LEN, HEAD_DIM), F32),
-                pltpu.VMEM((SEQ_LEN, HEAD_DIM), F32),
-            ],
-        ),
-        out_shape=jax.ShapeDtypeStruct(packed.shape, BF16),
-        compiler_params=pltpu.CompilerParams(vmem_limit_bytes=40 << 20),
-        cost_estimate=pl.CostEstimate(
-            flops=10 * rows * SEQ_LEN * HEAD_DIM * heads,
-            bytes_accessed=rows * heads * HEAD_DIM * 20,
-            transcendentals=rows * SEQ_LEN * heads,
-        ),
-        name="attend_backward",
-    )(bounds, packed, mixed, grad_mixed, peaks, cosine, sine, low[:, None], high[:, None])
 
 
 class Ring:
@@ -478,6 +423,7 @@
 SLOTS = 4
 LANDINGS = 3
 PIECE = 128
+EARLY = 2
 
 
 class Line:
@@ -842,15 +788,18 @@
     grad_mixed,
     grad_middle,
     sums,
-    unit_sums,
     shrink_part,
     expand_part,
     output_part,
     shrink_whole,
+    expand_whole,
+    grads_out,
     grads,
     buffer,
     factors,
     staged,
+    flipped,
+    turned_mixed,
     *rest,
 ):
     rows, width = middle.shape
@@ -866,6 +815,13 @@
     pieces = [
         (shrink_part.at[pl.ds(a, n), :], shrink_whole.at[pl.ds(a, n), :]) for a, n in parts
     ]
+    pieces[-1:] = [
+        (expand_part.at[pl.ds(a, n), :], expand_whole.at[pl.ds(a, n), :])
+        for a, n in parts[:EARLY]
+    ] + pieces[-1:]
+    copy_of = lambda k: (
+        k if k < len(parts) - 1 else len(parts) - 1 if k == len(pieces) - 1 else k + 1
+    )
     line = Line(line_count, pieces, *rest[4:7], sems[9:19])
     barrier = ring.greet()
     line.greet(barrier)
@@ -889,15 +845,20 @@
             hidden[a : a + n, :], buffer[:, cut], preferred_element_type=F32
         )
 
-    for k, (a, n) in enumerate(parts):
-        stage.emit(shrink_work(a, n), n, pieces[k][0])
-        if k > 0:
-            stage.settle(k - 1)
-            if k == 1:
-                line.ready(0)
-            if k <= LANDINGS:
-                line.begin(k - 1)
-    stage.settle(len(parts) - 1)
+    shrinks = list(parts)
+
+    def emit_shrinks(many):
+        for a, n in shrinks[:many]:
+            stage.emit(shrink_work(a, n), n, shrink_part.at[pl.ds(a, n), :])
+        del shrinks[:many]
+
+    begun = min(LANDINGS, len(parts) - 1)
+    emit_shrinks(begun)
+    for k in range(begun):
+        stage.settle(k)
+        if k == 0:
+            line.ready(0)
+        line.begin(k)
 
     @pl.loop(0, tokens // BLOCK)
     def _(block):
@@ -920,21 +881,30 @@
             grads[1, own, cut] = (grad_hidden * factors[slot, 1, own, :].astype(F32)).astype(BF16)
 
     load = pltpu.make_async_copy(second_all, buffer, big_sem.at[1])
-    load.start()
-    acts = []
-    for t in range(len(pieces) + 1):
+    out = pltpu.make_async_copy(grads, grads_out, big_sem.at[2])
+    out.start()
+    turns, following = list(range(len(pieces) + 1)), list(range(begun, len(pieces)))
+
+    def turn():
+        if not turns:
+            return
+        new = [k for k in following if k <= turns[0] + LANDINGS]
+        if any(copy_of(k) >= len(stage.copies) for k in new):
+            return
+        t = turns.pop(0)
         if t < len(pieces):
-            acts.append(functools.partial(line.join, t))
+            line.join(t)
             if t + 1 < len(pieces):
-                acts.append(functools.partial(line.ready, t + 1))
+                stage.settle(copy_of(t + 1))
+                line.ready(t + 1)
         if t > 0:
-            acts.append(functools.partial(line.close, t - 1))
-        if t + LANDINGS < len(pieces):
-            acts.append(functools.partial(line.begin, t + LANDINGS))
-    expands = []
-    for c in range(2):
-        for a, n in parts:
-            expands.append((c, a, n))
+            line.close(t - 1)
+        for k in new:
+            stage.settle(copy_of(k))
+            line.begin(k)
+            following.remove(k)
+
+    expands = [(0, a, n) for a, n in parts[:EARLY]]
 
     def expand_work(c, a, n):
         return lambda cut: jnp.dot(
@@ -944,31 +914,34 @@
     def emit_expands(many):
         for _ in range(min(many, len(expands))):
             c, a, n = expands.pop(0)
-            stage.emit(expand_work(c, a, n), n, expand_part.at[pl.ds(c * units + a, n), :])
-
-    def serve(many):
-        for _ in range(min(many, len(acts))):
-            acts.pop(0)()
+            stage.emit(expand_work(c, a, n), n, expand_part.at[pl.ds(a, n), :])
 
     def make(device, target):
         part = pl.ds(pl.multiple_of(device * rows, rows), rows)
+        for c in range(2):
+            flipped[c] = grads[c, :, part].T
 
         @pl.loop(0, width // TILE)
         def _(tile):
             cut = pl.ds(pl.multiple_of(tile * TILE, TILE), TILE)
             target[:, cut] = (
-                dot(grads[0, :, part], gate_weight[:, cut], COLS)
-                + dot(grads[1, :, part], up_weight[:, cut], COLS)
+                jnp.dot(flipped[0], gate_weight[:, cut], preferred_element_type=F32)
+                + jnp.dot(flipped[1], up_weight[:, cut], preferred_element_type=F32)
             ).astype(target.dtype)
 
     def beside(far):
-        serve(3)
-        if far == ring.chips - 1:
+        step = ring.chips - 1 - far
+        if step < 2:
+            emit_shrinks(-(-(len(parts) - begun) // 2))
+        if step == 1:
+            emit_shrinks(len(shrinks))
+            load.start()
+        if step == 2:
             load.wait()
-        emit_expands(-(-2 * len(parts) // (ring.chips - 1)))
+            emit_expands(len(expands))
+        turn()
 
     scatter.run(make, beside)
-    emit_expands(len(expands))
     grad_output = cotangent[...].astype(F32)
     hat, scale = normalize(middle[...])
     grad_in, gain, offset = normalize_back(
@@ -984,37 +957,52 @@
     sums[2:3, :] = jnp.sum(grad_middle[...].astype(BF16).astype(F32), axis=0, keepdims=True)
     sums[3:4, :] = jnp.sum(cotangent[...].astype(F32), axis=0, keepdims=True)
     sums[4:8, :] = jnp.zeros((4, width), F32)
+    ones = jnp.ones((16, tokens), BF16)
+    for c in range(2):
+        sums[4 + c : 5 + c, :units] = dot(ones, grads[c], ROWS)[:1]
+
+    summed = scatter.total.at[pl.ds(0, mixed.shape[1]), :]
+    summed[...] = jnp.zeros(summed.shape, F32)
 
     def work(device):
         part = pl.ds(pl.multiple_of(device * rows, rows), rows)
         grad_mixed[part, :] = dot(buffer[part, :], output_weight[...], ROWS).astype(BF16)
+        turned_mixed[...] = mixed[part, :].T
+
+        @pl.loop(0, width // TILE)
+        def _(tile):
+            cut = pl.ds(pl.multiple_of(tile * TILE, TILE), TILE)
+            summed[:, cut] += jnp.dot(
+                turned_mixed[...], buffer[part, cut], preferred_element_type=F32
+            )
+
 
     work(ring.me)
     ring.from_mate(0)
     work(ring.mate)
-    for c in range(2):
-        unit_sums[c] = jnp.dot(
-            grads[c], jnp.ones((tokens, 128), BF16), preferred_element_type=F32
-        )
-    serve(3)
+    turn()
     for hop in range(1, ring.chips):
         ring.advance(hop)
         work(ring.origin(hop))
         ring.from_mate(hop)
         work(ring.mates_origin(hop))
-        serve(3)
+        turn()
+        if hop > 1:
+            turn()
     for a, n in piece_rows(0, mixed.shape[1]):
         stage.emit(
-            lambda cut: dot(mixed[:, a : a + n], buffer[:, cut], COLS),
+            lambda cut: summed[a : a + n, cut],
             n,
             output_part.at[pl.ds(a, n), :],
         )
     ring.finish()
-    serve(len(acts))
+    for _ in range(len(pieces) + 1):
+        turn()
     for k in range(len(pieces)):
         line.spread(k)
     line.finish()
     stage.finish()
+    out.wait()
 
 
 def back(
@@ -1039,26 +1027,30 @@
     units, total = hidden.shape
     heads = mixed.shape[1]
     vmem, any_ = pl.BlockSpec(memory_space=pltpu.VMEM), pl.BlockSpec(memory_space=pl.ANY)
-    pieces = len(piece_rows(0, used))
+    parts = piece_rows(0, used)
+    pieces = len(parts) + len(parts[:EARLY])
     return pl.pallas_call(
         functools.partial(back_kernel, count, line_count, used),
         in_specs=[vmem] * 9 + [any_] * 4,
-        out_specs=[vmem] * 4 + [any_] * 4,
+        out_specs=[vmem] * 3 + [any_] * 6,
         out_shape=[
             jax.ShapeDtypeStruct((total, heads), BF16),
             jax.ShapeDtypeStruct((rows, width), F32),
             jax.ShapeDtypeStruct((8, width), F32),
-            jax.ShapeDtypeStruct((2, units, 128), F32),
             jax.ShapeDtypeStruct((used, width), BF16),
-            jax.ShapeDtypeStruct((2 * units, width), BF16),
+            jax.ShapeDtypeStruct((sum(n for _, n in parts[:EARLY]), width), BF16),
             jax.ShapeDtypeStruct((heads, width), BF16),
             jax.ShapeDtypeStruct((used, width), BF16),
+            jax.ShapeDtypeStruct((sum(n for _, n in parts[:EARLY]), width), BF16),
+            jax.ShapeDtypeStruct((2, units, total), BF16),
         ],
         scratch_shapes=[
             pltpu.VMEM((2, units, total), BF16),
             pltpu.VMEM((total, width), BF16),
             pltpu.VMEM((2, 2, units, BLOCK), BF16),
             pltpu.VMEM((2, PIECE, width), BF16),
+            pltpu.VMEM((2, rows, units), BF16),
+            pltpu.VMEM((heads, rows), BF16),
         ]
         + scatter_space(count, rows, width)
         + line_space(width)
@@ -1066,9 +1058,9 @@
         + scatter_sems(count)
         + line_sems(pieces)
         + [
-            pltpu.SemaphoreType.DMA((2,)),
+            pltpu.SemaphoreType.DMA((3,)),
             pltpu.SemaphoreType.DMA((2, 2)),
-            pltpu.SemaphoreType.DMA((3 * pieces + heads // PIECE,)),
+            pltpu.SemaphoreType.DMA((pieces + heads // PIECE,)),
         ],
         compiler_params=pltpu.CompilerParams(
             collective_id=2, has_side_effects=True, vmem_limit_bytes=60 << 20
@@ -1094,11 +1086,25 @@
     )
 
 
+def blocks_turned(values):
+    side = values.shape[0]
+    return jnp.concatenate(
+        [values[:, at : at + side].T for at in range(0, values.shape[1], side)], axis=1
+    )
+
+
 def tail_kernel(
     count,
     line_count,
     used,
-    grad_projected,
+    packed,
+    mixed,
+    grad_mixed,
+    peaks,
+    cosine,
+    sine,
+    low,
+    high,
     input_weight,
     hidden,
     shrink,
@@ -1108,63 +1114,189 @@
     gains,
     offsets,
     shrink_offset,
+    early_sums,
     first_all,
-    expand_part,
+    second_all,
+    grads,
     output_part,
     layer_out,
     tokens_grad,
     sums,
-    input_sums,
+    expand_part,
     input_part,
     expand_whole,
     output_whole,
     input_whole,
-    first,
+    grad_projected,
+    keys_t,
+    inner,
+    grad_keys,
+    grad_values,
+    buffer,
+    lefts,
     staged,
+    group_box,
+    line_box,
     *rest,
 ):
     rows, width = middle.shape
     units = hidden.shape[0]
+    seq_count, heads = peaks.shape[0], peaks.shape[1]
     sems = rest[7:]
-    big_sem, stage_sem = sems[15:17]
+    big_sem, left_sem, stage_sem = sems[15:18]
     residual_scale = (2.0 * LAYERS) ** 0.5
     ring = Ring(count, rows, None, [None] * 4)
     scatter = Scatter(ring, *rest[:4], sems[:5])
     stage = Stage(staged, stage_sem)
-    pieces = [
-        (expand_part.at[pl.ds(c * units + a, n), :], expand_whole.at[pl.ds(c * units + a, n), :])
-        for c in range(2)
-        for a, n in piece_rows(0, used)
-    ] + [
-        (output_part.at[pl.ds(a, n), :], output_whole.at[pl.ds(a, n), :])
-        for a, n in piece_rows(0, output_part.shape[0])
-    ]
-    early = len(pieces)
+    expands = [(c, a, n) for c in range(2) for a, n in piece_rows(0, used)[EARLY if c == 0 else 0 :]]
+    short = [e for e in expands if e[2] < PIECE]
+    expands = [e for e in expands if e[2] == PIECE] + short
     lasts = piece_rows(0, grad_projected.shape[1])
-    pieces += [(input_part.at[pl.ds(a, n), :], input_whole.at[pl.ds(a, n), :]) for a, n in lasts]
+    outs = piece_rows(0, output_part.shape[0])
+    pieces = (
+        [(output_part.at[pl.ds(a, n), :], output_whole.at[pl.ds(a, n), :]) for a, n in outs]
+        + [
+            (
+                expand_part.at[pl.ds(c * units + a, n), :],
+                expand_whole.at[pl.ds(c * units + a, n), :],
+            )
+            for c, a, n in expands
+        ]
+        + [(input_part.at[pl.ds(a, n), :], input_whole.at[pl.ds(a, n), :]) for a, n in lasts]
+    )
+    ahead = len(outs)
+    full = ahead + len(expands) - len(short)
+    tail_order = pieces[full : full + len(short)]
+    pieces = pieces[:full] + pieces[full + len(short) :] + tail_order
     line = Line(line_count, pieces, *rest[4:7], sems[5:15])
-    barrier = ring.greet()
-    line.greet(barrier)
-    load = pltpu.make_async_copy(first_all, first, big_sem.at[0])
+    me, here = ring.me, lax.axis_index("dp")
+    barrier = pltpu.get_barrier_semaphore()
+    for axis, place, size in (("tp", me, count), ("dp", here, line_count)):
+        for i in range(1, size):
+            pl.semaphore_signal(
+                barrier, inc=1, device_id={axis: (place + i) % size}, device_id_type=MESH
+            )
+    load = pltpu.make_async_copy(second_all, buffer, big_sem.at[0])
     load.start()
+
+    def left(e):
+        c, a, n = expands[e]
+        return pltpu.make_async_copy(
+            grads.at[c, pl.ds(a, n), :], lefts.at[e % 2, pl.ds(0, n), :], left_sem.at[e]
+        )
+
+    left(0).start()
     line.ready(0)
-    line.met(barrier, 3)
-    for k in range(LANDINGS):
-        line.begin(k)
-    turns = iter(range(len(pieces) + 1))
+    pl.semaphore_wait(barrier, count + line_count - 2)
+    done = [0]
+
+    def copy_of(k):
+        if k < full:
+            return k - ahead
+        if k < full + len(lasts):
+            return k - full + len(expands)
+        return k - len(lasts) - ahead
+
+
+    def emit():
+        e = done[0]
+        if e == len(expands):
+            return
+        done[0] += 1
+        left(e).wait()
+        if e + 1 < len(expands):
+            left(e + 1).start()
+        n = expands[e][2]
+        stage.emit(
+            lambda cut: jnp.dot(
+                lefts[e % 2, pl.ds(0, n), :], buffer[:, cut], preferred_element_type=F32
+            ),
+            n,
+            expand_part.at[pl.ds(expands[e][0] * units + expands[e][1], n), :],
+        )
+
+    def there(k):
+        if k >= ahead:
+            while copy_of(k) >= len(stage.copies) and done[0] < len(expands):
+                emit()
+            stage.settle(copy_of(k))
+
+    turns = list(range(len(pieces) + 1))
 
     def turn():
-        t = next(turns, None)
-        if t is None:
+        if not turns:
             return
+        new = [k for k in following if k <= turns[0] + LANDINGS]
+        for k in new:
+            late = full <= k < full + len(lasts)
+            if k >= ahead and copy_of(k) >= len(stage.copies):
+                if late or done[0] == len(expands):
+                    return
+        t = turns.pop(0)
         if t < len(pieces):
             line.join(t)
             if t + 1 < len(pieces):
+                there(t + 1)
                 line.ready(t + 1)
         if t > 0:
             line.close(t - 1)
-        if t + LANDINGS < len(pieces):
-            line.begin(t + LANDINGS)
+        for k in new:
+            there(k)
+            line.begin(k)
+            following.remove(k)
+
+    following = list(range(LANDINGS, len(pieces)))
+    for k in range(min(ahead, LANDINGS)):
+        line.begin(k)
+    load.wait()
+    for k in range(ahead, LANDINGS):
+        there(k)
+        line.begin(k)
+
+    for s in range(seq_count):
+        for h in range(heads):
+            span = pl.ds(s * SEQ_LEN, SEQ_LEN)
+            head = pl.ds(h * HEAD_DIM, HEAD_DIM)
+            three = pl.ds(h * 3 * HEAD_DIM, 3 * HEAD_DIM)
+            attend_back(
+                packed.at[span, three],
+                mixed.at[span, head],
+                grad_mixed.at[span, head],
+                peaks.at[s, h],
+                cosine.at[s],
+                sine.at[s],
+                low.at[s],
+                high.at[s],
+                grad_projected.at[span, three],
+                keys_t,
+                inner,
+                grad_keys,
+                grad_values,
+            )
+            emit()
+            turn()
+            emit()
+
+    while done[0] < len(expands):
+        emit()
+    load = pltpu.make_async_copy(first_all, buffer, big_sem.at[1])
+    load.start()
+    load.wait()
+    inputs = list(lasts)
+
+    def emit_input():
+        if inputs:
+            a, n = inputs.pop(0)
+            stage.emit(
+                lambda cut: blocks_turned(dot(grad_projected[:, a : a + n], buffer[:, cut], COLS)),
+                n,
+                input_part.at[pl.ds(a, n), :],
+            )
+
+    def between(far):
+        emit_input()
+        turn()
+        emit_input()
 
     def make(device, target):
         part = pl.ds(pl.multiple_of(device * rows, rows), rows)
@@ -1176,30 +1308,49 @@
                 target.dtype
             )
 
-    scatter.run(make, lambda far: turn())
+    scatter.run(make, between)
+    while inputs:
+        emit_input()
     hat, scale = normalize(tokens[...].astype(F32))
     grad_in, gain, offset = normalize_back(
         residual_scale * grad_middle[...] + scatter.total[...], gains[0:1, :], hat, scale
     )
-    tokens_grad[...] = grad_in
-    sums[0:1, :] = gain[None]
-    sums[1:2, :] = offset[None]
-    sums[2:8, :] = jnp.zeros((6, width), F32)
+    scatter.total[...] = grad_in
+    keep = pltpu.make_async_copy(scatter.total, tokens_grad, big_sem.at[2])
+    keep.start()
+    small = group_box.at[me]
+    small[0:1, :] = gain[None]
+    small[1:2, :] = early_sums[0:1, :]
+    small[2:3, :] = offset[None]
+    small[3:4, :] = early_sums[1:2, :]
+    small[4:6, :] = early_sums[2:4, :]
+    small[6:8, :] = early_sums[4:6, :]
     scatter.release()
-    load.wait()
-
-    def input_work(a, n):
-        return lambda cut: dot(grad_projected[:, a : a + n], first[:, cut], COLS)
-
     turn()
-    for a, n in lasts:
-        stage.emit(input_work(a, n), n, input_part.at[pl.ds(a, n), :])
-    input_sums[...] = jnp.dot(
+    wide = grad_projected.shape[1]
+    small[6:7, width - wide :] = jnp.dot(
         jnp.ones((16, grad_projected.shape[0]), BF16),
         grad_projected[...],
         preferred_element_type=F32,
-    )
-    stage.finish()
+    )[:1]
+
+    def swaps(box, axis, place, size, send, recv):
+        return [
+            pltpu.make_async_remote_copy(
+                src_ref=box.at[place],
+                dst_ref=box.at[place],
+                send_sem=send.at[i],
+                recv_sem=recv.at[i],
+                device_id={axis: (place + i) % size},
+                device_id_type=MESH,
+            )
+            for i in range(1, size)
+        ]
+
+    group_swaps = swaps(group_box, "tp", me, count, *sems[18:20])
+    line_swaps = swaps(line_box, "dp", here, line_count, *sems[20:22])
+    for copy in group_swaps:
+        copy.start()
     turn()
 
     def make_out(device, target):
@@ -1210,25 +1361,47 @@
             cut = pl.ds(pl.multiple_of(tile * TILE, TILE), TILE)
             target[:, cut] = dot(hidden[:, part], shrink[:, cut], COLS).astype(target.dtype)
 
+    keep.wait()
     scatter.run(make_out, lambda far: turn())
     hat, _ = normalize(middle[...])
-    layer_out[...] = (
+    scatter.total[...] = (
         residual_scale * (hat * gains[1:2, :] + offsets[1:2, :])
         + scatter.total[...]
         + shrink_offset[...]
     )
+    keep = pltpu.make_async_copy(scatter.total, layer_out, big_sem.at[3])
+    keep.start()
+    turn()
+    for copy in group_swaps:
+        copy.wait()
+    line_box[here, 0:6, :] = sum(group_box[d, 0:6, :] for d in range(count))
+    line_box[here, 6:8, :] = small[6:8, :]
+    for copy in line_swaps:
+        copy.start()
     for _ in range(len(pieces) + 1):
         turn()
+    for copy in line_swaps:
+        copy.wait()
+    sums[...] = sum(line_box[d] for d in range(line_count))
     for k in range(len(pieces)):
         line.spread(k)
     line.finish()
+    stage.finish()
+    keep.wait()
 
 
 def tail(
     count,
     line_count,
     used,
-    grad_projected,
+    packed,
+    mixed,
+    grad_mixed,
+    peaks,
+    cosine,
+    sine,
+    low,
+    high,
     input_weight,
     hidden,
     shrink,
@@ -1238,37 +1411,58 @@
     gains,
     offsets,
     shrink_offset,
+    early_sums,
     first_all,
-    expand_part,
+    second_all,
+    grads,
     output_part,
 ):
     rows, width = middle.shape
     units, total = hidden.shape
-    columns = grad_projected.shape[1]
+    columns = packed.shape[1]
     heads = output_part.shape[0]
     vmem, any_ = pl.BlockSpec(memory_space=pltpu.VMEM), pl.BlockSpec(memory_space=pl.ANY)
-    lasts = len(piece_rows(0, columns))
-    pieces = 2 * len(piece_rows(0, used)) + len(piece_rows(0, heads)) + lasts
+    parts, lasts = piece_rows(0, used), len(piece_rows(0, columns))
+    expands = len(parts[EARLY:]) + len(parts)
+    pieces = expands + len(piece_rows(0, heads)) + lasts
+    blocks = SEQ_LEN // BLOCK
     return pl.pallas_call(
         functools.partial(tail_kernel, count, line_count, used),
-        in_specs=[vmem] * 10 + [any_] * 3,
-        out_specs=[vmem] * 4 + [any_] * 4,
+        in_specs=[vmem] * 18 + [any_] * 4,
+        out_specs=[any_] * 2 + [vmem] + [any_] * 5,
         out_shape=[
             jax.ShapeDtypeStruct((rows, width), F32),
             jax.ShapeDtypeStruct((rows, width), F32),
             jax.ShapeDtypeStruct((8, width), F32),
-            jax.ShapeDtypeStruct((16, columns), F32),
+            jax.ShapeDtypeStruct((2 * units, width), BF16),
             jax.ShapeDtypeStruct((columns, width), BF16),
             jax.ShapeDtypeStruct((2 * units, width), BF16),
             jax.ShapeDtypeStruct((heads, width), BF16),
             jax.ShapeDtypeStruct((columns, width), BF16),
         ],
-        scratch_shapes=[pltpu.VMEM((total, width), BF16), pltpu.VMEM((2, PIECE, width), BF16)]
+        scratch_shapes=[
+            pltpu.VMEM((total, columns), BF16),
+            pltpu.VMEM((blocks, HEAD_DIM, BLOCK), BF16),
+            pltpu.VMEM((blocks, 1, BLOCK), F32),
+            pltpu.VMEM((SEQ_LEN, HEAD_DIM), F32),
+            pltpu.VMEM((SEQ_LEN, HEAD_DIM), F32),
+            pltpu.VMEM((total, width), BF16),
+            pltpu.VMEM((2, PIECE, width), BF16),
+            pltpu.VMEM((2, PIECE, width), BF16),
+            pltpu.VMEM((count, 8, width), F32),
+            pltpu.VMEM((line_count, 8, width), F32),
+        ]
         + scatter_space(count, rows, width)
         + line_space(width)
         + scatter_sems(count)
         + line_sems(pieces)
-        + [pltpu.SemaphoreType.DMA((1,)), pltpu.SemaphoreType.DMA((lasts,))],
+        + [
+            pltpu.SemaphoreType.DMA((4,)),
+            pltpu.SemaphoreType.DMA((expands,)),
+            pltpu.SemaphoreType.DMA((expands + lasts,)),
+        ]
+        + [pltpu.SemaphoreType.DMA((count,))] * 2
+        + [pltpu.SemaphoreType.DMA((line_count,))] * 2,
         compiler_params=pltpu.CompilerParams(
             collective_id=3, has_side_effects=True, vmem_limit_bytes=60 << 20
         ),
@@ -1279,7 +1473,14 @@
         ),
         name="tail",
     )(
-        grad_projected,
+        packed,
+        mixed,
+        grad_mixed,
+        peaks,
+        cosine,
+        sine,
+        low[:, None],
+        high[:, None],
         input_weight,
         hidden,
         shrink,
@@ -1289,34 +1490,62 @@
         gains,
         offsets,
         shrink_offset[None],
+        early_sums,
         first_all,
-        expand_part,
+        second_all,
+        grads,
         output_part,
     )
 
 
-def weave_kernel(gate, up, out):
-    rows = out.shape[0]
-    out[:, 0, :] = gate[:rows, :].astype(F32)
-    out[:, 1, :] = up[:rows, :].astype(F32)
-
-
-def weave(both, rows):
+def finish_kernel(early, gate, up, shrink, output, inputs, expand_out, shrink_out, output_out, input_out):
+    rows, ahead = expand_out.shape[0], early.shape[0]
+    expand_out[:ahead, 0, :] = early[...].astype(F32)
+    expand_out[ahead:, 0, :] = gate[ahead:rows, :].astype(F32)
+    expand_out[:, 1, :] = up[:rows, :].astype(F32)
+    shrink_out[...] = shrink[:rows, :].astype(F32)
+    output_out[...] = output[...].astype(F32)
+    for at in range(0, inputs.shape[0], PIECE):
+        for cut in range(0, inputs.shape[1], PIECE):
+            input_out[cut : cut + PIECE, at : at + PIECE] = inputs[
+                at : at + PIECE, cut : cut + PIECE
+            ].astype(F32)
+
+
+def finish(early, both, shrink, output, inputs, rows):
     units, width = both.shape[0] // 2, both.shape[1]
+    columns, heads = inputs.shape[0], output.shape[0]
     tile = 256
+    part = lambda a: pl.BlockSpec((a.shape[0], tile), lambda j: (0, j))
     return pl.pallas_call(
-        weave_kernel,
+        finish_kernel,
         grid=(width // tile,),
         in_specs=[
+            part(early),
             pl.BlockSpec((units, tile), lambda j: (0, j)),
             pl.BlockSpec((units, tile), lambda j: (1, j)),
+            part(shrink),
+            part(output),
+            part(inputs),
         ],
-        out_specs=pl.BlockSpec((rows, 2, tile), lambda j: (0, 0, j)),
-        out_shape=jax.ShapeDtypeStruct((rows, 2, width), F32),
+        out_specs=[
+            pl.BlockSpec((rows, 2, tile), lambda j: (0, 0, j)),
+            pl.BlockSpec((rows, tile), lambda j: (0, j)),
+            pl.BlockSpec((heads, tile), lambda j: (0, j)),
+            pl.BlockSpec((tile, columns), lambda j: (j, 0)),
+        ],
+        out_shape=[
+            jax.ShapeDtypeStruct((rows, 2, width), F32),
+            jax.ShapeDtypeStruct((rows, width), F32),
+            jax.ShapeDtypeStruct((heads, width), F32),
+            jax.ShapeDtypeStruct((width, columns), F32),
+        ],
         compiler_params=pltpu.CompilerParams(vmem_limit_bytes=40 << 20),
-        cost_estimate=pl.CostEstimate(flops=0, bytes_accessed=12 * rows * width, transcendentals=0),
-        name="weave",
-    )(both, both)
+        cost_estimate=pl.CostEstimate(
+            flops=0, bytes_accessed=6 * width * (3 * rows + heads + columns), transcendentals=0
+        ),
+        name="finish",
+    )(early, both, both, shrink, output, inputs)
 
 
 def local(
@@ -1384,7 +1613,7 @@
         columns,
     )
 
-    grad_mixed, grad_middle, sums, unit_sums, _, expand_part, output_part, shrink_whole = back(
+    grad_mixed, grad_middle, sums, _, _, output_part, shrink_whole, expand_early, grads = back(
         tp,
         dp,
         used,
@@ -1402,14 +1631,18 @@
         gate_factor,
         up_factor,
     )
-    grad_projected = attend_backward(
-        packed, mixed, grad_mixed, peaks, cosine, sine, low, high, bounds
-    )
-    layer_out, tokens_grad, late_sums, input_sums, _, expand_whole, output_whole, input_whole = tail(
+    layer_out, tokens_grad, small_sums, _, _, expand_whole, output_whole, input_whole = tail(
         tp,
         dp,
         used,
-        grad_projected,
+        packed,
+        mixed,
+        grad_mixed,
+        peaks,
+        cosine,
+        sine,
+        low,
+        high,
         input_weight,
         hidden,
         shrink,
@@ -1419,29 +1652,29 @@
         norm_gains,
         norm_offsets,
         shrink_offset,
+        sums,
         first_all,
-        expand_part,
+        second_all,
+        grads,
         output_part,
     )
 
-    whole_sums = swap_sum(jnp.concatenate([late_sums[:2], sums[:4]]), tp, "tp")
-    whole_sums = swap_sum(whole_sums, dp, "dp")
-    group_sums = swap_sum(
-        jnp.concatenate([unit_sums[:, :units_used, 0].reshape(-1), input_sums[0]]), dp, "dp"
+    expand_grad, shrink_grad, output_grad, input_grad = finish(
+        expand_early, expand_whole, shrink_whole, output_whole, input_whole, units_used
     )
     return (
         layer_out,
         tokens_grad,
-        input_whole.astype(F32).T,
-        group_sums[2 * units_used :],
-        output_whole.astype(F32),
-        whole_sums[4],
-        jnp.transpose(weave(expand_whole, units_used), (2, 1, 0)),
-        group_sums[: 2 * units_used].reshape(2, units_used),
-        shrink_whole[:units_used].astype(F32),
-        whole_sums[5],
-        jnp.stack([whole_sums[0], whole_sums[2]]),
-        jnp.stack([whole_sums[1], whole_sums[3]]),
+        input_grad,
+        small_sums[6, small_sums.shape[1] - input_weight.shape[1] :],
+        output_grad,
+        small_sums[4],
+        jnp.transpose(expand_grad, (2, 1, 0)),
+        small_sums[6:8, :units_used],
+        shrink_grad,
+        small_sums[5],
+        small_sums[0:2],
+        small_sums[2:4],
     )
 
 

time: 683 us -> 624 us (0.914)
  Pallas kernels: 585 us -> 557 us
  other arithmetic: 17 us -> 5.12 us
  local copies, waits for them, and re-layouts: 43.8 us -> 35.5 us
    pallas_call x2 -> x1, Pallas kernels: 32 us -> 10.3 us  [finish(): pl.pallas_call(finish_kernel, grid=(width // tile,), in_specs=[part(early...]
    pallas_call x1, Pallas kernels: 251 us -> 239 us  [tail(): pl.pallas_call(functools.partial(tail_kernel, count, line_count, used), i...]
    unnamed x44 -> x49, local copies, waits for them, and re-layouts: 29.5 us -> 20.5 us
  transfers between devices with their start and end apart: 8 -> 1, of which waited for: 3 -> 0; matrix products, arithmetic and copies ran while one was open for 5% -> 3% of each run, Pallas kernels for 19% -> 19%
where the time goes in v4:
time: 624 us; the launch traced here: 612 us
  Pallas kernels  557 us (89%)
  local copies, waits for them, and re-layouts  35.5 us (6%)
  between operations  14.8 us (2%)
    pallas_call x1, Pallas kernels, tail(): pl.pallas_call(functools.partial(tail_kernel, count, line_count, used), i...  239 us
    pallas_call x1, Pallas kernels, back(): pl.pallas_call(functools.partial(back_kernel, count, line_count, used), i...  147 us
    pallas_call x1, Pallas kernels, attention_to_feed(): pl.pallas_call(functools.partial(middle_kernel, count), in_specs=[vmem] *...  98.2 us
    pallas_call x1, Pallas kernels, project(): pl.pallas_call(functools.partial(project_kernel, count), in_specs=[vmem]...  43.6 us
    unnamed x49, local copies, waits for them, and re-layouts  20.5 us
    pallas_call x1, Pallas kernels, attend_forward(): pl.pallas_call(attend_forward_kernel, grid_spec=pltpu.PrefetchScalarGridS...  18.9 us
  transfers between devices with their start and end apart: 1, of which 0 were waited for; matrix products, arithmetic and copies ran while one was open for 3% of the time, Pallas kernels for 19%

profile of v4, /device:TPU:2, one launch (start us, length us, event | category | flops | bytes accessed | tf_op | source)
XLA Modules:
  0.0 612.2 jit_solution(3765062121592993568)
XLA Ops:
  9.4 1.9 copy-done.9
  11.3 1.2 copy-done.11
  12.5 43.6 %project.1 = (f32[2048,768]{1,0:T(8,128)}, bf16[2048,2048]{1,0:T(8,128)(2,1)}) custom-call(bf16[256,2048]{1,0:T(8,128)(2,1)S(1)} %copy-done.11, f32[1,2048]{1,0:T(1,128)S(1)} %slice.36.gains, f32[1,2048]{1,0:T(1,128)S(1)} %slice.37.offsets, bf16[2048,768]{1,0:T(8,128)(2,1)S(1)} %copy-done.9, f32[1,768]{1,0:T(1,128)S(1)} %broadcast_in_dim.36.bias), custom_call_target="tpu_custom_call" | custom-call | flops 6442450944 | bytes 33554432 | tf_op jit(solution)/shard_map/project/pallas_call | solution.py:316
  57.1 5.3 copy.76
  62.4 1.8 pad.17.shrink
  64.7 1.8 pad.15.up_weight
  66.5 1.8 pad.14.gate_weight
  69.2 4.0 fusion
  74.0 18.9 %attend_forward.1 = (bf16[2048,768]{1,0:T(8,128)(2,1)S(1)}, bf16[2048,256]{1,0:T(8,128)(2,1)S(1)}, f32[2,2,1,1024]{3,2,1,0:T(1,128)S(1)}) custom-call(s32[2,4,2]{2,1,0:T(4,128)S(1)} %pad_add_fusion.bounds, f32[2048,768]{1,0:T(8,128)S(1)} %bitcast.21, f32[2,1024,128]{2,1,0:T(8,128)S(1)} %get-tuple-element.87.cosine, ...), custom_call_target="tpu_custom_call" | custom-call | flops 2147483648 | bytes 10485760 | tf_op jit(solution)/shard_map/attend_forward/pallas_call | solution.py:118
  92.9 1.7 copy-done.10
  95.5 98.2 %attention_to_feed.1 = (bf16[704,2048]{1,0:T(8,128)(2,1)}, bf16[704,2048]{1,0:T(8,128)(2,1)}, bf16[704,2048]{1,0:T(8,128)(2,1)}, bf16[2048,2048]{1,0:T(8,128)(2,1)}, f32[256,2048]{1,0:T(8,128)}) custom-call(bf16[2048,256]{1,0:T(8,128)(2,1)} %copy-done.12, bf16[256,2048]{1,0:T(8,128)(2,1)} %output_weight.1, bf16[256,2048]{1,0:T(8,128)(2,1)} %tokens.5, ...), custom_call_target="tpu_custom_call" | custom-call | flops 11811160064 | bytes 33554432 | tf_op jit(solution)/shard_map/attention_to_feed/pallas_call | solution.py:716
  193.7 146.8 %back.1 = (bf16[2048,256]{1,0:T(8,128)(2,1)}, f32[256,2048]{1,0:T(8,128)}, f32[8,2048]{1,0:T(8,128)}, bf16[688,2048]{1,0:T(8,128)(2,1)}, bf16[256,2048]{1,0:T(8,...) custom-call(bf16[704,2048]{1,0:T(8,128)(2,1)} %get-tuple-element.44., ...), custom_call_target="tpu_custom_call" | custom-call | flops 53150220288 | bytes 33554432 | tf_op jit(solution)/shard_map/back/pallas_call | solution.py:1032
  340.6 238.9 %tail.1 = (f32[256,2048]{1,0:T(8,128)}, f32[256,2048]{1,0:T(8,128)}, f32[8,2048]{1,0:T(8,128)}, bf16[1408,2048]{1,0:T(8,128)(2,1)}, bf16[768,2048]{1,0:T(8,128)(...) custom-call(bf16[2048,768]{1,0:T(8,128)(2,1)} %copy-done.10, ...), custom_call_target="tpu_custom_call" | custom-call | flops 24696061952 | bytes 33554432 | tf_op jit(solution)/shard_map/tail/pallas_call | solution.py:1429
  579.5 1.3 slice_reduce_fusion
  580.8 1.3 slice.44
  582.1 1.5 fusion.8
  583.7 1.5 fusion.7
  585.2 2.6 copy-done
  587.8 1.9 copy-done.3
  589.7 1.2 copy-done.6
  591.0 10.3 %finish.1 = (f32[684,2,2048]{2,1,0:T(2,128)}, f32[684,2048]{1,0:T(8,128)}, f32[256,2048]{1,0:T(8,128)}, f32[2048,768]{1,0:T(8,128)}) custom-call(bf16[256,2048]{1,0:T(8,128)(2,1)S(1)} %copy-done.5, bf16[1408,2048]{1,0:T(8,128)(2,1)S(1)} %copy-done, bf16[1408,2048]{1,0:T(8,128)(2,1)S(1)} %copy-done, bf16[688,2048]{1,0:T(8,128)(2,1)S(1)} %copy-done.4, ...), custom_call_target="tpu_custom_call" | custom-call | bytes 37797888 | tf_op jit(solution)/shard_map/finish/pallas_call | solution.py:1520
  601.3 1.3 copy.79
  602.6 1.0 copy-done.15
  603.6 1.3 copy.80
  (66 shorter events, 6.0 us)
Async XLA Ops:
  7.2 186.5 %all-gather.2.cloned.1.call-start = ((), (), s32[]{:S(2)}) async-start(), calls=%async_computation | async-start | bytes 9437184 | tf_op jit(solution)/shard_map/all_gather | solution.py:1601
  9.4 1.9 copy-start.9
  11.3 1.2 copy-start.11
  12.5 43.7 %copy-start.17 = (s32[2,1024]{1,0:T(2,128)S(1)}, s32[2,1024]{1,0:T(2,128)}, u32[]{:S(2)}) copy-start(s32[2,1024]{1,0:T(2,128)} %param.16) | copy-start | bytes 24580
  12.5 43.7 %copy-start.20 = (s32[2,4]{1,0:T(2,128)S(1)}, s32[2,4]{1,0:T(2,128)}, u32[]{:S(2)}) copy-start(s32[2,4]{1,0:T(2,128)} %param.17) | copy-start | bytes 100
  12.5 43.8 %copy-start.18 = (s32[2,1024]{1,0:T(2,128)S(1)}, s32[2,1024]{1,0:T(2,128)}, u32[]{:S(2)}) copy-start(s32[2,1024]{1,0:T(2,128)} %param.18) | copy-start | bytes 24580
  12.5 44.4 %copy-start.19 = (f32[2,684]{1,0:T(2,128)S(1)}, f32[2,684]{1,0:T(2,128)}, u32[]{:S(2)}) copy-start(f32[2,684]{1,0:T(2,128)} %param.26) | copy-start | bytes 16420
  56.3 17.6 %copy-start.7 = (s32[2,1,1024]{2,1,0:T(1,128)}, s32[2,1,1024]{2,1,0:T(1,128)S(1)}, u32[]{:S(2)}) copy-start(s32[2,1,1024]{2,1,0:T(1,128)S(1)} %broadcast_in_dim.38.high) | copy-start | bytes 24580
  56.4 17.6 %copy-start.8 = (s32[2,1,1024]{2,1,0:T(1,128)}, s32[2,1,1024]{2,1,0:T(1,128)S(1)}, u32[]{:S(2)}) copy-start(s32[2,1,1024]{2,1,0:T(1,128)S(1)} %copy.71.low) | copy-start | bytes 24580
  57.1 5.3 copy-start.14
  66.5 7.4 %slice-start = ((s8[6291456]{0:T(1024)(128)(4,1)}), s8[4194304]{0:T(1024)(128)(4,1)S(1)}, s32[]{:S(2)}) async-start(s8[6291456]{0:T(1024)(128)(4,1)} %bitcast.20), calls=%async_computation.1 | async-start | bytes 8388608
  69.2 4.7 slice-start.1
  73.9 19.0 %copy-start.1 = (f32[2,1024,128]{2,1,0:T(8,128)}, f32[2,1024,128]{2,1,0:T(8,128)S(1)}, u32[]{:S(2)}) copy-start(f32[2,1024,128]{2,1,0:T(8,128)S(1)} %get-tuple-element.87.cosine) | copy-start | bytes 3145732
  73.9 19.0 %copy-start.2 = (f32[2,1024,128]{2,1,0:T(8,128)}, f32[2,1024,128]{2,1,0:T(8,128)S(1)}, u32[]{:S(2)}) copy-start(f32[2,1024,128]{2,1,0:T(8,128)S(1)} %get-tuple-element.88.sine) | copy-start | bytes 3145732
  92.9 1.7 copy-start.10
  94.5 1.0 copy-start.12
  95.5 98.2 %copy-start.13 = (f32[2,2,1,1024]{3,2,1,0:T(1,128)}, f32[2,2,1,1024]{3,2,1,0:T(1,128)S(1)}, u32[]{:S(2)}) copy-start(f32[2,2,1,1024]{3,2,1,0:T(1,128)S(1)} %get-tuple-element.52.peaks) | copy-start | bytes 49156
  340.5 244.7 %copy-start.4 = (bf16[688,2048]{1,0:T(8,128)(2,1)S(1)}, bf16[688,2048]{1,0:T(8,128)(2,1)}, u32[]{:S(2)}) copy-start(bf16[688,2048]{1,0:T(8,128)(2,1)} %get-tuple-element.62.shrink) | copy-start | bytes 8454148
  340.6 244.6 %copy-start.5 = (bf16[256,2048]{1,0:T(8,128)(2,1)S(1)}, bf16[256,2048]{1,0:T(8,128)(2,1)}, u32[]{:S(2)}) copy-start(bf16[256,2048]{1,0:T(8,128)(2,1)} %get-tuple-element.60.early) | copy-start | bytes 3145732
  585.2 2.6 copy-start
  587.8 1.9 copy-start.3
  589.7 1.2 copy-start.6
  591.0 10.3 %copy-start.16 = (f32[256,2048]{1,0:T(8,128)S(1)}, f32[256,2048]{1,0:T(8,128)}, u32[]{:S(2)}) copy-start(f32[256,2048]{1,0:T(8,128)} %get-tuple-element.101) | copy-start | bytes 6291460
  601.3 2.3 copy-start.15
Sparse Core Ops, SparseCore 0:
  56.3 58.4 all-gather.1

commit v5 on v4

--- a/solution.py
+++ b/solution.py
@@ -273,8 +273,25 @@
     return [pltpu.SemaphoreType.DMA((chips, 2))] * 4
 
 
-def project_kernel(count, tokens, gains, offsets, weight, bias, projected, gathered, buffer, *rest):
-    sems, out_sem = rest[:4], rest[4]
+def project_kernel(
+    count,
+    tokens,
+    gains,
+    offsets,
+    weight,
+    bias,
+    expand,
+    projected,
+    gate_weight,
+    up_weight,
+    gathered,
+    buffer,
+    woven,
+    *rest,
+):
+    sems, out_sem, load_sem = rest[:4], rest[4], rest[5]
+    load = pltpu.make_async_copy(expand, woven, load_sem)
+    load.start()
     rows = tokens.shape[0]
     ring = Ring(count, rows, buffer, sems)
     barrier = ring.greet()
@@ -295,35 +312,54 @@
             jnp.dot(buffer[part, :], weight[...], preferred_element_type=F32) + bias[...]
         )
 
+    used, units = woven.shape[0], gate_weight.shape[0]
+    tiles = woven.shape[2] // BLOCK
+    share = -(-tiles // ring.chips)
+
+    def part_ways(turn):
+        @pl.loop(min(turn * share, tiles), min((turn + 1) * share, tiles))
+        def _(tile):
+            cut = pl.ds(pl.multiple_of(tile * BLOCK, BLOCK), BLOCK)
+            for c, target in enumerate((gate_weight, up_weight)):
+                target[used - used % 16 :, cut] = jnp.zeros(
+                    (units - used + used % 16, BLOCK), BF16
+                )
+                target[:used, cut] = woven[:, c, cut]
+
     work(ring.me)
     ring.from_mate(0)
     work(ring.mate)
+    load.wait()
+    part_ways(0)
     for hop in range(1, ring.chips):
         ring.advance(hop)
         work(ring.origin(hop))
         ring.from_mate(hop)
         work(ring.mates_origin(hop))
+        part_ways(hop)
     ring.finish()
     for device in range(count):
         keep(device).wait()
 
 
-def project(count, tokens, gains, offsets, weight, bias):
+def project(count, tokens, gains, offsets, weight, bias, expand, units):
     rows, width = tokens.shape
     columns = weight.shape[1]
     total = rows * count
     vmem = pl.BlockSpec(memory_space=pltpu.VMEM)
     return pl.pallas_call(
         functools.partial(project_kernel, count),
-        in_specs=[vmem] * 5,
-        out_specs=[vmem, pl.BlockSpec(memory_space=pl.ANY)],
+        in_specs=[vmem] * 5 + [pl.BlockSpec(memory_space=pl.ANY)],
+        out_specs=[vmem] * 3 + [pl.BlockSpec(memory_space=pl.ANY)],
         out_shape=[
             jax.ShapeDtypeStruct((total, columns), F32),
+            jax.ShapeDtypeStruct((units, width), BF16),
+            jax.ShapeDtypeStruct((units, width), BF16),
             jax.ShapeDtypeStruct((total, width), BF16),
         ],
-        scratch_shapes=[pltpu.VMEM((total, width), BF16)]
+        scratch_shapes=[pltpu.VMEM((total, width), BF16), pltpu.VMEM(expand.shape, BF16)]
         + ring_sems(count)
-        + [pltpu.SemaphoreType.DMA((count,))],
+        + [pltpu.SemaphoreType.DMA((count,)), pltpu.SemaphoreType.DMA],
         compiler_params=pltpu.CompilerParams(
             collective_id=0, has_side_effects=True, vmem_limit_bytes=48 << 20
         ),
@@ -331,7 +367,7 @@
             flops=2 * total * width * columns, bytes_accessed=total * width * 8, transcendentals=0
         ),
         name="project",
-    )(tokens, gains, offsets, weight, bias[None])
+    )(tokens, gains, offsets, weight, bias[None], expand)
 
 
 class Scatter:
@@ -1574,7 +1610,6 @@
 
     pad = ((0, units - units_used), (0, 0))
     turned_expand = jnp.transpose(expand_weight, (2, 1, 0))
-    gate_weight, up_weight = jnp.pad(turned_expand[:, 0], pad), jnp.pad(turned_expand[:, 1], pad)
     shrink = jnp.pad(shrink_weight, pad)
     unit_index = lax.axis_index("tp") * units_used + lax.iota(jnp.int32, units_used)
     keep_units = (unit_index < FF_USED).astype(F32)
@@ -1594,8 +1629,15 @@
     )
     cosine, sine = rotary_tables(positions)
 
-    projected, first_all = project(
-        tp, tokens, norm_gains[:1], norm_offsets[:1], input_weight, input_offset
+    projected, gate_weight, up_weight, first_all = project(
+        tp,
+        tokens,
+        norm_gains[:1],
+        norm_offsets[:1],
+        input_weight,
+        input_offset,
+        turned_expand,
+        units,
     )
     waiting, first_all = lax.optimization_barrier((cotangent, first_all))
     cotangent_all = lax.all_gather(waiting, "tp", axis=0, tiled=True)

time: 624 us -> 622 us (level)
  Pallas kernels: 557 us -> 571 us
  local copies, waits for them, and re-layouts: 35.5 us -> 25.8 us
    pallas_call x1, Pallas kernels: 98.2 us -> 107 us  [attention_to_feed(): pl.pallas_call(functools.partial(middle_kernel, count), in_specs=[vmem] *...]
    unnamed x49 -> x48, local copies, waits for them, and re-layouts: 20.5 us -> 14.9 us
  transfers between devices with their start and end apart: 1 -> 1, of which waited for: 0 -> 0; matrix products, arithmetic and copies ran while one was open for 3% -> 1% of each run, Pallas kernels for 19% -> 21%
where the time goes in v5:
time: 622 us; the launch traced here: 616 us
  Pallas kernels  571 us (92%)
  local copies, waits for them, and re-layouts  25.8 us (4%)
  between operations  14.6 us (2%)
    pallas_call x1, Pallas kernels, tail(): pl.pallas_call(functools.partial(tail_kernel, count, line_count, used), i...  239 us
    pallas_call x1, Pallas kernels, back(): pl.pallas_call(functools.partial(back_kernel, count, line_count, used), i...  146 us
    pallas_call x1, Pallas kernels, attention_to_feed(): pl.pallas_call(functools.partial(middle_kernel, count), in_specs=[vmem] *...  107 us
    pallas_call x1, Pallas kernels, project(): pl.pallas_call(functools.partial(project_kernel, count), in_specs=[vmem]...  48.9 us
    pallas_call x1, Pallas kernels, attend_forward(): pl.pallas_call(attend_forward_kernel, grid_spec=pltpu.PrefetchScalarGridS...  19.4 us
    unnamed x48, local copies, waits for them, and re-layouts  14.9 us
  transfers between devices with their start and end apart: 1, of which 0 were waited for; matrix products, arithmetic and copies ran while one was open for 1% of the time, Pallas kernels for 21%

profile of v5, /device:TPU:2, one launch (start us, length us, event | category | flops | bytes accessed | tf_op | source)
XLA Modules:
  0.0 616.4 jit_solution(17558673618667129084)
XLA Ops:
  7.9 0.7 slice.31.offsets
  9.4 1.2 copy-done.10
  10.6 48.9 %project.1 = (f32[2048,768]{1,0:T(8,128)}, bf16[704,2048]{1,0:T(8,128)(2,1)S(1)}, bf16[704,2048]{1,0:T(8,128)(2,1)}, bf16[2048,2048]{1,0:T(8,128)(2,1)}) custom-call(bf16[256,2048]{1,0:T(8,128)(2,1)S(1)} %copy-done.10, f32[1,2048]{1,0:T(1,128)S(1)} %slice.30.gains, f32[1,2048]{1,0:T(1,128)S(1)} %slice.31.offsets, bf16[2048,768]{1,0:T(8,128)(2,1)} %input_weight.1, ...), custom_call_target="tpu_custom_call" | custom-call | flops 6442450944 | bytes 33554432 | tf_op jit(solution)/shard_map/project/pallas_call | solution.py:350
  59.5 1.6 copy-done.13
  62.0 0.8 pad.8.columns
  62.8 1.8 pad.9.shrink
  64.7 3.7 fusion
  69.1 19.4 %attend_forward.1 = (bf16[2048,768]{1,0:T(8,128)(2,1)S(1)}, bf16[2048,256]{1,0:T(8,128)(2,1)S(1)}, f32[2,2,1,1024]{3,2,1,0:T(1,128)S(1)}) custom-call(s32[2,4,2]{2,1,0:T(4,128)S(1)} %pad_add_fusion.bounds, f32[2048,768]{1,0:T(8,128)S(1)} %bitcast.15, f32[2,1024,128]{2,1,0:T(8,128)S(1)} %get-tuple-element.89.cosine, ...), custom_call_target="tpu_custom_call" | custom-call | flops 2147483648 | bytes 10485760 | tf_op jit(solution)/shard_map/attend_forward/pallas_call | solution.py:118
  88.6 1.7 copy-done.9
  90.2 1.0 copy-done.11
  91.2 107.2 %attention_to_feed.1 = (bf16[704,2048]{1,0:T(8,128)(2,1)}, bf16[704,2048]{1,0:T(8,128)(2,1)}, bf16[704,2048]{1,0:T(8,128)(2,1)}, bf16[2048,2048]{1,0:T(8,128)(2,1)}, f32[256,2048]{1,0:T(8,128)}) custom-call(bf16[2048,256]{1,0:T(8,128)(2,1)} %copy-done.11, bf16[256,2048]{1,0:T(8,128)(2,1)} %output_weight.1, bf16[256,2048]{1,0:T(8,128)(2,1)} %tokens.5, ...), custom_call_target="tpu_custom_call" | custom-call | flops 11811160064 | bytes 33554432 | tf_op jit(solution)/shard_map/attention_to_feed/pallas_call | solution.py:752
  198.5 146.5 %back.1 = (bf16[2048,256]{1,0:T(8,128)(2,1)}, f32[256,2048]{1,0:T(8,128)}, f32[8,2048]{1,0:T(8,128)}, bf16[688,2048]{1,0:T(8,128)(2,1)}, bf16[256,2048]{1,0:T(8,...) custom-call(bf16[704,2048]{1,0:T(8,128)(2,1)} %get-tuple-element.48., ...), custom_call_target="tpu_custom_call" | custom-call | flops 53150220288 | bytes 33554432 | tf_op jit(solution)/shard_map/back/pallas_call | solution.py:1068
  345.0 238.9 %tail.1 = (f32[256,2048]{1,0:T(8,128)}, f32[256,2048]{1,0:T(8,128)}, f32[8,2048]{1,0:T(8,128)}, bf16[1408,2048]{1,0:T(8,128)(2,1)}, bf16[768,2048]{1,0:T(8,128)(...) custom-call(bf16[2048,768]{1,0:T(8,128)(2,1)} %copy-done.9, ...), custom_call_target="tpu_custom_call" | custom-call | flops 24696061952 | bytes 33554432 | tf_op jit(solution)/shard_map/tail/pallas_call | solution.py:1465
  583.8 1.3 slice_reduce_fusion
  585.2 1.3 slice.36
  586.5 1.5 fusion.8
  588.1 1.5 fusion.7
  589.6 2.6 copy-done
  592.2 1.9 copy-done.3
  594.1 1.2 copy-done.6
  595.3 10.3 %finish.1 = (f32[684,2,2048]{2,1,0:T(2,128)}, f32[684,2048]{1,0:T(8,128)}, f32[256,2048]{1,0:T(8,128)}, f32[2048,768]{1,0:T(8,128)}) custom-call(bf16[256,2048]{1,0:T(8,128)(2,1)S(1)} %copy-done.5, bf16[1408,2048]{1,0:T(8,128)(2,1)S(1)} %copy-done, bf16[1408,2048]{1,0:T(8,128)(2,1)S(1)} %copy-done, bf16[688,2048]{1,0:T(8,128)(2,1)S(1)} %copy-done.4, ...), custom_call_target="tpu_custom_call" | custom-call | bytes 37797888 | tf_op jit(solution)/shard_map/finish/pallas_call | solution.py:1556
  605.7 1.3 copy.73
  607.0 1.0 copy-done.15
  608.0 1.3 copy.74
  (62 shorter events, 3.1 us)
Async XLA Ops:
  7.2 191.3 %all-gather.2.cloned.1.call-start = ((), (), s32[]{:S(2)}) async-start(), calls=%async_computation | async-start | bytes 9437184 | tf_op jit(solution)/shard_map/all_gather | solution.py:1643
  9.4 1.2 copy-start.10
  10.6 50.5 %copy-start.17 = (s32[2,1024]{1,0:T(2,128)S(1)}, s32[2,1024]{1,0:T(2,128)}, u32[]{:S(2)}) copy-start(s32[2,1024]{1,0:T(2,128)} %param.16) | copy-start | bytes 24580
  10.6 50.5 %copy-start.20 = (s32[2,4]{1,0:T(2,128)S(1)}, s32[2,4]{1,0:T(2,128)}, u32[]{:S(2)}) copy-start(s32[2,4]{1,0:T(2,128)} %param.17) | copy-start | bytes 100
  10.6 50.6 %copy-start.18 = (s32[2,1024]{1,0:T(2,128)S(1)}, s32[2,1024]{1,0:T(2,128)}, u32[]{:S(2)}) copy-start(s32[2,1024]{1,0:T(2,128)} %param.18) | copy-start | bytes 24580
  10.6 51.2 %copy-start.19 = (f32[2,684]{1,0:T(2,128)S(1)}, f32[2,684]{1,0:T(2,128)}, u32[]{:S(2)}) copy-start(f32[2,684]{1,0:T(2,128)} %param.26) | copy-start | bytes 16420
  10.6 52.2 %copy-start.14 = (bf16[684,2048]{1,0:T(8,128)(2,1)S(1)}, bf16[684,2048]{1,0:T(8,128)(2,1)}, u32[]{:S(2)}) copy-start(bf16[684,2048]{1,0:T(8,128)(2,1)} %param.27) | copy-start | bytes 8404996
  59.5 1.6 copy-start.13
  61.3 7.8 %copy-start.7 = (s32[2,1,1024]{2,1,0:T(1,128)}, s32[2,1,1024]{2,1,0:T(1,128)S(1)}, u32[]{:S(2)}) copy-start(s32[2,1,1024]{2,1,0:T(1,128)S(1)} %broadcast_in_dim.38.high) | copy-start | bytes 24580
  61.3 7.8 %copy-start.8 = (s32[2,1,1024]{2,1,0:T(1,128)}, s32[2,1,1024]{2,1,0:T(1,128)S(1)}, u32[]{:S(2)}) copy-start(s32[2,1,1024]{2,1,0:T(1,128)S(1)} %copy.68.low) | copy-start | bytes 24580
  62.8 6.3 %slice-start = ((s8[6291456]{0:T(1024)(128)(4,1)}), s8[4194304]{0:T(1024)(128)(4,1)S(1)}, s32[]{:S(2)}) async-start(s8[6291456]{0:T(1024)(128)(4,1)} %bitcast.14), calls=%async_computation.1 | async-start | bytes 8388608
  64.7 4.4 slice-start.1
  69.1 19.5 %copy-start.1 = (f32[2,1024,128]{2,1,0:T(8,128)}, f32[2,1024,128]{2,1,0:T(8,128)S(1)}, u32[]{:S(2)}) copy-start(f32[2,1024,128]{2,1,0:T(8,128)S(1)} %get-tuple-element.89.cosine) | copy-start | bytes 3145732
  69.1 19.5 %copy-start.2 = (f32[2,1024,128]{2,1,0:T(8,128)}, f32[2,1024,128]{2,1,0:T(8,128)S(1)}, u32[]{:S(2)}) copy-start(f32[2,1024,128]{2,1,0:T(8,128)S(1)} %get-tuple-element.90.sine) | copy-start | bytes 3145732
  88.6 1.7 copy-start.9
  90.2 1.0 copy-start.11
  91.2 107.2 %copy-start.12 = (f32[2,2,1,1024]{3,2,1,0:T(1,128)}, f32[2,2,1,1024]{3,2,1,0:T(1,128)S(1)}, u32[]{:S(2)}) copy-start(f32[2,2,1,1024]{3,2,1,0:T(1,128)S(1)} %get-tuple-element.56.peaks) | copy-start | bytes 49156
  345.0 244.6 %copy-start.4 = (bf16[688,2048]{1,0:T(8,128)(2,1)S(1)}, bf16[688,2048]{1,0:T(8,128)(2,1)}, u32[]{:S(2)}) copy-start(bf16[688,2048]{1,0:T(8,128)(2,1)} %get-tuple-element.66.shrink) | copy-start | bytes 8454148
  345.0 244.6 %copy-start.5 = (bf16[256,2048]{1,0:T(8,128)(2,1)S(1)}, bf16[256,2048]{1,0:T(8,128)(2,1)}, u32[]{:S(2)}) copy-start(bf16[256,2048]{1,0:T(8,128)(2,1)} %get-tuple-element.64.early) | copy-start | bytes 3145732
  589.6 2.6 copy-start
  592.2 1.9 copy-start.3
  594.1 1.2 copy-start.6
  595.3 10.3 %copy-start.16 = (f32[256,2048]{1,0:T(8,128)S(1)}, f32[256,2048]{1,0:T(8,128)}, u32[]{:S(2)}) copy-start(f32[256,2048]{1,0:T(8,128)} %get-tuple-element.103) | copy-start | bytes 6291460
  605.7 2.3 copy-start.15
Sparse Core Ops, SparseCore 0:
  61.2 62.8 all-gather.1
